TPU v7x, 256 devices: a whole 4x4x8 slice. The times are simulated.
256 devices in a mesh: seq: 64 (over y, z_lo, x), mp: 4 (over z_hi, core).
Axes of the slice: x: 4, y: 4, z: 8 (z_hi: 2, z_lo: 4; z = z_hi * 4 + z_lo), core: 2. Of those that a mesh axis runs over, the one named last changes fastest.
Arguments:
- projected: bfloat16 [3, 8192, 8192], P(None, 'mp', 'seq'), may hold values from -6 to 6
- short_taps: float32 [3, 3, 8192], replicated, may hold values from -4 to 4
- skip_gain: float32 [8192], replicated, may hold values from -4 to 4
- residue: float32 [2048, 16], P('seq'), may hold values from -4 to 4
- decay_rate: float32 [2048, 16], P('seq'), may hold values from 6.1035156e-05 to 0.05
Outputs:
- gated: bfloat16 [8192, 8192], P('mp', 'seq')
All inputs are finite; a program needn't handle non-finite values.
Results may differ from a plain program's by a relative error of at most 0.012.
Values may be sent and summed in bfloat16 or wider, within the bound.
No kernel may reach another device: no remote copies, remote signals or barrier semaphores. Data moves between devices by JAX's collectives and lax.ppermute only.
A program may use at most 128 MiB of HBM per device.

v0:
```python
import math

import jax
import jax.numpy as jnp
from jax import lax
from jax.sharding import PartitionSpec as P

exact_mode = lax.Precision.HIGHEST
full_turn = 2.0 * math.pi


def unit_table(row_count, column_count, period):
    indices = lax.broadcasted_iota(jnp.int32, (row_count, column_count), 0) * lax.broadcasted_iota(
        jnp.int32, (row_count, column_count), 1
    )
    angles = -full_turn / period * (indices % period).astype(jnp.float32)
    return (jnp.cos(angles), jnp.sin(angles))


def dft_tables(length):
    padded_len = 2 * length
    narrow = padded_len // 128
    outer_table = unit_table(128, 128, 128)
    twiddle = unit_table(128, narrow, padded_len)
    inner_table = unit_table(narrow, narrow, narrow)
    return (outer_table, twiddle, inner_table)


def forward(signal, tables):
    outer_table, twiddle, inner_table = tables
    signal_count = signal.shape[0]
    narrow = inner_table[0].shape[0]
    blocks = signal.reshape(signal_count, 64, narrow)
    section_re = jnp.einsum("ca,mab->mcb", outer_table[0][:, :64], blocks, precision=exact_mode)
    section_im = jnp.einsum("ca,mab->mcb", outer_table[1][:, :64], blocks, precision=exact_mode)
    turned_re = section_re * twiddle[0] - section_im * twiddle[1]
    turned_im = section_re * twiddle[1] + section_im * twiddle[0]
    spec_re = jnp.einsum(
        "mcb,bd->mcd", turned_re, inner_table[0], precision=exact_mode
    ) - jnp.einsum("mcb,bd->mcd", turned_im, inner_table[1], precision=exact_mode)
    spec_im = jnp.einsum(
        "mcb,bd->mcd", turned_re, inner_table[1], precision=exact_mode
    ) + jnp.einsum("mcb,bd->mcd", turned_im, inner_table[0], precision=exact_mode)
    return (spec_re, spec_im)


def inverse(spec_re, spec_im, tables):
    outer_table, twiddle, inner_table = tables
    signal_count = spec_re.shape[0]
    narrow = inner_table[0].shape[0]
    back_re = jnp.einsum("mcd,bd->mcb", spec_re, inner_table[0], precision=exact_mode) + jnp.einsum(
        "mcd,bd->mcb", spec_im, inner_table[1], precision=exact_mode
    )
    back_im = jnp.einsum("mcd,bd->mcb", spec_im, inner_table[0], precision=exact_mode) - jnp.einsum(
        "mcd,bd->mcb", spec_re, inner_table[1], precision=exact_mode
    )
    turned_re = back_re * twiddle[0] + back_im * twiddle[1]
    turned_im = back_im * twiddle[0] - back_re * twiddle[1]
    result = jnp.einsum(
        "ca,mcb->mab", outer_table[0][:, :64], turned_re, precision=exact_mode
    ) + jnp.einsum("ca,mcb->mab", outer_table[1][:, :64], turned_im, precision=exact_mode)
    return result.reshape(signal_count, 64 * narrow) / (128.0 * narrow)


def filter_kernel(residue, decay_rate, length):
    positions = lax.broadcasted_iota(jnp.float32, (1, length), 1)

    def add_term(state_index, kernel):
        rates = lax.dynamic_slice_in_dim(decay_rate, state_index, 1, 1)
        weight = lax.dynamic_slice_in_dim(residue, state_index, 1, 1) * jnp.sqrt(rates)
        return kernel + weight * jnp.exp(-rates * positions)

    return lax.fori_loop(
        0, residue.shape[1], add_term, jnp.zeros((residue.shape[0], length), jnp.float32)
    )


def long_convolve(product, residue, decay_rate):
    signal_count, length = product.shape
    tables = dft_tables(length)
    signal_re, signal_im = forward(product.astype(jnp.float32), tables)
    mp_count = lax.axis_size("mp")
    per_group = signal_count // mp_count
    local_residue = lax.dynamic_slice_in_dim(
        residue, lax.axis_index("mp") * per_group, per_group, 0
    )
    local_rate = lax.dynamic_slice_in_dim(
        decay_rate, lax.axis_index("mp") * per_group, per_group, 0
    )
    kernel_re, kernel_im = forward(filter_kernel(local_residue, local_rate, length), tables)
    grouped_shape = (mp_count, per_group) + signal_re.shape[1:]
    signal_re = signal_re.reshape(grouped_shape)
    signal_im = signal_im.reshape(grouped_shape)
    kernel_re = kernel_re[None]
    kernel_im = kernel_im[None]
    mixed_re = (signal_re * kernel_re - signal_im * kernel_im).reshape(
        (signal_count,) + signal_re.shape[-2:]
    )
    mixed_im = (signal_re * kernel_im + signal_im * kernel_re).reshape(
        (signal_count,) + signal_re.shape[-2:]
    )
    return inverse(mixed_re, mixed_im, tables).astype(jnp.bfloat16)


def to_channels(streams):
    stream_count, chan_width, row_count = streams.shape
    seq_count = lax.axis_size("seq")
    mp_count = lax.axis_size("mp")
    arranged = streams.reshape(
        stream_count, seq_count, mp_count, chan_width // (seq_count * mp_count), row_count
    )
    arrived = lax.all_to_all(
        lax.all_to_all(arranged, "seq", split_axis=1, concat_axis=4, tiled=True),
        "mp",
        split_axis=2,
        concat_axis=2,
        tiled=True,
    )
    return arrived.reshape(stream_count, chan_width // seq_count, row_count * seq_count)


def from_channels(values):
    chan_dev, length = values.shape
    seq_count = lax.axis_size("seq")
    mp_count = lax.axis_size("mp")
    arranged = values.reshape(1, mp_count, chan_dev // mp_count, length)
    arrived = lax.all_to_all(
        lax.all_to_all(arranged, "seq", split_axis=3, concat_axis=0, tiled=True),
        "mp",
        split_axis=1,
        concat_axis=1,
        tiled=True,
    )
    return arrived.reshape(seq_count * chan_dev, length // seq_count)


def chosen_channels(full, chan_dev, chan_width):
    model_index = lax.axis_index("mp")
    seq_index = lax.axis_index("seq")
    mp_count = lax.axis_size("mp")
    piece_size = chan_dev // mp_count
    grouped = full.reshape(full.shape[:-1] + (mp_count, chan_width))
    selected = lax.dynamic_slice_in_dim(
        grouped, seq_index * chan_dev + model_index * piece_size, piece_size, grouped.ndim - 1
    )
    return selected.reshape(full.shape[:-1] + (chan_dev,))


def short_convolve(extended, tap_block):
    return (
        tap_block[0][:, :, None] * extended[:, :, 2:]
        + tap_block[1][:, :, None] * extended[:, :, 1:-1]
        + tap_block[2][:, :, None] * extended[:, :, :-2]
    )


def body(projected, short_taps, skip_gain, residue, decay_rate):
    chan_width = projected.shape[1]
    chan_dev = chan_width // lax.axis_size("seq")
    streams = to_channels(projected)
    taps_here = chosen_channels(short_taps, chan_dev, chan_width)
    skip_here = chosen_channels(skip_gain, chan_dev, chan_width)
    extended = jnp.pad(streams.astype(jnp.float32), ((0, 0), (0, 0), (2, 0)))
    mixed = short_convolve(extended, taps_here)
    product = (mixed[1] * mixed[2]).astype(jnp.bfloat16)
    long_part = long_convolve(product, residue, decay_rate)
    total = long_part.astype(jnp.float32) + skip_here[:, None] * product.astype(jnp.float32)
    return from_channels((mixed[0] * total).astype(jnp.bfloat16))


def solution(mesh):
    in_specs = (P(None, "mp", "seq"), P(), P(), P("seq", None), P("seq", None))
    out_specs = P("mp", "seq")
    return jax.shard_map(body, mesh=mesh, in_specs=in_specs, out_specs=out_specs, check_vma=False)
```

profile of v0, /device:TPU:2, one launch (start us, length us, event | category | flops | bytes accessed | tf_op | source)
XLA Modules:
  0.0 226.8 jit_solution(2267840420173184764)
XLA Ops:
  0.0 2.8 %copy.98 = bf16[3,64,4,8,128]{4,3,2,0,1:T(8,128)(2,1)} copy(bf16[3,64,4,8,128]{4,3,2,1,0:T(8,128)(2,1)} %bitcast.146) | data formatting | bytes 3145728 | tf_op jit(solution)/shard_map/reshape | solution.py:109
  2.8 12.2 %all-to-all-start = ((bf16[3,64,4,8,128]{4,3,2,0,1:T(8,128)(2,1)}), bf16[3,64,4,8,128]{4,3,2,0,1:T(8,128)(2,1)S(1)}, u32[]{:S(2)}, u32[]{:S(2)}) async-start(bf16[3,64,4,8,128]{4,3,2,0,1:T(8,128)(2,1)} %copy.98), calls=%async_computation | async-start | bytes 3145728 | tf_op jit(solution)/shard_map/all_to_all | solution.py:113
  15.2 39.3 %all-to-all-done = bf16[3,64,4,8,128]{4,3,2,0,1:T(8,128)(2,1)S(1)} async-done(((bf16[3,64,4,8,128]{4,3,2,0,1:T(8,128)(2,1)}), bf16[3,64,4,8,128]{4,3,2,0,1:T(8,128)(2,1)S(1)}, u32[]{:S(2)}, u32[]{:S(2)}) %all-to-all-start) | async-done | bytes 1572896 | tf_op jit(solution)/shard_map/all_to_all | solution.py:113
  54.5 0.6 copy.159
  55.1 2.1 reshape.166
  57.2 5.8 %all-to-all-start.1 = ((bf16[3,1,4,8,8192]{4,3,0,1,2:T(8,128)(2,1)}), bf16[3,1,4,8,8192]{4,3,0,1,2:T(8,128)(2,1)S(1)}, u32[]{:S(2)}, u32[]{:S(2)}) async-start(bf16[3,1,4,8,8192]{4,3,0,1,2:T(8,128)(2,1)} %reshape.166), calls=%async_computation.1 | async-start | bytes 3145728 | tf_op jit(solution)/shard_map/all_to_all | solution.py:112
  62.9 2.9 %while.14 = (s32[]{:T(128)}, f32[8,8192]{1,0:T(8,128)S(1)}, f32[8,16]{0,1:T(8,128)S(1)}, f32[8,16]{0,1:T(8,128)S(1)}, s32[]{:T(128)}, /*index=5*/s32[]{:T(128)}) while((s32[]{:T(128)}, f32[8,8192]{1,0:T(8,128)S(1)}, f32[8,16]{0,1:T(8,128)S(1)}, f32[8,16]{0,1:T(8,128)S(1)}, s32[]{:T(128)}, /*index=5*/s32[]{:T(128)}) %tuple.40), condition=%wide.region_1.2_spmd.clone, body=%wide.region_0.1_spmd.clone.sunk | while | flops 262163 | bytes 524571 | solution.py:73
  63.0 0.1 fusion.149
  63.1 0.1 fusion.149
  63.7 0.1 fusion.149
  63.8 0.1 fusion.149
  64.0 0.1 fusion.149
  64.9 0.1 fusion.149
  65.1 0.1 fusion.149
  65.9 0.3 reshape.144
  66.6 0.3 fusion.77
  66.9 0.3 fusion.78
  67.1 0.3 fusion.75
  67.4 1.0 convolution_bitcast_fusion
  68.4 1.0 convolution_bitcast_fusion.1
  69.4 1.2 fusion.48
  70.7 1.2 fusion.49
  71.9 2.0 convolution_add_fusion.2
  73.9 2.0 convolution_subtract_fusion.2
  75.9 26.0 %all-to-all-done.1 = bf16[3,1,4,8,8192]{4,3,0,1,2:T(8,128)(2,1)S(1)} async-done(((bf16[3,1,4,8,8192]{4,3,0,1,2:T(8,128)(2,1)}), bf16[3,1,4,8,8192]{4,3,0,1,2:T(8,128)(2,1)S(1)}, u32[]{:S(2)}, u32[]{:S(2)}) %all-to-all-start.1) | async-done | bytes 1572896 | tf_op jit(solution)/shard_map/all_to_all | solution.py:112
  101.9 0.3 bitcast_convert_fusion
  102.2 1.7 multiply_add_fusion
  104.2 1.2 fusion.92
  105.4 1.4 fusion.91
  106.8 3.6 %fusion.44 = f32[32,128,128]{2,1,0:T(8,128)S(1)} fusion(f32[32,128,128]{2,1,0:T(8,128)S(1)} %fusion.92, f32[32,128,128]{2,1,0:T(8,128)S(1)} %fusion.91, f32[128,128]{0,1:T(8,128)S(1)} %get-tuple-element.132, f32[128,128]{0,1:T(8,128)S(1)} %get-tuple-element.133), kind=kOutput, calls=%fused_computation.55 | convolution fusion | flops 807108608 | bytes 6422528 | tf_op jit(solution)/shard_map/mcb,bd->mcd/dot_general | solution.py:38
  110.5 3.6 %fusion.42 = f32[32,128,128]{2,1,0:T(8,128)S(1)} fusion(f32[32,128,128]{2,1,0:T(8,128)S(1)} %fusion.92, f32[32,128,128]{2,1,0:T(8,128)S(1)} %fusion.91, f32[128,128]{0,1:T(8,128)S(1)} %get-tuple-element.132, f32[128,128]{0,1:T(8,128)S(1)} %get-tuple-element.133), kind=kOutput, calls=%fused_computation.54 | convolution fusion | flops 807108608 | bytes 6422528 | tf_op jit(solution)/shard_map/mcb,bd->mcd/dot_general | solution.py:41
  114.1 3.6 %convolution_subtract_fusion.1 = f32[32,128,128]{2,1,0:T(8,128)S(1)} fusion(f32[32,128,128]{2,1,0:T(8,128)S(1)} %fusion.44, f32[32,128,128]{2,1,0:T(8,128)S(1)} %fusion.92, f32[32,128,128]{2,1,0:T(8,128)S(1)} %fusion.91, f32[128,128]{0,1:T(8,128)S(1)} %get-tuple-element.132, f32[128,128]{0,1:T(8,128)S(1)} %get-tuple-element.133), kind=kOutput, calls=%fused_computation.32 | convolution fusion | flops 807632896 | bytes 8519680 | tf_op jit(solution)/shard_map/mcb,bd->mcd/dot_general | solution.py:40
  117.8 4.2 %fusion.6 = (f32[32,128,128]{2,1,0:T(8,128)S(1)}, f32[32,128,128]{2,1,0:T(8,128)S(1)}) fusion(f32[32,128,128]{2,1,0:T(8,128)S(1)} %convolution_subtract_fusion.1, f32[8,128,128]{2,1,0:T(8,128)S(1)} %copy-done, f32[8,128,128]{2,1,0:T(8,128)S(1)} %copy-done.1, f32[32,128,128]{2,1,0:T(8,128)S(1)} %fusion.42, f32[32,128,128]{2,1,0:T(8,128)S(1)} %fusion.92, ...), kind=kOutput, calls=%fused_computation.14 | convolution fusion | flops 810778624 | bytes 13762560 | tf_op jit(solution)/shard_map/mcb,bd->mcd/dot_general | solution.py:43
  122.0 2.3 fusion.62
  124.3 2.3 %fusion.60 = f32[32,128,128]{1,2,0:T(8,128)S(1)} fusion(f32[32,128,128]{2,1,0:T(8,128)S(1)} %get-tuple-element.127), kind=kOutput, calls=%fused_computation.77 | convolution fusion | flops 805535744 | bytes 4194304 | tf_op jit(solution)/shard_map/mcd,bd->mcb/dot_general | solution.py:54
  126.6 2.3 convolution_add_fusion
  128.8 2.5 %convolution_subtract_fusion = f32[32,128,128]{1,2,0:T(8,128)S(1)} fusion(f32[32,128,128]{1,2,0:T(8,128)S(1)} %fusion.60, f32[32,128,128]{2,1,0:T(8,128)S(1)} %get-tuple-element.128), kind=kOutput, calls=%fused_computation.29 | convolution fusion | flops 806060032 | bytes 6291456 | tf_op jit(solution)/shard_map/mcd,bd->mcb/dot_general | solution.py:54
  131.3 2.6 %fusion.9 = f32[32,128,64]{1,2,0:T(8,128)S(1)} fusion(f32[32,128,128]{1,2,0:T(8,128)S(1)} %convolution_add_fusion, f32[32,128,128]{1,2,0:T(8,128)S(1)} %convolution_subtract_fusion, f32[128,128]{0,1:T(8,128)S(1)} %get-tuple-element.132, f32[128,128]{0,1:T(8,128)S(1)} %get-tuple-element.133, f32[128,128]{0,1:T(8,128)S(1)} %fusion.77), kind=kOutput, calls=%fused_computation.21 | convolution fusion | flops 404226048 | bytes 5406720 | tf_op jit(solution)/shard_map/ca,mcb->mab/dot_general | solution.py:61
  133.9 3.6 %fusion.29 = f32[32,64,128]{2,1,0:T(8,128)} fusion(f32[32,128,64]{1,2,0:T(8,128)S(1)} %fusion.9, f32[32,128,128]{1,2,0:T(8,128)S(1)} %convolution_subtract_fusion, f32[32,128,128]{1,2,0:T(8,128)S(1)} %convolution_add_fusion, f32[128,128]{0,1:T(8,128)S(1)} %get-tuple-element.132, f32[128,128]{0,1:T(8,128)S(1)} %get-tuple-element.133, f32[128,128]{0,1:T(8,128)S(1)} %fusion.78), kind=kOutput, calls=%fused_computation.38 | convolution fusion | flops 405274624 | bytes 6455296 | tf_op jit(solution)/shard_map/ca,mcb->mab/dot_general | solution.py:59
  137.6 2.4 %reshape.150 = f32[1,4,8,8192]{3,2,1,0:T(8,128)} reshape(f32[32,64,128]{2,1,0:T(8,128)} %fusion.29) | data formatting | bytes 2097152 | tf_op jit(solution)/shard_map/convert_element_type | solution.py:167
  140.0 2.2 fusion.34
  142.2 9.6 %copy.130 = bf16[1,4,8,8192]{2,1,0,3:T(4,128)(2,1)} copy(bf16[1,4,8,8192]{3,2,1,0:T(8,128)(2,1)} %fusion.34) | data formatting | bytes 1048576 | tf_op jit(solution)/shard_map/convert_element_type | solution.py:168
  151.8 10.5 %reshape.167 = bf16[64,2,2048]{2,1,0:T(2,128)(2,1)S(1)} reshape(bf16[8192,1,4,8]{3,2,1,0:T(4,128)(2,1)} %bitcast.138) | data formatting | bytes 1048576
  162.3 23.7 %all_to_all.46 = bf16[64,2,2048]{2,1,0:T(2,128)(2,1)S(1)} all-to-all(bf16[64,2,2048]{2,1,0:T(2,128)(2,1)S(1)} %reshape.167), channel_id=1, replica_groups=mesh['seq'=64,'mp'=4] {'seq'}, dimensions={0} | all-to-all | bytes 1048576 | tf_op jit(solution)/shard_map/all_to_all | solution.py:128
  186.1 10.9 %reshape.168 = bf16[8192,1,4,8]{3,2,1,0:T(4,128)(2,1)} reshape(bf16[64,2,2048]{2,1,0:T(2,128)(2,1)S(1)} %all_to_all.46) | data formatting | bytes 1048576
  197.0 9.9 %copy.131 = bf16[1,4,8,64,128]{4,2,3,1,0:T(8,128)(2,1)S(1)} copy(bf16[1,4,8,64,128]{2,1,4,3,0:T(4,128)(2,1)} %bitcast.139) | data formatting | bytes 1048576 | tf_op jit(solution)/shard_map/all_to_all | solution.py:128
  206.9 18.8 %all_to_all.47 = bf16[64,4,8,128]{3,2,0,1:T(8,128)(2,1)S(1)} all-to-all(bf16[64,4,8,128]{3,2,0,1:T(8,128)(2,1)S(1)} %bitcast.145), channel_id=1, replica_groups=mesh['seq'=64,'mp'=4] {'mp'}, dimensions={1} | all-to-all | bytes 1048576 | tf_op jit(solution)/shard_map/all_to_all | solution.py:127
  225.7 0.9 copy.132
  (47 shorter events, 2.1 us)
Async XLA Ops:
  2.8 12.2 %copy-start.4 = (f32[32,16]{0,1:T(8,128)S(1)}, f32[32,16]{0,1:T(8,128)}, u32[]{:S(2)}) copy-start(f32[32,16]{0,1:T(8,128)} %param.11) | copy-start | bytes 6148
  2.8 12.3 %copy-start.5 = (f32[32,16]{0,1:T(8,128)S(1)}, f32[32,16]{0,1:T(8,128)}, u32[]{:S(2)}) copy-start(f32[32,16]{0,1:T(8,128)} %param.10) | copy-start | bytes 6148
  2.8 51.6 %all-to-all-start = ((bf16[3,64,4,8,128]{4,3,2,0,1:T(8,128)(2,1)}), bf16[3,64,4,8,128]{4,3,2,0,1:T(8,128)(2,1)S(1)}, u32[]{:S(2)}, u32[]{:S(2)}) async-start(bf16[3,64,4,8,128]{4,3,2,0,1:T(8,128)(2,1)} %copy.98), calls=%async_computation | async-start | bytes 3145728 | tf_op jit(solution)/shard_map/all_to_all | solution.py:113
  57.2 44.7 %all-to-all-start.1 = ((bf16[3,1,4,8,8192]{4,3,0,1,2:T(8,128)(2,1)}), bf16[3,1,4,8,8192]{4,3,0,1,2:T(8,128)(2,1)S(1)}, u32[]{:S(2)}, u32[]{:S(2)}) async-start(bf16[3,1,4,8,8192]{4,3,0,1,2:T(8,128)(2,1)} %reshape.166), calls=%async_computation.1 | async-start | bytes 3145728 | tf_op jit(solution)/shard_map/all_to_all | solution.py:112
  62.9 3.0 %copy-start.2 = (f32[3,3,8192]{2,1,0:T(4,128)S(1)}, f32[3,3,8192]{2,1,0:T(4,128)}, u32[]{:S(2)}) copy-start(f32[3,3,8192]{2,1,0:T(4,128)} %param.8) | copy-start | bytes 884740
  62.9 3.6 %copy-start.3 = (f32[8192]{0:T(1024)S(1)}, f32[8192]{0:T(1024)}, u32[]{:S(2)}) copy-start(f32[8192]{0:T(1024)} %param.9) | copy-start | bytes 98308
  114.1 3.7 %copy-start = (f32[8,128,128]{2,1,0:T(8,128)S(1)}, f32[8,128,128]{2,1,0:T(8,128)}, u32[]{:S(2)}) copy-start(f32[8,128,128]{2,1,0:T(8,128)} %convolution_add_fusion.2) | copy-start | bytes 1572868
  114.1 3.7 %copy-start.1 = (f32[8,128,128]{2,1,0:T(8,128)S(1)}, f32[8,128,128]{2,1,0:T(8,128)}, u32[]{:S(2)}) copy-start(f32[8,128,128]{2,1,0:T(8,128)} %convolution_subtract_fusion.2) | copy-start | bytes 1572868
where the time goes:
time: 231 us; the launch traced here: 227 us
  waiting for transfers between devices  65.3 us (28%)
  local copies, waits for them, and re-layouts  50.6 us (22%)
  blocking collectives  42.6 us (18%)
  matrix products  41.7 us (18%)
  starting transfers between devices  18 us (8%)
  other arithmetic  7.44 us (3%)
    all_to_all x1, waiting for transfers between devices, to_channels(): lax.all_to_all(arranged, 'seq', split_axis=1, concat_axis=4, tiled=True)  39.3 us
    all_to_all x1, waiting for transfers between devices, to_channels(): lax.all_to_all(lax.all_to_all(arranged, 'seq', split_axis=1, concat_axis=...  26 us
    all_to_all x1, blocking collectives, from_channels(): lax.all_to_all(arranged, 'seq', split_axis=3, concat_axis=0, tiled=True)  23.7 us
    unnamed x15, local copies, waits for them, and re-layouts  21.5 us
    all_to_all x1, blocking collectives, from_channels(): lax.all_to_all(lax.all_to_all(arranged, 'seq', split_axis=3, concat_axis=...  18.8 us
    all_to_all x1, starting transfers between devices, to_channels(): lax.all_to_all(arranged, 'seq', split_axis=1, concat_axis=4, tiled=True)  12.2 us
    all_to_all x1, local copies, waits for them, and re-layouts, from_channels(): lax.all_to_all(arranged, 'seq', split_axis=3, concat_axis=0, tiled=True)  9.86 us
    convert_element_type x1, local copies, waits for them, and re-layouts, body(): return from_channels((mixed[0] * total).astype(jnp.bfloat16))  9.63 us
  transfers between devices with their start and end apart: 2, of which 2 were waited for; matrix products, arithmetic and copies ran while one was open for 5% of the time, Pallas kernels for 0%

commit v1 on v0

v1 whole, which is shorter than its diff:
```python
import math

import jax
import jax.numpy as jnp
import ml_dtypes
import numpy as np
from jax import lax
from jax.experimental import pallas as pl
from jax.experimental.pallas import tpu as pltpu
from jax.sharding import PartitionSpec as P

BLOCK = 128
MODES = 16
GROUP = 16
LANES = GROUP * MODES
f32 = jnp.float32
bf16 = jnp.bfloat16


def split_pair(value):
    high = value.astype(bf16)
    return high, (value - high.astype(f32)).astype(bf16)


def transform_tables():
    steps = np.arange(BLOCK, dtype=np.float64)
    angles = 2.0 * math.pi / BLOCK * np.outer(steps, steps - 0.25)
    table = np.concatenate([np.cos(angles), -np.sin(angles)], axis=1)
    high = table.astype(np.float32).astype(ml_dtypes.bfloat16)
    low = (table - high.astype(np.float64)).astype(np.float32).astype(ml_dtypes.bfloat16)
    return high, low


def mm(left, right):
    return lax.dot_general(left, right, (((1,), (0,)), ((), ())), preferred_element_type=f32)


def mm_nt(left, right, precision=None):
    return lax.dot_general(
        left, right, (((1,), (1,)), ((), ())), preferred_element_type=f32, precision=precision
    )


def halo_kernel(x_ref, out_ref):
    step = pl.program_id(0)
    lane = lax.broadcasted_iota(jnp.int32, (BLOCK, BLOCK), 1)

    @pl.when(step == 0)
    def _():
        out_ref[...] = jnp.zeros_like(out_ref)

    acc = jnp.zeros((BLOCK, BLOCK), f32)
    for part in range(4):
        for stream in range(3):
            tile = x_ref[stream, part * BLOCK : (part + 1) * BLOCK, :].astype(f32)
            slot = 8 * part + 2 * stream
            acc = jnp.where(
                (lane // 2) == slot // 2, pltpu.roll(tile, (slot - BLOCK + 2) % BLOCK, 1), acc
            )
    rolled = pltpu.roll(acc, step * 32, 1)
    out_ref[...] = jnp.where((lane // 32) == step, rolled, out_ref[...].astype(f32)).astype(bf16)


def pack_halo(projected):
    return pl.pallas_call(
        halo_kernel,
        grid=(4,),
        in_specs=[pl.BlockSpec((3, 512, BLOCK), lambda i: (0, i, 0))],
        out_specs=pl.BlockSpec((BLOCK, BLOCK), lambda i: (0, 0)),
        out_shape=jax.ShapeDtypeStruct((BLOCK, BLOCK), bf16),
        name="pack_halo",
    )(projected)


def short_mix(tile, before, taps, stream, lane):
    one = pltpu.roll(jnp.where(lane == BLOCK - 1, before, tile), 1, 1)
    two = pltpu.roll(jnp.where(lane >= BLOCK - 2, before, tile), 2, 1)
    return (
        taps[:, stream : stream + 1] * tile
        + taps[:, 3 + stream : 4 + stream] * one
        + taps[:, 6 + stream : 7 + stream] * two
    )


def tap_columns(taps_ref, span):
    rows = [taps_ref[lag, :, span] for lag in range(3)]
    rows.append(jnp.zeros((7, BLOCK), f32))
    return jnp.concatenate(rows, axis=0).T


def product_kernel(mp_ref, k_ref, v_ref, halo_ref, taps_ref, out_ref):
    step = pl.program_id(0)
    lane = lax.broadcasted_iota(jnp.int32, (BLOCK, BLOCK), 1)
    halo = halo_ref[...].astype(f32)
    for part in range(4):
        span = slice(part * BLOCK, (part + 1) * BLOCK)
        taps = tap_columns(taps_ref, span)
        place = step * 32 + part * 8
        k_before = pltpu.roll(halo, 2 * BLOCK - 4 - place, 1)
        v_before = pltpu.roll(halo, 2 * BLOCK - 6 - place, 1)
        k_mix = short_mix(k_ref[0, span, :].astype(f32), k_before, taps, 1, lane)
        v_mix = short_mix(v_ref[0, span, :].astype(f32), v_before, taps, 2, lane)
        out_ref[span, :] = (k_mix * v_mix).astype(bf16)


def make_product(projected, halo, short_taps, mp_index):
    stream_spec = lambda s: pl.BlockSpec((1, 512, BLOCK), lambda i, mp: (s, i, 0))
    return pl.pallas_call(
        product_kernel,
        grid_spec=pltpu.PrefetchScalarGridSpec(
            num_scalar_prefetch=1,
            grid=(4,),
            in_specs=[
                stream_spec(1),
                stream_spec(2),
                pl.BlockSpec((BLOCK, BLOCK), lambda i, mp: (0, 0)),
                pl.BlockSpec((3, 3, 512), lambda i, mp: (0, 0, mp[0] * 4 + i)),
            ],
            out_specs=pl.BlockSpec((512, BLOCK), lambda i, mp: (i, 0)),
        ),
        out_shape=jax.ShapeDtypeStruct((2048, BLOCK), bf16),
        name="product",
    )(mp_index, projected, projected, halo, short_taps)


def gate_kernel(mp_ref, q_ref, product_ref, long_ref, halo_ref, taps_ref, skip_ref, out_ref):
    step = pl.program_id(0)
    lane = lax.broadcasted_iota(jnp.int32, (BLOCK, BLOCK), 1)
    halo = halo_ref[...].astype(f32)
    for part in range(4):
        span = slice(part * BLOCK, (part + 1) * BLOCK)
        taps = tap_columns(taps_ref, span)
        skip = jnp.broadcast_to(skip_ref[:, span], (16, BLOCK)).T[:, 0:1]
        place = step * 32 + part * 8
        q_before = pltpu.roll(halo, 2 * BLOCK - 2 - place, 1)
        q_mix = short_mix(q_ref[0, span, :].astype(f32), q_before, taps, 0, lane)
        total = long_ref[span, :].astype(f32) + skip * product_ref[span, :].astype(f32)
        out_ref[span, :] = (q_mix * total).astype(bf16)


def apply_gate(projected, product, long_part, halo, short_taps, skip_gain, mp_index):
    rows = pl.BlockSpec((512, BLOCK), lambda i, mp: (i, 0))
    return pl.pallas_call(
        gate_kernel,
        grid_spec=pltpu.PrefetchScalarGridSpec(
            num_scalar_prefetch=1,
            grid=(4,),
            in_specs=[
                pl.BlockSpec((1, 512, BLOCK), lambda i, mp: (0, i, 0)),
                rows,
                rows,
                pl.BlockSpec((BLOCK, BLOCK), lambda i, mp: (0, 0)),
                pl.BlockSpec((3, 3, 512), lambda i, mp: (0, 0, mp[0] * 4 + i)),
                pl.BlockSpec((1, 512), lambda i, mp: (0, mp[0] * 4 + i)),
            ],
            out_specs=rows,
        ),
        out_shape=jax.ShapeDtypeStruct((2048, BLOCK), bf16),
        name="gate",
    )(mp_index, projected, product, long_part, halo, short_taps, skip_gain.reshape(1, -1))


def flat_row(values, groups):
    mode = lax.broadcasted_iota(jnp.int32, (MODES, LANES), 0)
    lane = lax.broadcasted_iota(jnp.int32, (MODES, LANES), 1)
    pick = (lane % MODES == mode).astype(f32)
    own = (lane // MODES) == mode
    spread = lax.dot_general(
        values, pick, (((1,), (0,)), ((), ())), preferred_element_type=f32,
        precision=lax.Precision.HIGHEST,
    )
    rows = [
        jnp.sum(jnp.where(own, spread[g * GROUP : (g + 1) * GROUP], 0.0), axis=0, keepdims=True)
        for g in range(groups)
    ]
    return jnp.concatenate(rows, axis=1)


def long_kernel(
    x_ref, residue_ref, rate_ref, high_ref, low_ref, out_ref,
    in_hi, in_lo, out_hi, out_lo, spec_ref, state_ref,
):
    blocks, channels, _ = x_ref.shape
    groups = channels // GROUP
    lanes = groups * LANES
    rate_row = flat_row(rate_ref[...], groups)
    weight_row = flat_row(residue_ref[...], groups) * jnp.sqrt(rate_row)
    place = lax.broadcasted_iota(jnp.int32, (BLOCK, lanes), 0).astype(f32)
    in_hi[...], in_lo[...] = split_pair(jnp.exp(-rate_row * (BLOCK - 1.0 - place)))
    weighted = weight_row * jnp.exp(-rate_row * place)
    out_hi[...], out_lo[...] = split_pair(weighted * jnp.exp(-rate_row))
    member = (
        lax.broadcasted_iota(jnp.int32, (channels, lanes), 1) // MODES
        == lax.broadcasted_iota(jnp.int32, (channels, lanes), 0)
    ).astype(f32)
    kernel = mm_nt(member, weighted, lax.Precision.HIGHEST)
    k_hi, k_lo = split_pair(kernel)
    spec_ref[...] = (
        mm(k_hi, high_ref[...]) + mm(k_hi, low_ref[...]) + mm(k_lo, high_ref[...])
    ) * (1.0 / BLOCK)

    own = (
        lax.broadcasted_iota(jnp.int32, (GROUP, LANES), 1) // MODES
        == lax.broadcasted_iota(jnp.int32, (GROUP, LANES), 0)
    )
    chunk = 8
    rows = chunk * GROUP

    def gather_states(i, carry):
        at = pl.multiple_of(i * chunk, chunk)
        for g in range(groups):
            x = x_ref[pl.ds(at, chunk), g * GROUP : (g + 1) * GROUP, :].reshape(rows, BLOCK)
            span = slice(g * LANES, (g + 1) * LANES)
            found = mm(x, in_hi[:, span]) + mm(x, in_lo[:, span])
            found = jnp.where(own, found.reshape(chunk, GROUP, LANES), 0.0)
            state_ref[pl.ds(at, chunk), span] = jnp.sum(found, axis=1)
        return carry

    lax.fori_loop(0, blocks // chunk, gather_states, 0)
    decay = jnp.exp(-float(BLOCK) * rate_row)
    state = jnp.zeros((1, lanes), f32)
    for b in range(blocks):
        ended = state_ref[b : b + 1, :]
        state_ref[b : b + 1, :] = state
        state = state * decay + ended

    def convolve(i, carry):
        at = pl.multiple_of(i * chunk, chunk)
        for g in range(groups):
            x = x_ref[pl.ds(at, chunk), g * GROUP : (g + 1) * GROUP, :].reshape(rows, BLOCK)
            span = slice(g * LANES, (g + 1) * LANES)
            turned = (mm(x, high_ref[...]) + mm(x, low_ref[...])).reshape(chunk, GROUP, 2 * BLOCK)
            x_re, x_im = turned[:, :, :BLOCK], turned[:, :, BLOCK:]
            spec = spec_ref[g * GROUP : (g + 1) * GROUP, :]
            k_re, k_im = spec[:, :BLOCK], spec[:, BLOCK:]
            mixed = jnp.concatenate(
                [x_re * k_re - x_im * k_im, x_re * k_im + x_im * k_re], axis=2
            ).reshape(rows, 2 * BLOCK)
            m_hi, m_lo = split_pair(mixed)
            state = jnp.where(own, state_ref[pl.ds(at, chunk), span][:, None, :], 0.0)
            s_hi, s_lo = split_pair(state.reshape(rows, LANES))
            result = (
                mm_nt(m_hi, high_ref[...]) + mm_nt(m_hi, low_ref[...]) + mm_nt(m_lo, high_ref[...])
            ) + (
                mm_nt(s_hi, out_hi[:, span]) + mm_nt(s_hi, out_lo[:, span]) + mm_nt(s_lo, out_hi[:, span])
            )
            out_ref[pl.ds(at, chunk), g * GROUP : (g + 1) * GROUP, :] = result.astype(bf16).reshape(
                chunk, GROUP, BLOCK
            )
        return carry

    lax.fori_loop(0, blocks // chunk, convolve, 0)


def long_convolve(blocks, residue, decay_rate):
    count, channels, _ = blocks.shape
    lanes = channels * MODES
    high, low = transform_tables()
    return pl.pallas_call(
        long_kernel,
        out_shape=jax.ShapeDtypeStruct(blocks.shape, bf16),
        scratch_shapes=[pltpu.VMEM((BLOCK, lanes), bf16)] * 4
        + [pltpu.VMEM((channels, 2 * BLOCK), f32), pltpu.VMEM((count, lanes), f32)],
        compiler_params=pltpu.CompilerParams(vmem_limit_bytes=32 << 20),
        name="long_conv",
    )(blocks, residue, decay_rate, jnp.asarray(high), jnp.asarray(low))


def body(projected, short_taps, skip_gain, residue, decay_rate):
    seq_count = lax.axis_size("seq")
    mp_index = lax.axis_index("mp").astype(jnp.int32).reshape(1)
    halo = lax.ppermute(
        pack_halo(projected), "seq", [(i, i + 1) for i in range(seq_count - 1)]
    )
    product = make_product(projected, halo, short_taps, mp_index)
    arrived = lax.all_to_all(
        product.reshape(seq_count, -1, BLOCK), "seq", split_axis=0, concat_axis=0, tiled=True
    )
    result = long_convolve(arrived, residue, decay_rate)
    long_part = lax.all_to_all(result, "seq", split_axis=0, concat_axis=0, tiled=True)
    return apply_gate(
        projected, product, long_part.reshape(product.shape), halo, short_taps, skip_gain, mp_index
    )


def solution(mesh):
    in_specs = (P(None, "mp", "seq"), P(), P(), P("seq", None), P("seq", None))
    out_specs = P("mp", "seq")
    return jax.shard_map(body, mesh=mesh, in_specs=in_specs, out_specs=out_specs, check_vma=False)
```

time: 231 us -> 80.5 us (0.35); the launches traced: 227 us -> 80.1 us
  local copies, waits for them, and re-layouts: 50.6 us -> 0.76 us
  waiting for transfers between devices: 65.3 us -> 18.6 us
  matrix products: 41.7 us -> 0 us
  Pallas kernels: 0 us -> 22.9 us
  blocking collectives: 42.6 us -> 22.3 us
  other arithmetic: 7.44 us -> 0 us
  starting transfers between devices: 18 us -> 15.5 us
    all_to_all x2 -> x1, waiting for transfers between devices: 65.3 us -> 16 us  [body(): lax.all_to_all(product.reshape(seq_count, -1, BLOCK), 'seq', split_axis=0...]
    dot_general x18 -> x0, matrix products: 41.7 us -> none  [the longest x2 6.19 us: forward(): jnp.einsum('mcb,bd->mcd', turned_im, inner_table[0], precision=exact_mode)]
    pallas_call x0 -> x4, Pallas kernels: none -> 22.9 us  [the longest x1 7.07 us: long_convolve(): pl.pallas_call(long_kernel, out_shape=jax.ShapeDtypeStruct(blocks.shape,...]
    unnamed x15 -> x12, local copies, waits for them, and re-layouts: 21.5 us -> 0.76 us
    all_to_all x2 -> x1, blocking collectives: 42.6 us -> 22.3 us  [body(): lax.all_to_all(result, 'seq', split_axis=0, concat_axis=0, tiled=True)]
    all_to_all x4 -> x0, local copies, waits for them, and re-layouts: 13.4 us -> none  [the longest x1 9.86 us: from_channels(): lax.all_to_all(arranged, 'seq', split_axis=3, concat_axis=0, tiled=True)]
    convert_element_type x2 -> x0, local copies, waits for them, and re-layouts: 12 us -> none  [the longest x1 9.63 us: body(): return from_channels((mixed[0] * total).astype(jnp.bfloat16))]
    all_to_all x2 -> x1, starting transfers between devices: 18 us -> 12.1 us  [body(): lax.all_to_all(product.reshape(seq_count, -1, BLOCK), 'seq', split_axis=0...]
  transfers between devices with their start and end apart: 2 -> 2, of which waited for: 2 -> 2; matrix products, arithmetic and copies ran while one was open for 5% -> 0% of each run, Pallas kernels for 0% -> 0%
where the time goes in v1:
time: 80.5 us; the launch traced here: 80.1 us
  Pallas kernels  22.9 us (28%)
  blocking collectives  22.3 us (28%)
  waiting for transfers between devices  18.6 us (23%)
  starting transfers between devices  15.5 us (19%)
    all_to_all x1, blocking collectives, body(): lax.all_to_all(result, 'seq', split_axis=0, concat_axis=0, tiled=True)  22.3 us
    all_to_all x1, waiting for transfers between devices, body(): lax.all_to_all(product.reshape(seq_count, -1, BLOCK), 'seq', split_axis=0...  16 us
    all_to_all x1, starting transfers between devices, body(): lax.all_to_all(product.reshape(seq_count, -1, BLOCK), 'seq', split_axis=0...  12.1 us
    pallas_call x1, Pallas kernels, long_convolve(): pl.pallas_call(long_kernel, out_shape=jax.ShapeDtypeStruct(blocks.shape,...  7.07 us
    pallas_call x1, Pallas kernels, make_product(): pl.pallas_call(product_kernel, grid_spec=pltpu.PrefetchScalarGridSpec(num...  6.33 us
    pallas_call x1, Pallas kernels, apply_gate(): pl.pallas_call(gate_kernel, grid_spec=pltpu.PrefetchScalarGridSpec(num_sc...  6.1 us
    ppermute x1, starting transfers between devices, body(): lax.ppermute(pack_halo(projected), 'seq', [(i, i + 1) for i in range(seq_...  3.39 us
    pallas_call x1, Pallas kernels, pack_halo(): pl.pallas_call(halo_kernel, grid=(4,), in_specs=[pl.BlockSpec((3, 512, BL...  3.37 us
  transfers between devices with their start and end apart: 2, of which 2 were waited for; matrix products, arithmetic and copies ran while one was open for 0% of the time, Pallas kernels for 0%

profile of v1, /device:TPU:2, one launch (start us, length us, event | category | flops | bytes accessed | tf_op | source)
XLA Modules:
  0.0 80.1 jit_solution(7593360734445821888)
XLA Ops:
  0.0 3.4 %pack_halo.1 = bf16[128,128]{1,0:T(8,128)(2,1)} custom-call(bf16[3,2048,128]{2,1,0:T(8,128)(2,1)} %q_ref.1), custom_call_target="tpu_custom_call" | custom-call | tf_op jit(solution)/shard_map/pack_halo/pallas_call | solution.py:65
  3.4 3.4 %collective-permute-start = (bf16[128,128]{1,0:T(8,128)(2,1)}, bf16[128,128]{1,0:T(8,128)(2,1)S(1)}, u32[]{:S(2)}, u32[]{:S(2)}) collective-permute-start(bf16[128,128]{1,0:T(8,128)(2,1)} %pack_halo.1), channel_id=1, source_target_pairs={{0,4},{4,8},{8,12},{12,16},{16,20},{20,24},{24,28},{28,32},{32,36}... | collective-permute-start | bytes 98312 | tf_op jit(solution)/shard_map/ppermute | solution.py:272
  6.8 2.6 %collective-permute-done.halo_ref = bf16[128,128]{1,0:T(8,128)(2,1)S(1)} collective-permute-done((bf16[128,128]{1,0:T(8,128)(2,1)}, bf16[128,128]{1,0:T(8,128)(2,1)S(1)}, u32[]{:S(2)}, u32[]{:S(2)}) %collective-permute-start) | collective-permute-done | bytes 32800 | tf_op jit(solution)/shard_map/ppermute | solution.py:272
  9.4 0.0 copy-start.2
  9.4 0.6 copy-done.2
  10.0 0.0 copy-start.3
  10.0 0.0 copy-start.4
  10.0 0.0 copy-start
  10.0 0.0 copy-start.1
  10.0 6.3 %product.1.product_ref = bf16[2048,128]{1,0:T(8,128)(2,1)} custom-call(s32[1]{0:T(128)} %bitcast.mp_ref, bf16[3,2048,128]{2,1,0:T(8,128)(2,1)} %q_ref.1, bf16[3,2048,128]{2,1,0:T(8,128)(2,1)} %q_ref.1, bf16[128,128]{1,0:T(8,128)(2,1)} %copy-done.2, f32[3,3,8192]{2,1,0:T(4,128)} %taps_ref.3), custom_call_target="tpu_custom_call" | custom-call | tf_op jit(solution)/shard_map/product/pallas_call | solution.py:108
  16.3 12.1 %all-to-all-start = ((bf16[64,32,128]{2,1,0:T(8,128)(2,1)}), bf16[64,32,128]{2,1,0:T(8,128)(2,1)S(1)}, u32[]{:S(2)}, u32[]{:S(2)}) async-start(bf16[64,32,128]{2,1,0:T(8,128)(2,1)} %bitcast.4), calls=%async_computation | async-start | bytes 1048576 | tf_op jit(solution)/shard_map/all_to_all | solution.py:276
  28.4 0.0 copy-done.3
  28.4 0.1 copy.8.residue_ref
  28.5 0.0 copy-done.4
  28.5 0.1 copy.9.rate_ref
  28.6 16.0 %all-to-all-done.x_ref = bf16[64,32,128]{2,1,0:T(8,128)(2,1)S(1)} async-done(((bf16[64,32,128]{2,1,0:T(8,128)(2,1)}), bf16[64,32,128]{2,1,0:T(8,128)(2,1)S(1)}, u32[]{:S(2)}, u32[]{:S(2)}) %all-to-all-start) | async-done | bytes 524320 | tf_op jit(solution)/shard_map/all_to_all | solution.py:276
  44.5 0.0 copy-done
  44.6 0.0 copy-done.1
  44.6 7.1 %long_conv.1 = bf16[64,32,128]{2,1,0:T(8,128)(2,1)S(1)} custom-call(bf16[64,32,128]{2,1,0:T(8,128)(2,1)S(1)} %all-to-all-done.x_ref, f32[32,16]{1,0:T(8,128)S(1)} %copy.8.residue_ref, f32[32,16]{1,0:T(8,128)S(1)} %copy.9.rate_ref, bf16[128,256]{1,0:T(8,128)(2,1)S(1)} %copy-done.1, bf16[128,256]{1,0:T(8,128)(2,1)S(1)} %copy-done), custom_call_target="tpu_custom_call" | custom-call | tf_op jit(solution)/shard_map/long_conv/pallas_call | solution.py:259
  51.6 22.3 %all_to_all.10 = bf16[64,32,128]{2,1,0:T(8,128)(2,1)} all-to-all(bf16[64,32,128]{2,1,0:T(8,128)(2,1)S(1)} %long_conv.1), channel_id=1, replica_groups=mesh['seq'=64,'mp'=4] {'seq'}, dimensions={0} | all-to-all | bytes 1048576 | tf_op jit(solution)/shard_map/all_to_all | solution.py:280
  74.0 6.1 %gate.1 = bf16[2048,128]{1,0:T(8,128)(2,1)} custom-call(s32[1]{0:T(128)} %bitcast.mp_ref, bf16[3,2048,128]{2,1,0:T(8,128)(2,1)} %q_ref.1, bf16[2048,128]{1,0:T(8,128)(2,1)} %product.1.product_ref, bf16[2048,128]{1,0:T(8,128)(2,1)} %bitcast.5, bf16[128,128]{1,0:T(8,128)(2,1)} %copy-done.2, f32[3,3,8192]{2,1,0:T(4,128)} %taps_ref.3, f32[1,8192]{1,0:T(1,128)} %bitcast.6), custom_call_target="tpu_custom_call" | custom-call | tf_op jit(solution)/shard_map/gate/pallas_call | solution.py:143
Async XLA Ops:
  3.4 6.0 %collective-permute-start = (bf16[128,128]{1,0:T(8,128)(2,1)}, bf16[128,128]{1,0:T(8,128)(2,1)S(1)}, u32[]{:S(2)}, u32[]{:S(2)}) collective-permute-start(bf16[128,128]{1,0:T(8,128)(2,1)} %pack_halo.1), channel_id=1, source_target_pairs={{0,4},{4,8},{8,12},{12,16},{16,20},{20,24},{24,28},{28,32},{32,36}... | collective-permute-start | bytes 98312 | tf_op jit(solution)/shard_map/ppermute | solution.py:272
  9.4 0.6 copy-start.2
  10.0 18.4 %copy-start.3 = (f32[32,16]{0,1:T(8,128)S(1)}, f32[32,16]{0,1:T(8,128)}, u32[]{:S(2)}) copy-start(f32[32,16]{0,1:T(8,128)} %param.10) | copy-start | bytes 6148
  10.0 18.5 %copy-start.4 = (f32[32,16]{0,1:T(8,128)S(1)}, f32[32,16]{0,1:T(8,128)}, u32[]{:S(2)}) copy-start(f32[32,16]{0,1:T(8,128)} %param.11) | copy-start | bytes 6148
  10.0 34.6 %copy-start = (bf16[128,256]{1,0:T(8,128)(2,1)S(1)}, bf16[128,256]{1,0:T(8,128)(2,1)}, u32[]{:S(2)}) copy-start(bf16[128,256]{1,0:T(8,128)(2,1)} %constant.9.clone.low_ref) | copy-start | bytes 196612
  10.0 34.6 %copy-start.1 = (bf16[128,256]{1,0:T(8,128)(2,1)S(1)}, bf16[128,256]{1,0:T(8,128)(2,1)}, u32[]{:S(2)}) copy-start(bf16[128,256]{1,0:T(8,128)(2,1)} %constant.8.clone.high_ref) | copy-start | bytes 196612
  16.3 28.2 %all-to-all-start = ((bf16[64,32,128]{2,1,0:T(8,128)(2,1)}), bf16[64,32,128]{2,1,0:T(8,128)(2,1)S(1)}, u32[]{:S(2)}, u32[]{:S(2)}) async-start(bf16[64,32,128]{2,1,0:T(8,128)(2,1)} %bitcast.4), calls=%async_computation | async-start | bytes 1048576 | tf_op jit(solution)/shard_map/all_to_all | solution.py:276

commit v2 on v0

v2 whole, which is shorter than its diff:
```python
import math

import jax
import jax.numpy as jnp
import ml_dtypes
import numpy as np
from jax import lax
from jax.experimental import pallas as pl
from jax.experimental.pallas import tpu as pltpu
from jax.sharding import Mesh, PartitionSpec as P

BLOCK = 128
MODES = 16
SIDE = 4
OWNERS = SIDE * SIDE
f32 = jnp.float32
bf16 = jnp.bfloat16
SMALL = pltpu.CompilerParams(vmem_limit_bytes=16 << 20)


def split_pair(value):
    high = value.astype(bf16)
    return high, (value - high.astype(f32)).astype(bf16)


def transform_tables():
    steps = np.arange(BLOCK, dtype=np.float64)
    angles = 2.0 * math.pi / BLOCK * np.outer(steps, steps - 0.25)
    table = np.concatenate([np.cos(angles), -np.sin(angles)], axis=1)
    high = table.astype(np.float32).astype(ml_dtypes.bfloat16)
    low = (table - high.astype(np.float64)).astype(np.float32).astype(ml_dtypes.bfloat16)
    forward = np.concatenate([high.T, low.T], axis=1)
    backward = np.concatenate([high, low], axis=0)
    return jnp.asarray(forward), jnp.asarray(backward)


def shift_table():
    row = lax.broadcasted_iota(jnp.int32, (BLOCK, BLOCK), 0)
    column = lax.broadcasted_iota(jnp.int32, (BLOCK, BLOCK), 1)
    return jnp.concatenate([(row - lag == column).astype(bf16) for lag in range(3)], axis=0)


def mm(left, right):
    return lax.dot_general(left, right, (((1,), (0,)), ((), ())), preferred_element_type=f32)


def mm_nt(left, right, precision=None):
    return lax.dot_general(
        left, right, (((1,), (1,)), ((), ())), preferred_element_type=f32, precision=precision
    )


def full(shape):
    return pl.BlockSpec(shape, lambda *_: (0,) * len(shape))


def owner_rows(x):
    return [slice(128 * zl + 32 * x, 128 * zl + 32 * x + 32) for zl in range(SIDE)]


def mix_kernel(
    mp_ref, x_ref, taps_ref, skip_ref, residue_ref, rate_ref,
    product_ref, gate_ref, head_ref, halo_ref, rows_ref, params_ref,
):
    shifts = shift_table()
    lane = lax.broadcasted_iota(jnp.int32, (16, BLOCK), 1) // 32
    table = jnp.concatenate(
        [taps_ref[0], taps_ref[1], taps_ref[2], skip_ref[...], jnp.zeros((6, 4 * BLOCK), f32)], axis=0
    )
    for x in range(SIDE):
        rows = jnp.zeros((16, BLOCK), f32)
        for zl in range(SIDE):
            piece = table[:, zl * BLOCK : (zl + 1) * BLOCK]
            if zl != x:
                piece = pltpu.roll(piece, (32 * (zl - x)) % BLOCK, 1)
            rows = jnp.where(lane == zl, piece, rows)
        rows_ref[x] = rows
        mixes = []
        for stream in range(3):
            tile = jnp.concatenate([x_ref[stream, span, :] for span in owner_rows(x)], axis=0)
            moved = mm_nt(shifts, tile)
            halo_ref[x, 2 * stream : 2 * stream + 2, :] = moved[BLOCK - 2 : BLOCK]
            mixes.append(
                rows[stream : stream + 1] * moved[:BLOCK]
                + rows[3 + stream : 4 + stream] * moved[BLOCK : 2 * BLOCK]
                + rows[6 + stream : 7 + stream] * moved[2 * BLOCK :]
            )
        halo_ref[x, 6:8, :] = jnp.zeros((2, BLOCK), f32)
        gate_ref[x] = mixes[0]
        head_ref[0, x] = mixes[1][:8]
        head_ref[1, x] = mixes[2][:8]
        product_ref[x] = (mixes[1] * mixes[2]).astype(bf16)

    @pl.when(pl.program_id(0) == 0)
    def _():
        rate = rate_ref[...]
        count = rate.shape[1]
        params_ref[...] = jnp.zeros((2 * MODES, BLOCK), f32)
        params_ref[:MODES, :count] = rate
        params_ref[MODES:, :count] = residue_ref[...] * jnp.sqrt(rate)


def mix_streams(projected, short_taps, skip_gain, residue, decay_rate, mp_index):
    tile = lambda n: pl.BlockSpec((4, n, BLOCK), lambda i, mp: (i, 0, 0))
    projected = pltpu.with_memory_space_constraint(projected, pltpu.HBM)
    short_taps = pltpu.with_memory_space_constraint(short_taps, pltpu.HBM)
    return pl.pallas_call(
        mix_kernel,
        grid_spec=pltpu.PrefetchScalarGridSpec(
            num_scalar_prefetch=1,
            grid=(4,),
            in_specs=[
                pl.BlockSpec((3, 512, BLOCK), lambda i, mp: (0, i, 0)),
                pl.BlockSpec((3, 3, 512), lambda i, mp: (0, 0, mp[0] * 4 + i)),
                pl.BlockSpec((1, 512), lambda i, mp: (0, mp[0] * 4 + i)),
                full(residue.shape[::-1]),
                full(decay_rate.shape[::-1]),
            ],
            out_specs=[
                tile(BLOCK),
                tile(BLOCK),
                pl.BlockSpec((2, 4, 8, BLOCK), lambda i, mp: (0, i, 0, 0)),
                tile(8),
                tile(16),
                full((2 * MODES, BLOCK)),
            ],
        ),
        out_shape=[
            jax.ShapeDtypeStruct((OWNERS, BLOCK, BLOCK), bf16),
            jax.ShapeDtypeStruct((OWNERS, BLOCK, BLOCK), f32),
            jax.ShapeDtypeStruct((2, OWNERS, 8, BLOCK), f32),
            jax.ShapeDtypeStruct((OWNERS, 8, BLOCK), f32),
            jax.ShapeDtypeStruct((OWNERS, 16, BLOCK), f32),
            jax.ShapeDtypeStruct((2 * MODES, BLOCK), f32),
        ],
        compiler_params=SMALL,
        name="mix",
    )(mp_index, projected, short_taps, skip_gain.reshape(1, -1), residue.T, decay_rate.T)


def halo_term(halo, rows, stream):
    at = lax.broadcasted_iota(jnp.int32, (8, BLOCK), 0)
    older = halo[2 * stream : 2 * stream + 1]
    newer = halo[2 * stream + 1 : 2 * stream + 2]
    one = rows[3 + stream : 4 + stream]
    two = rows[6 + stream : 7 + stream]
    return jnp.where(at == 0, one * newer + two * older, jnp.where(at == 1, two * newer, 0.0))


def head_kernel(product_ref, head_ref, halo_ref, rows_ref, out_ref):
    for g in range(OWNERS):
        halo = halo_ref[g]
        rows = rows_ref[g]
        k_mix = head_ref[0, g] + halo_term(halo, rows, 1)
        v_mix = head_ref[1, g] + halo_term(halo, rows, 2)
        rest = product_ref[g, 8:16, :].astype(f32)
        out_ref[g] = jnp.concatenate([k_mix * v_mix, rest], axis=0).astype(bf16)


def finish_product(product, head, halo, rows):
    top = pl.BlockSpec((OWNERS, 16, BLOCK), lambda i: (0, 0, 0))
    return pl.pallas_call(
        head_kernel,
        grid=(1,),
        in_specs=[top, full(head.shape), full(halo.shape), full(rows.shape)],
        out_specs=top,
        out_shape=jax.ShapeDtypeStruct(product.shape, bf16),
        input_output_aliases={0: 0},
        compiler_params=SMALL,
        name="head",
    )(product, head, halo, rows)


def gate_kernel(mix_ref, product_ref, long_ref, halo_ref, rows_ref, out_ref):
    for x in range(SIDE):
        mix = mix_ref[x]
        rows = rows_ref[x]
        mix = jnp.concatenate([mix[:8] + halo_term(halo_ref[x], rows, 0), mix[8:]], axis=0)
        total = long_ref[x].astype(f32) + rows[9:10] * product_ref[x].astype(f32)
        gated = (mix * total).T.astype(bf16)
        for zl, span in enumerate(owner_rows(x)):
            out_ref[span, :] = gated[32 * zl : 32 * zl + 32]


def apply_gate(mix, product, long_part, halo, rows):
    tile = lambda n: pl.BlockSpec((4, n, BLOCK), lambda i: (i, 0, 0))
    return pl.pallas_call(
        gate_kernel,
        grid=(4,),
        in_specs=[tile(BLOCK), tile(BLOCK), tile(BLOCK), tile(8), tile(16)],
        out_specs=pl.BlockSpec((512, BLOCK), lambda i: (i, 0)),
        out_shape=jax.ShapeDtypeStruct((OWNERS * BLOCK, BLOCK), bf16),
        compiler_params=SMALL,
        name="gate",
    )(mix, product, long_part, halo, rows)


def table_kernel(
    zl_ref, p0_ref, p1_ref, p2_ref, p3_ref, forward_ref,
    spec_ref, step_ref, tail_ref, start_ref, decay_ref,
):
    params = (
        p0_ref[...]
        + pltpu.roll(p1_ref[...], 32, 1)
        + pltpu.roll(p2_ref[...], 64, 1)
        + pltpu.roll(p3_ref[...], 96, 1)
    )
    params = pltpu.roll(params, zl_ref[0] * 32, 1)
    rate = params[:MODES]
    weight = params[MODES:]
    decay_ref[...] = jnp.exp(-float(BLOCK) * rate)
    place = lax.broadcasted_iota(jnp.int32, (BLOCK, BLOCK), 0).astype(f32)
    row = lax.broadcasted_iota(jnp.int32, (8, BLOCK), 0).astype(f32)
    kernel = jnp.zeros((BLOCK, BLOCK), f32)
    for n in range(MODES):
        own = rate[n : n + 1]
        gain = weight[n : n + 1]
        kernel = kernel + gain * jnp.exp(-own * place)
        step_ref[n] = jnp.broadcast_to(jnp.exp(-8.0 * own), (8, BLOCK))
        tail_ref[n] = jnp.exp(-own * (7.0 - row))
        start_ref[n] = gain * jnp.exp(-own * (row + 1.0))
    high, low = split_pair(kernel)
    table = forward_ref[...]
    spec = mm(table, jnp.concatenate([high, high], axis=0)) + mm(table[:, :BLOCK], low)
    spec = spec * (1.0 / BLOCK)
    spec_ref[...] = jnp.concatenate([spec, spec], axis=1)


def make_tables(pieces, forward, zl_index):
    part = jax.ShapeDtypeStruct((MODES, 8, BLOCK), f32)
    return pl.pallas_call(
        table_kernel,
        grid_spec=pltpu.PrefetchScalarGridSpec(
            num_scalar_prefetch=1,
            grid=(1,),
            in_specs=[full((2 * MODES, BLOCK))] * 4 + [full(forward.shape)],
            out_specs=[full((2 * BLOCK, 2 * BLOCK))] + [full(part.shape)] * 3 + [full((MODES, BLOCK))],
        ),
        out_shape=[
            jax.ShapeDtypeStruct((2 * BLOCK, 2 * BLOCK), f32), part, part, part,
            jax.ShapeDtypeStruct((MODES, BLOCK), f32),
        ],
        compiler_params=SMALL,
        name="tables",
    )(zl_index, *pieces, forward)


def state_kernel(x_ref, step_ref, tail_ref, decay_ref, state_ref, run_ref):
    step = step_ref[...]
    tail = tail_ref[...]

    def one_block(b, carry):
        x = x_ref[b].astype(f32)
        state = jnp.zeros((MODES, 8, BLOCK), f32)
        for i in range(BLOCK // 8):
            state = state * step + x[8 * i : 8 * i + 8][None]
        state_ref[b] = jnp.sum(state * tail, axis=1)
        return carry

    lax.fori_loop(0, OWNERS, one_block, 0)
    decay = decay_ref[...]
    for y in range(SIDE):
        run = state_ref[SIDE * y]
        for x in range(1, SIDE):
            run = run * decay + state_ref[SIDE * y + x]
        run_ref[y] = run


def block_states(blocks, step, tail, decay):
    return pl.pallas_call(
        state_kernel,
        out_shape=[
            jax.ShapeDtypeStruct((OWNERS, MODES, BLOCK), f32),
            jax.ShapeDtypeStruct((SIDE, MODES, BLOCK), f32),
        ],
        compiler_params=SMALL,
        name="states",
    )(blocks, step, tail, decay)


def conv_kernel(x_ref, spec_ref, forward_ref, backward_ref, out_ref):
    for pair in range(OWNERS // 2):
        x = jnp.concatenate([x_ref[2 * pair], x_ref[2 * pair + 1]], axis=1)
        turned = mm(forward_ref[...], jnp.concatenate([x, x], axis=0))
        x_re, x_im = turned[:BLOCK], turned[BLOCK:]
        k_re, k_im = spec_ref[:BLOCK, :], spec_ref[BLOCK:, :]
        mixed = jnp.concatenate([x_re * k_re - x_im * k_im, x_re * k_im + x_im * k_re], axis=0)
        high, low = split_pair(mixed)
        both = mm(backward_ref[...], high)
        result = both[:BLOCK] + both[BLOCK:] + mm(backward_ref[:BLOCK, :], low)
        out_ref[2 * pair] = result[:, :BLOCK]
        out_ref[2 * pair + 1] = result[:, BLOCK:]


def convolve_blocks(blocks, spec, forward, backward):
    return pl.pallas_call(
        conv_kernel,
        out_shape=jax.ShapeDtypeStruct(blocks.shape, f32),
        compiler_params=SMALL,
        name="conv",
    )(blocks, spec, forward, backward)


def readout_kernel(
    zl_ref, inner_ref, state_ref, r0_ref, r1_ref, r2_ref, r3_ref, step_ref, start_ref, decay_ref,
    out_ref, runs_ref, enter_ref,
):
    own = zl_ref[0]
    for k, ref in enumerate((r0_ref, r1_ref, r2_ref, r3_ref)):
        runs_ref[(own + k) % SIDE] = ref[...]
    decay = decay_ref[...]
    squared = decay * decay
    run_decay = squared * squared
    state = jnp.zeros((MODES, BLOCK), f32)
    for y in range(SIDE):
        for zl in range(SIDE):

            @pl.when(own == zl)
            def _(state=state, y=y):
                enter_ref[SIDE * y] = state

            state = state * run_decay + runs_ref[zl, y]
        inside = enter_ref[SIDE * y]
        for x in range(1, SIDE):
            inside = inside * decay + state_ref[SIDE * y + x - 1]
            enter_ref[SIDE * y + x] = inside
    step = step_ref[...]

    def one_block(b, carry):
        share = start_ref[...] * enter_ref[b][:, None, :]
        for i in range(BLOCK // 16):
            parts = []
            for half in range(2):
                at = 16 * i + 8 * half
                parts.append(inner_ref[b, at : at + 8, :] + jnp.sum(share, axis=0))
                share = share * step
            out_ref[b, 16 * i : 16 * i + 16, :] = jnp.concatenate(parts, axis=0).astype(bf16)
        return carry

    lax.fori_loop(0, OWNERS, one_block, 0)


def add_states(inner, states, runs, step, start, decay, zl_index):
    return pl.pallas_call(
        readout_kernel,
        grid_spec=pltpu.PrefetchScalarGridSpec(
            num_scalar_prefetch=1,
            grid=(1,),
            in_specs=[full(inner.shape), full(states.shape)]
            + [full((SIDE, MODES, BLOCK))] * 4
            + [full(step.shape)] * 2
            + [full(decay.shape)],
            out_specs=full(inner.shape),
            scratch_shapes=[
                pltpu.VMEM((SIDE, SIDE, MODES, BLOCK), f32),
                pltpu.VMEM((OWNERS, MODES, BLOCK), f32),
            ],
        ),
        out_shape=jax.ShapeDtypeStruct(inner.shape, bf16),
        compiler_params=SMALL,
        name="readout",
    )(zl_index, inner, states, *runs, step, start, decay)


def body(projected, short_taps, skip_gain, residue, decay_rate):
    mp_index = lax.axis_index("mp").astype(jnp.int32).reshape(1)
    zl_index = lax.axis_index("zl").astype(jnp.int32).reshape(1)
    count = SIDE ** 3

    def from_zl(value, k):
        return lax.ppermute(value, "zl", [(zl, (zl - k) % SIDE) for zl in range(SIDE)])

    product, gate_mix, head, halo, rows, params = mix_streams(
        projected, short_taps, skip_gain, residue, decay_rate, mp_index
    )
    halo = lax.ppermute(halo, ("y", "zl", "x"), [(i, i + 1) for i in range(count - 1)])
    pieces = [params] + [from_zl(params, k) for k in range(1, SIDE)]
    product = finish_product(product, head, halo, rows)
    product, *pieces = lax.optimization_barrier((product, *pieces))
    blocks = lax.all_to_all(product, ("y", "x"), split_axis=0, concat_axis=0, tiled=True)
    forward, backward = transform_tables()
    spec, step, tail, start, decay = make_tables(pieces, forward, zl_index)
    states, run = block_states(blocks, step, tail, decay)
    runs = [run] + [from_zl(run, k) for k in range(1, SIDE)]
    inner = convolve_blocks(blocks, spec, forward, backward)
    result = add_states(inner, states, runs, step, start, decay, zl_index)
    long_part = lax.all_to_all(result, ("y", "x"), split_axis=0, concat_axis=0, tiled=True)
    return apply_gate(gate_mix, product, long_part, halo, rows)


def solution(mesh):
    split = Mesh(mesh.devices.reshape(SIDE, SIDE, SIDE, -1), ("y", "zl", "x", "mp"))
    seq = ("y", "zl", "x")
    in_specs = (P(None, "mp", seq), P(), P(), P(seq, None), P(seq, None))
    out_specs = P("mp", seq)
    return jax.shard_map(body, mesh=split, in_specs=in_specs, out_specs=out_specs, check_vma=False)
```

time: 231 us -> 63.3 us (0.27); the launches traced: 227 us -> 62.7 us
  waiting for transfers between devices: 65.3 us -> 13.8 us
  local copies, waits for them, and re-layouts: 50.6 us -> 2.16 us
  matrix products: 41.7 us -> 0 us
  blocking collectives: 42.6 us -> 13 us
  Pallas kernels: 0 us -> 14.4 us
  other arithmetic: 7.44 us -> 0 us
    all_to_all x2 -> x1, waiting for transfers between devices: 65.3 us -> 8.19 us  [body(): lax.all_to_all(product, ('y', 'x'), split_axis=0, concat_axis=0, tiled=True)]
    dot_general x18 -> x0, matrix products: 41.7 us -> none  [the longest x2 6.19 us: forward(): jnp.einsum('mcb,bd->mcd', turned_im, inner_table[0], precision=exact_mode)]
    all_to_all x2 -> x1, blocking collectives: 42.6 us -> 13 us  [body(): lax.all_to_all(result, ('y', 'x'), split_axis=0, concat_axis=0, tiled=True)]
    unnamed x15 -> x10, local copies, waits for them, and re-layouts: 21.5 us -> 2.16 us
    pallas_call x0 -> x7, Pallas kernels: none -> 14.4 us  [the longest x1 4.29 us: mix_streams(): pl.pallas_call(mix_kernel, grid_spec=pltpu.PrefetchScalarGridSpec(num_sca...]
    all_to_all x4 -> x0, local copies, waits for them, and re-layouts: 13.4 us -> none  [the longest x1 9.86 us: from_channels(): lax.all_to_all(arranged, 'seq', split_axis=3, concat_axis=0, tiled=True)]
    ppermute x0 -> x7, starting transfers between devices: none -> 12.1 us  [the longest x6 8.6 us: from_zl(): lax.ppermute(value, 'zl', [(zl, (zl - k) % SIDE) for zl in range(SIDE)])]
    convert_element_type x2 -> x0, local copies, waits for them, and re-layouts: 12 us -> none  [the longest x1 9.63 us: body(): return from_channels((mixed[0] * total).astype(jnp.bfloat16))]
  transfers between devices with their start and end apart: 2 -> 8, of which waited for: 2 -> 5; matrix products, arithmetic and copies ran while one was open for 5% -> 0% of each run, Pallas kernels for 0% -> 6%
where the time goes in v2:
time: 63.3 us; the launch traced here: 62.7 us
  starting transfers between devices  19.3 us (30%)
  Pallas kernels  14.4 us (23%)
  waiting for transfers between devices  13.8 us (22%)
  blocking collectives  13 us (21%)
  local copies, waits for them, and re-layouts  2.16 us (3%)
    all_to_all x1, blocking collectives, body(): lax.all_to_all(result, ('y', 'x'), split_axis=0, concat_axis=0, tiled=True)  13 us
    ppermute x6, starting transfers between devices, from_zl(): lax.ppermute(value, 'zl', [(zl, (zl - k) % SIDE) for zl in range(SIDE)])  8.6 us
    all_to_all x1, waiting for transfers between devices, body(): lax.all_to_all(product, ('y', 'x'), split_axis=0, concat_axis=0, tiled=True)  8.19 us
    all_to_all x1, starting transfers between devices, body(): lax.all_to_all(product, ('y', 'x'), split_axis=0, concat_axis=0, tiled=True)  7.18 us
    ppermute x6, waiting for transfers between devices, from_zl(): lax.ppermute(value, 'zl', [(zl, (zl - k) % SIDE) for zl in range(SIDE)])  5.57 us
    pallas_call x1, Pallas kernels, mix_streams(): pl.pallas_call(mix_kernel, grid_spec=pltpu.PrefetchScalarGridSpec(num_sca...  4.29 us
    ppermute x1, starting transfers between devices, body(): lax.ppermute(halo, ('y', 'zl', 'x'), [(i, i + 1) for i in range(count - 1)])  3.52 us
    pallas_call x1, Pallas kernels, apply_gate(): pl.pallas_call(gate_kernel, grid=(4,), in_specs=[tile(BLOCK), tile(BLOCK)...  3.4 us
  transfers between devices with their start and end apart: 8, of which 5 were waited for; matrix products, arithmetic and copies ran while one was open for 0% of the time, Pallas kernels for 6%

profile of v2, /device:TPU:2, one launch (start us, length us, event | category | flops | bytes accessed | tf_op | source)
XLA Modules:
  0.0 62.7 jit_solution(79381930363234840)
XLA Ops:
  0.0 0.0 copy-start.2
  0.0 0.8 %copy-done.2 = f32[8192]{0:T(1024)S(1)} copy-done((f32[8192]{0:T(1024)S(1)}, f32[8192]{0:T(1024)}, u32[]{:S(2)}) %copy-start.2) | copy-done | bytes 32792
  0.8 0.0 copy-start.3
  0.8 0.7 %copy-done.3 = f32[32,16]{0,1:T(8,128)S(1)} copy-done((f32[32,16]{0,1:T(8,128)S(1)}, f32[32,16]{0,1:T(8,128)}, u32[]{:S(2)}) %copy-start.3) | copy-done | bytes 2072
  1.5 0.0 copy-start.4
  1.5 0.7 %copy-done.4 = f32[32,16]{0,1:T(8,128)S(1)} copy-done((f32[32,16]{0,1:T(8,128)S(1)}, f32[32,16]{0,1:T(8,128)}, u32[]{:S(2)}) %copy-start.4) | copy-done | bytes 2072
  2.2 4.3 %mix.1 = (bf16[16,128,128]{2,1,0:T(8,128)(2,1)}, f32[16,128,128]{2,1,0:T(8,128)S(1)}, f32[2,16,8,128]{3,2,1,0:T(8,128)S(1)}, f32[16,8,128]{2,1,0:T(8,128)S(1)}, ...) custom-call(s32[1]{0:T(128)} %bitcast.mp_ref, bf16[3,2048,128]{2,1,0:T(8,128)(2,1)} %x_ref.1, f32[3,3,8192]{2,1,0:T(4,128)} %taps_ref.1, ...), custom_call_target="tpu_custom_call" | custom-call | tf_op jit(solution)/shard_map/mix/pallas_call | solution.py:107
  6.4 0.0 copy-start
  6.5 3.5 %collective-permute-start = (f32[16,8,128]{2,1,0:T(8,128)S(1)}, f32[16,8,128]{2,1,0:T(8,128)S(1)}, u32[]{:S(2)}, u32[]{:S(2)}) collective-permute-start(f32[16,8,128]{2,1,0:T(8,128)S(1)} %get-tuple-element.26), channel_id=1, source_target_pairs={{0,4},{4,8},{8,12},{12,16},{16,20},{20,24},{24,28},{28,32},{32,36}... | collective-permute-start | bytes 196616 | tf_op jit(solution)/shard_map/ppermute | solution.py:376
  10.0 4.7 %collective-permute-start.1 = (f32[32,128]{1,0:T(8,128)S(1)}, f32[32,128]{1,0:T(8,128)S(1)}, u32[]{:S(2)}, u32[]{:S(2)}) collective-permute-start(f32[32,128]{1,0:T(8,128)S(1)} %get-tuple-element.30.p0_ref), channel_id=1, source_target_pairs={{0,48},{16,0},{32,16},{48,32},{1,49},{17,1},{33,17},{49,33},{2,50}... | collective-permute-start | bytes 49160 | tf_op jit(solution)/shard_map/ppermute | solution.py:371
  14.7 0.0 collective-permute-start.2
  14.7 0.7 %collective-permute-start.3 = (f32[32,128]{1,0:T(8,128)S(1)}, f32[32,128]{1,0:T(8,128)S(1)}, u32[]{:S(2)}, u32[]{:S(2)}) collective-permute-start(f32[32,128]{1,0:T(8,128)S(1)} %get-tuple-element.30.p0_ref), channel_id=1, source_target_pairs={{0,16},{16,32},{32,48},{48,0},{1,17},{17,33},{33,49},{49,1},{2,18}... | collective-permute-start | bytes 49160 | tf_op jit(solution)/shard_map/ppermute | solution.py:371
  15.4 0.0 collective-permute-done.halo_ref
  15.4 0.0 copy-start.1
  15.4 1.6 %head.1.product_ref = bf16[16,128,128]{2,1,0:T(8,128)(2,1)} custom-call(bf16[16,128,128]{2,1,0:T(8,128)(2,1)} %get-tuple-element.24.product_ref, f32[2,16,8,128]{3,2,1,0:T(8,128)S(1)} %get-tuple-element.25.head_ref, f32[16,8,128]{2,1,0:T(8,128)S(1)} %collective-permute-done.halo_ref, ...), custom_call_target="tpu_custom_call", output_to_operand_aliasing={{}: (0, {})} | custom-call | tf_op jit(solution)/shard_map/head/pallas_call | solution.py:162
  16.9 0.0 collective-permute-done.1.p1_ref
  16.9 2.4 %collective-permute-done.2.p2_ref = f32[32,128]{1,0:T(8,128)S(1)} collective-permute-done((f32[32,128]{1,0:T(8,128)S(1)}, f32[32,128]{1,0:T(8,128)S(1)}, u32[]{:S(2)}, u32[]{:S(2)}) %collective-permute-start.2) | collective-permute-done | bytes 16416 | tf_op jit(solution)/shard_map/ppermute | solution.py:371
  19.3 0.9 %collective-permute-done.3.p3_ref = f32[32,128]{1,0:T(8,128)S(1)} collective-permute-done((f32[32,128]{1,0:T(8,128)S(1)}, f32[32,128]{1,0:T(8,128)S(1)}, u32[]{:S(2)}, u32[]{:S(2)}) %collective-permute-start.3) | collective-permute-done | bytes 16416 | tf_op jit(solution)/shard_map/ppermute | solution.py:371
  20.2 7.2 %all-to-all-start = ((bf16[16,128,128]{2,1,0:T(8,128)(2,1)}), bf16[16,128,128]{2,1,0:T(8,128)(2,1)S(1)}, u32[]{:S(2)}, u32[]{:S(2)}) async-start(bf16[16,128,128]{2,1,0:T(8,128)(2,1)} %head.1.product_ref), calls=%async_computation | async-start | bytes 1048576 | tf_op jit(solution)/shard_map/all_to_all | solution.py:380
  27.4 0.0 copy-done
  27.4 0.5 tables.1
  27.9 8.2 %all-to-all-done.x_ref = bf16[16,128,128]{2,1,0:T(8,128)(2,1)S(1)} async-done(((bf16[16,128,128]{2,1,0:T(8,128)(2,1)}), bf16[16,128,128]{2,1,0:T(8,128)(2,1)S(1)}, u32[]{:S(2)}, u32[]{:S(2)}) %all-to-all-start) | async-done | bytes 524320 | tf_op jit(solution)/shard_map/all_to_all | solution.py:380
  36.1 1.5 %states.1 = (f32[16,16,128]{2,1,0:T(8,128)S(1)}, f32[4,16,128]{2,1,0:T(8,128)S(1)}) custom-call(bf16[16,128,128]{2,1,0:T(8,128)(2,1)S(1)} %all-to-all-done.x_ref, f32[16,8,128]{2,1,0:T(8,128)S(1)} %get-tuple-element.35.step_ref, f32[16,8,128]{2,1,0:T(8,128)S(1)} %get-tuple-element.36.tail_ref, f32[16,128]{1,0:T(8,128)S(1)} %get-tuple-element.37.decay_ref), custom_call_target="tpu_custom_call" | custom-call | tf_op jit(solution)/shard_map/states/pallas_call | solution.py:270
  37.6 0.7 %collective-permute-start.4 = (f32[4,16,128]{2,1,0:T(8,128)S(1)}, f32[4,16,128]{2,1,0:T(8,128)S(1)}, u32[]{:S(2)}, u32[]{:S(2)}) collective-permute-start(f32[4,16,128]{2,1,0:T(8,128)S(1)} %get-tuple-element.39.r0_ref), channel_id=1, source_target_pairs={{0,48},{16,0},{32,16},{48,32},{1,49},{17,1},{33,17},{49,33},{2,50}... | collective-permute-start | bytes 98312 | tf_op jit(solution)/shard_map/ppermute | solution.py:371
  38.3 0.8 %collective-permute-start.5 = (f32[4,16,128]{2,1,0:T(8,128)S(1)}, f32[4,16,128]{2,1,0:T(8,128)S(1)}, u32[]{:S(2)}, u32[]{:S(2)}) collective-permute-start(f32[4,16,128]{2,1,0:T(8,128)S(1)} %get-tuple-element.39.r0_ref), channel_id=1, source_target_pairs={{0,32},{16,48},{32,0},{48,16},{1,33},{17,49},{33,1},{49,17},{2,34}... | collective-permute-start | bytes 98312 | tf_op jit(solution)/shard_map/ppermute | solution.py:371
  39.1 1.8 %collective-permute-start.6 = (f32[4,16,128]{2,1,0:T(8,128)S(1)}, f32[4,16,128]{2,1,0:T(8,128)S(1)}, u32[]{:S(2)}, u32[]{:S(2)}) collective-permute-start(f32[4,16,128]{2,1,0:T(8,128)S(1)} %get-tuple-element.39.r0_ref), channel_id=1, source_target_pairs={{0,16},{16,32},{32,48},{48,0},{1,17},{17,33},{33,49},{49,1},{2,18}... | collective-permute-start | bytes 98312 | tf_op jit(solution)/shard_map/ppermute | solution.py:371
  40.8 0.0 copy-done.1
  40.8 1.6 %conv.1.inner_ref = f32[16,128,128]{2,1,0:T(8,128)S(1)} custom-call(bf16[16,128,128]{2,1,0:T(8,128)(2,1)S(1)} %all-to-all-done.x_ref, f32[256,256]{1,0:T(8,128)S(1)} %get-tuple-element.34.spec_ref, bf16[256,256]{1,0:T(8,128)(2,1)S(1)} %copy-done, bf16[256,256]{1,0:T(8,128)(2,1)S(1)} %copy-done.1), custom_call_target="tpu_custom_call" | custom-call | tf_op jit(solution)/shard_map/conv/pallas_call | solution.py:296
  42.5 0.0 collective-permute-done.4.r1_ref
  42.5 0.6 %collective-permute-done.5.r2_ref = f32[4,16,128]{2,1,0:T(8,128)S(1)} collective-permute-done((f32[4,16,128]{2,1,0:T(8,128)S(1)}, f32[4,16,128]{2,1,0:T(8,128)S(1)}, u32[]{:S(2)}, u32[]{:S(2)}) %collective-permute-start.5) | collective-permute-done | bytes 32800 | tf_op jit(solution)/shard_map/ppermute | solution.py:371
  43.1 1.6 %collective-permute-done.6.r3_ref = f32[4,16,128]{2,1,0:T(8,128)S(1)} collective-permute-done((f32[4,16,128]{2,1,0:T(8,128)S(1)}, f32[4,16,128]{2,1,0:T(8,128)S(1)}, u32[]{:S(2)}, u32[]{:S(2)}) %collective-permute-start.6) | collective-permute-done | bytes 32800 | tf_op jit(solution)/shard_map/ppermute | solution.py:371
  44.8 1.5 %readout.1 = bf16[16,128,128]{2,1,0:T(8,128)(2,1)S(1)} custom-call(s32[1]{0:T(128)} %bitcast.4.zl_ref, f32[16,128,128]{2,1,0:T(8,128)S(1)} %conv.1.inner_ref, f32[16,16,128]{2,1,0:T(8,128)S(1)} %get-tuple-element.38.state_ref, f32[4,16,128]{2,1,0:T(8,128)S(1)} %get-tuple-element.39.r0_ref, f32[4,16,128]{2,1,0:T(8,128)S(1)} %collective-permute-done.4.r1_ref, ...), custom_call_target="tpu_custom_call" | custom-call | tf_op jit(solution)/shard_map/readout/pallas_call | solution.py:344
  46.3 13.0 %all_to_all.10.long_ref = bf16[16,128,128]{2,1,0:T(8,128)(2,1)S(1)} all-to-all(bf16[16,128,128]{2,1,0:T(8,128)(2,1)S(1)} %readout.1), channel_id=1, replica_groups=mesh['y'=4,'zl'=4,'x'=4,'mp'=4] {'y','x'}, dimensions={0} | all-to-all | bytes 1048576 | tf_op jit(solution)/shard_map/all_to_all | solution.py:387
  59.3 3.4 %gate.1 = bf16[2048,128]{1,0:T(8,128)(2,1)} custom-call(f32[16,128,128]{2,1,0:T(8,128)S(1)} %get-tuple-element.23.mix_ref, bf16[16,128,128]{2,1,0:T(8,128)(2,1)} %head.1.product_ref, bf16[16,128,128]{2,1,0:T(8,128)(2,1)S(1)} %all_to_all.10.long_ref, f32[16,8,128]{2,1,0:T(8,128)S(1)} %collective-permute-done.halo_ref, ...), custom_call_target="tpu_custom_call" | custom-call | tf_op jit(solution)/shard_map/gate/pallas_call | solution.py:187
Async XLA Ops:
  0.0 0.8 %copy-start.2 = (f32[8192]{0:T(1024)S(1)}, f32[8192]{0:T(1024)}, u32[]{:S(2)}) copy-start(f32[8192]{0:T(1024)} %param.9) | copy-start | bytes 98308
  0.8 0.7 %copy-start.3 = (f32[32,16]{0,1:T(8,128)S(1)}, f32[32,16]{0,1:T(8,128)}, u32[]{:S(2)}) copy-start(f32[32,16]{0,1:T(8,128)} %param.10) | copy-start | bytes 6148
  1.5 0.7 %copy-start.4 = (f32[32,16]{0,1:T(8,128)S(1)}, f32[32,16]{0,1:T(8,128)}, u32[]{:S(2)}) copy-start(f32[32,16]{0,1:T(8,128)} %param.11) | copy-start | bytes 6148
  6.4 21.0 %copy-start = (bf16[256,256]{1,0:T(8,128)(2,1)S(1)}, bf16[256,256]{1,0:T(8,128)(2,1)}, u32[]{:S(2)}) copy-start(bf16[256,256]{1,0:T(8,128)(2,1)} %constant.12.clone.forward_ref) | copy-start | bytes 393220
  6.5 8.9 %collective-permute-start = (f32[16,8,128]{2,1,0:T(8,128)S(1)}, f32[16,8,128]{2,1,0:T(8,128)S(1)}, u32[]{:S(2)}, u32[]{:S(2)}) collective-permute-start(f32[16,8,128]{2,1,0:T(8,128)S(1)} %get-tuple-element.26), channel_id=1, source_target_pairs={{0,4},{4,8},{8,12},{12,16},{16,20},{20,24},{24,28},{28,32},{32,36}... | collective-permute-start | bytes 196616 | tf_op jit(solution)/shard_map/ppermute | solution.py:376
  10.0 7.0 %collective-permute-start.1 = (f32[32,128]{1,0:T(8,128)S(1)}, f32[32,128]{1,0:T(8,128)S(1)}, u32[]{:S(2)}, u32[]{:S(2)}) collective-permute-start(f32[32,128]{1,0:T(8,128)S(1)} %get-tuple-element.30.p0_ref), channel_id=1, source_target_pairs={{0,48},{16,0},{32,16},{48,32},{1,49},{17,1},{33,17},{49,33},{2,50}... | collective-permute-start | bytes 49160 | tf_op jit(solution)/shard_map/ppermute | solution.py:371
  14.7 4.6 %collective-permute-start.2 = (f32[32,128]{1,0:T(8,128)S(1)}, f32[32,128]{1,0:T(8,128)S(1)}, u32[]{:S(2)}, u32[]{:S(2)}) collective-permute-start(f32[32,128]{1,0:T(8,128)S(1)} %get-tuple-element.30.p0_ref), channel_id=1, source_target_pairs={{0,32},{16,48},{32,0},{48,16},{1,33},{17,49},{33,1},{49,17},{2,34}... | collective-permute-start | bytes 49160 | tf_op jit(solution)/shard_map/ppermute | solution.py:371
  14.7 5.5 %collective-permute-start.3 = (f32[32,128]{1,0:T(8,128)S(1)}, f32[32,128]{1,0:T(8,128)S(1)}, u32[]{:S(2)}, u32[]{:S(2)}) collective-permute-start(f32[32,128]{1,0:T(8,128)S(1)} %get-tuple-element.30.p0_ref), channel_id=1, source_target_pairs={{0,16},{16,32},{32,48},{48,0},{1,17},{17,33},{33,49},{49,1},{2,18}... | collective-permute-start | bytes 49160 | tf_op jit(solution)/shard_map/ppermute | solution.py:371
  15.4 25.5 %copy-start.1 = (bf16[256,256]{1,0:T(8,128)(2,1)S(1)}, bf16[256,256]{1,0:T(8,128)(2,1)}, u32[]{:S(2)}) copy-start(bf16[256,256]{1,0:T(8,128)(2,1)} %constant.13.clone.backward_ref) | copy-start | bytes 393220
  20.2 15.9 %all-to-all-start = ((bf16[16,128,128]{2,1,0:T(8,128)(2,1)}), bf16[16,128,128]{2,1,0:T(8,128)(2,1)S(1)}, u32[]{:S(2)}, u32[]{:S(2)}) async-start(bf16[16,128,128]{2,1,0:T(8,128)(2,1)} %head.1.product_ref), calls=%async_computation | async-start | bytes 1048576 | tf_op jit(solution)/shard_map/all_to_all | solution.py:380
  37.6 4.9 %collective-permute-start.4 = (f32[4,16,128]{2,1,0:T(8,128)S(1)}, f32[4,16,128]{2,1,0:T(8,128)S(1)}, u32[]{:S(2)}, u32[]{:S(2)}) collective-permute-start(f32[4,16,128]{2,1,0:T(8,128)S(1)} %get-tuple-element.39.r0_ref), channel_id=1, source_target_pairs={{0,48},{16,0},{32,16},{48,32},{1,49},{17,1},{33,17},{49,33},{2,50}... | collective-permute-start | bytes 98312 | tf_op jit(solution)/shard_map/ppermute | solution.py:371
  38.3 4.8 %collective-permute-start.5 = (f32[4,16,128]{2,1,0:T(8,128)S(1)}, f32[4,16,128]{2,1,0:T(8,128)S(1)}, u32[]{:S(2)}, u32[]{:S(2)}) collective-permute-start(f32[4,16,128]{2,1,0:T(8,128)S(1)} %get-tuple-element.39.r0_ref), channel_id=1, source_target_pairs={{0,32},{16,48},{32,0},{48,16},{1,33},{17,49},{33,1},{49,17},{2,34}... | collective-permute-start | bytes 98312 | tf_op jit(solution)/shard_map/ppermute | solution.py:371
  39.1 5.7 %collective-permute-start.6 = (f32[4,16,128]{2,1,0:T(8,128)S(1)}, f32[4,16,128]{2,1,0:T(8,128)S(1)}, u32[]{:S(2)}, u32[]{:S(2)}) collective-permute-start(f32[4,16,128]{2,1,0:T(8,128)S(1)} %get-tuple-element.39.r0_ref), channel_id=1, source_target_pairs={{0,16},{16,32},{32,48},{48,0},{1,17},{17,33},{33,49},{49,1},{2,18}... | collective-permute-start | bytes 98312 | tf_op jit(solution)/shard_map/ppermute | solution.py:371

commit v3 on v2

--- a/solution.py
+++ b/solution.py
@@ -54,92 +54,145 @@
     return pl.BlockSpec(shape, lambda *_: (0,) * len(shape))
 
 
-def owner_rows(x):
-    return [slice(128 * zl + 32 * x, 128 * zl + 32 * x + 32) for zl in range(SIDE)]
+def short_mix(moved, rows, stream):
+    return (
+        rows[stream : stream + 1] * moved[:BLOCK]
+        + rows[3 + stream : 4 + stream] * moved[BLOCK : 2 * BLOCK]
+        + rows[6 + stream : 7 + stream] * moved[2 * BLOCK :]
+    )
+
+
+def owner_rows(g):
+    first = 512 * (g // SIDE) + 32 * (g % SIDE)
+    return [slice(first + 128 * zl, first + 128 * zl + 32) for zl in range(SIDE)]
 
 
 def mix_kernel(
-    mp_ref, x_ref, taps_ref, skip_ref, residue_ref, rate_ref,
-    product_ref, gate_ref, head_ref, halo_ref, rows_ref, params_ref,
+    mp_ref, x_hbm, taps_hbm, skip_hbm, residue_hbm, rate_hbm,
+    product_hbm, head_ref, halo_ref, rows_ref, params_ref,
+    x_ref, taps_ref, skip_ref, residue_ref, rate_ref, product_ref, small_sems, x_sems, out_sems,
 ):
+    span = OWNERS * BLOCK
+    at = pl.multiple_of(mp_ref[0] * span, span)
+    small = [
+        pltpu.make_async_copy(source, target, small_sems.at[i])
+        for i, (source, target) in enumerate(
+            (
+                (taps_hbm.at[:, :, pl.ds(at, span)], taps_ref),
+                (skip_hbm.at[:, pl.ds(at, span)], skip_ref),
+                (residue_hbm, residue_ref),
+                (rate_hbm, rate_ref),
+            )
+        )
+    ]
+    large = [
+        [
+            pltpu.make_async_copy(
+                x_hbm.at[stream, pl.ds(512 * y, 512)],
+                x_ref.at[stream, pl.ds(512 * y, 512)],
+                x_sems.at[y, stream],
+            )
+            for stream in range(3)
+        ]
+        for y in range(SIDE)
+    ]
+    out = [
+        pltpu.make_async_copy(
+            product_ref.at[pl.ds(SIDE * y, SIDE)], product_hbm.at[pl.ds(SIDE * y, SIDE)], out_sems.at[y]
+        )
+        for y in range(SIDE)
+    ]
+    for copy in small[:2] + large[0] + large[1] + large[2] + large[3] + small[2:]:
+        copy.start()
     shifts = shift_table()
+    last = lax.broadcasted_iota(jnp.int32, (16, BLOCK), 0) + (BLOCK - 2)
+    last = (last == lax.broadcasted_iota(jnp.int32, (16, BLOCK), 1)).astype(bf16)
     lane = lax.broadcasted_iota(jnp.int32, (16, BLOCK), 1) // 32
-    table = jnp.concatenate(
-        [taps_ref[0], taps_ref[1], taps_ref[2], skip_ref[...], jnp.zeros((6, 4 * BLOCK), f32)], axis=0
-    )
-    for x in range(SIDE):
-        rows = jnp.zeros((16, BLOCK), f32)
-        for zl in range(SIDE):
-            piece = table[:, zl * BLOCK : (zl + 1) * BLOCK]
-            if zl != x:
-                piece = pltpu.roll(piece, (32 * (zl - x)) % BLOCK, 1)
-            rows = jnp.where(lane == zl, piece, rows)
-        rows_ref[x] = rows
-        mixes = []
-        for stream in range(3):
-            tile = jnp.concatenate([x_ref[stream, span, :] for span in owner_rows(x)], axis=0)
-            moved = mm_nt(shifts, tile)
-            halo_ref[x, 2 * stream : 2 * stream + 2, :] = moved[BLOCK - 2 : BLOCK]
-            mixes.append(
-                rows[stream : stream + 1] * moved[:BLOCK]
-                + rows[3 + stream : 4 + stream] * moved[BLOCK : 2 * BLOCK]
-                + rows[6 + stream : 7 + stream] * moved[2 * BLOCK :]
-            )
-        halo_ref[x, 6:8, :] = jnp.zeros((2, BLOCK), f32)
-        gate_ref[x] = mixes[0]
-        head_ref[0, x] = mixes[1][:8]
-        head_ref[1, x] = mixes[2][:8]
-        product_ref[x] = (mixes[1] * mixes[2]).astype(bf16)
-
-    @pl.when(pl.program_id(0) == 0)
-    def _():
-        rate = rate_ref[...]
-        count = rate.shape[1]
-        params_ref[...] = jnp.zeros((2 * MODES, BLOCK), f32)
-        params_ref[:MODES, :count] = rate
-        params_ref[MODES:, :count] = residue_ref[...] * jnp.sqrt(rate)
+    small[0].wait()
+    small[1].wait()
+    for y in range(SIDE):
+        table = jnp.concatenate(
+            [taps_ref[lag, :, 512 * y : 512 * y + 512] for lag in range(3)]
+            + [skip_ref[:, 512 * y : 512 * y + 512], jnp.zeros((6, 4 * BLOCK), f32)],
+            axis=0,
+        )
+        for copy in large[y]:
+            copy.wait()
+        for x in range(SIDE):
+            g = SIDE * y + x
+            rows = jnp.zeros((16, BLOCK), f32)
+            for zl in range(SIDE):
+                piece = table[:, zl * BLOCK : (zl + 1) * BLOCK]
+                if zl != x:
+                    piece = pltpu.roll(piece, (32 * (zl - x)) % BLOCK, 1)
+                rows = jnp.where(lane == zl, piece, rows)
+            rows_ref[g] = rows
+            tiles = [
+                jnp.concatenate([x_ref[stream, span, :] for span in owner_rows(g)], axis=0)
+                for stream in range(3)
+            ]
+            halo_ref[g, 0:2, :] = mm_nt(last, tiles[0])[0:2]
+            mixes = []
+            for stream in (1, 2):
+                moved = mm_nt(shifts, tiles[stream])
+                halo_ref[g, 2 * stream : 2 * stream + 2, :] = moved[BLOCK - 2 : BLOCK]
+                mixes.append(short_mix(moved, rows, stream))
+                head_ref[stream - 1, g] = mixes[-1][:16]
+            halo_ref[g, 6:8, :] = jnp.zeros((2, BLOCK), f32)
+            product_ref[g] = (mixes[0] * mixes[1]).astype(bf16)
+        out[y].start()
+    small[2].wait()
+    small[3].wait()
+    rate = rate_ref[...]
+    count = rate.shape[1]
+    params_ref[...] = jnp.zeros((2 * MODES, BLOCK), f32)
+    params_ref[:MODES, :count] = rate
+    params_ref[MODES:, :count] = residue_ref[...] * jnp.sqrt(rate)
+    for copy in out:
+        copy.wait()
+
+
+def in_hbm(value):
+    return pltpu.with_memory_space_constraint(value, pltpu.HBM)
 
 
 def mix_streams(projected, short_taps, skip_gain, residue, decay_rate, mp_index):
-    tile = lambda n: pl.BlockSpec((4, n, BLOCK), lambda i, mp: (i, 0, 0))
-    projected = pltpu.with_memory_space_constraint(projected, pltpu.HBM)
-    short_taps = pltpu.with_memory_space_constraint(short_taps, pltpu.HBM)
+    span = OWNERS * BLOCK
+    anywhere = pl.BlockSpec(memory_space=pl.ANY)
+    whole = pl.BlockSpec(memory_space=pltpu.VMEM)
+    mode_shape = residue.shape[::-1]
     return pl.pallas_call(
         mix_kernel,
-        grid_spec=pltpu.PrefetchScalarGridSpec(
-            num_scalar_prefetch=1,
-            grid=(4,),
-            in_specs=[
-                pl.BlockSpec((3, 512, BLOCK), lambda i, mp: (0, i, 0)),
-                pl.BlockSpec((3, 3, 512), lambda i, mp: (0, 0, mp[0] * 4 + i)),
-                pl.BlockSpec((1, 512), lambda i, mp: (0, mp[0] * 4 + i)),
-                full(residue.shape[::-1]),
-                full(decay_rate.shape[::-1]),
-            ],
-            out_specs=[
-                tile(BLOCK),
-                tile(BLOCK),
-                pl.BlockSpec((2, 4, 8, BLOCK), lambda i, mp: (0, i, 0, 0)),
-                tile(8),
-                tile(16),
-                full((2 * MODES, BLOCK)),
-            ],
-        ),
+        in_specs=[pl.BlockSpec(memory_space=pltpu.SMEM)] + [anywhere] * 5,
+        out_specs=[anywhere] + [whole] * 4,
         out_shape=[
             jax.ShapeDtypeStruct((OWNERS, BLOCK, BLOCK), bf16),
-            jax.ShapeDtypeStruct((OWNERS, BLOCK, BLOCK), f32),
-            jax.ShapeDtypeStruct((2, OWNERS, 8, BLOCK), f32),
+            jax.ShapeDtypeStruct((2, OWNERS, 16, BLOCK), f32),
             jax.ShapeDtypeStruct((OWNERS, 8, BLOCK), f32),
             jax.ShapeDtypeStruct((OWNERS, 16, BLOCK), f32),
             jax.ShapeDtypeStruct((2 * MODES, BLOCK), f32),
         ],
+        scratch_shapes=[
+            pltpu.VMEM(projected.shape, bf16),
+            pltpu.VMEM((3, 3, span), f32),
+            pltpu.VMEM((1, span), f32),
+            pltpu.VMEM(mode_shape, f32),
+            pltpu.VMEM(mode_shape, f32),
+            pltpu.VMEM((OWNERS, BLOCK, BLOCK), bf16),
+            pltpu.SemaphoreType.DMA((4,)),
+            pltpu.SemaphoreType.DMA((SIDE, 3)),
+            pltpu.SemaphoreType.DMA((SIDE,)),
+        ],
         compiler_params=SMALL,
         name="mix",
-    )(mp_index, projected, short_taps, skip_gain.reshape(1, -1), residue.T, decay_rate.T)
+    )(
+        mp_index, in_hbm(projected), in_hbm(short_taps), in_hbm(skip_gain.reshape(1, -1)),
+        in_hbm(residue.T), in_hbm(decay_rate.T),
+    )
 
 
 def halo_term(halo, rows, stream):
-    at = lax.broadcasted_iota(jnp.int32, (8, BLOCK), 0)
+    at = lax.broadcasted_iota(jnp.int32, (16, BLOCK), 0)
     older = halo[2 * stream : 2 * stream + 1]
     newer = halo[2 * stream + 1 : 2 * stream + 2]
     one = rows[3 + stream : 4 + stream]
@@ -148,22 +201,23 @@
 
 
 def head_kernel(product_ref, head_ref, halo_ref, rows_ref, out_ref):
+    del product_ref
     for g in range(OWNERS):
         halo = halo_ref[g]
         rows = rows_ref[g]
         k_mix = head_ref[0, g] + halo_term(halo, rows, 1)
         v_mix = head_ref[1, g] + halo_term(halo, rows, 2)
-        rest = product_ref[g, 8:16, :].astype(f32)
-        out_ref[g] = jnp.concatenate([k_mix * v_mix, rest], axis=0).astype(bf16)
+        out_ref[g] = (k_mix * v_mix).astype(bf16)
 
 
 def finish_product(product, head, halo, rows):
-    top = pl.BlockSpec((OWNERS, 16, BLOCK), lambda i: (0, 0, 0))
     return pl.pallas_call(
         head_kernel,
         grid=(1,),
-        in_specs=[top, full(head.shape), full(halo.shape), full(rows.shape)],
-        out_specs=top,
+        in_specs=[
+            pl.BlockSpec(memory_space=pl.ANY), full(head.shape), full(halo.shape), full(rows.shape)
+        ],
+        out_specs=pl.BlockSpec((OWNERS, 16, BLOCK), lambda i: (0, 0, 0)),
         out_shape=jax.ShapeDtypeStruct(product.shape, bf16),
         input_output_aliases={0: 0},
         compiler_params=SMALL,
@@ -171,28 +225,60 @@
     )(product, head, halo, rows)
 
 
-def gate_kernel(mix_ref, product_ref, long_ref, halo_ref, rows_ref, out_ref):
+def prepare_kernel(q_ref, product_ref, halo_ref, rows_ref, mix_ref, direct_ref):
+    shifts = shift_table()
     for x in range(SIDE):
-        mix = mix_ref[x]
         rows = rows_ref[x]
-        mix = jnp.concatenate([mix[:8] + halo_term(halo_ref[x], rows, 0), mix[8:]], axis=0)
-        total = long_ref[x].astype(f32) + rows[9:10] * product_ref[x].astype(f32)
-        gated = (mix * total).T.astype(bf16)
-        for zl, span in enumerate(owner_rows(x)):
+        tile = jnp.concatenate([q_ref[0, span, :] for span in owner_rows(x)], axis=0)
+        mix = short_mix(mm_nt(shifts, tile), rows, 0)
+        mix_ref[x, :16, :] = mix[:16] + halo_term(halo_ref[x], rows, 0)
+        mix_ref[x, 16:, :] = mix[16:]
+        direct_ref[x] = rows[9:10] * product_ref[x].astype(f32)
+
+
+def prepare_gate(projected, product, halo, rows):
+    tile = lambda n: pl.BlockSpec((4, n, BLOCK), lambda i: (i, 0, 0))
+    return pl.pallas_call(
+        prepare_kernel,
+        grid=(4,),
+        in_specs=[
+            pl.BlockSpec((1, 512, BLOCK), lambda i: (0, i, 0)), tile(BLOCK), tile(8), tile(16)
+        ],
+        out_specs=[tile(BLOCK), tile(BLOCK)],
+        out_shape=[jax.ShapeDtypeStruct(product.shape, f32)] * 2,
+        compiler_params=SMALL,
+        name="prepare",
+    )(in_hbm(projected), product, halo, rows)
+
+
+def gate_kernel(mix_ref, direct_ref, long_ref, out_hbm, out_ref, sems):
+    copies = [
+        pltpu.make_async_copy(
+            out_ref.at[pl.ds(512 * y, 512)], out_hbm.at[pl.ds(512 * y, 512)], sems.at[y]
+        )
+        for y in range(SIDE)
+    ]
+    for g in range(OWNERS):
+        gated = (mix_ref[g] * (long_ref[g].astype(f32) + direct_ref[g])).astype(bf16).T
+        for zl, span in enumerate(owner_rows(g)):
             out_ref[span, :] = gated[32 * zl : 32 * zl + 32]
-
-
-def apply_gate(mix, product, long_part, halo, rows):
-    tile = lambda n: pl.BlockSpec((4, n, BLOCK), lambda i: (i, 0, 0))
+        if g % SIDE == SIDE - 1:
+            copies[g // SIDE].start()
+    for copy in copies:
+        copy.wait()
+
+
+def apply_gate(mix, direct, long_part):
+    shape = (OWNERS * BLOCK, BLOCK)
     return pl.pallas_call(
         gate_kernel,
-        grid=(4,),
-        in_specs=[tile(BLOCK), tile(BLOCK), tile(BLOCK), tile(8), tile(16)],
-        out_specs=pl.BlockSpec((512, BLOCK), lambda i: (i, 0)),
-        out_shape=jax.ShapeDtypeStruct((OWNERS * BLOCK, BLOCK), bf16),
+        in_specs=[pl.BlockSpec(memory_space=pltpu.VMEM)] * 3,
+        out_specs=pl.BlockSpec(memory_space=pl.ANY),
+        out_shape=jax.ShapeDtypeStruct(shape, bf16),
+        scratch_shapes=[pltpu.VMEM(shape, bf16), pltpu.SemaphoreType.DMA((SIDE,))],
         compiler_params=SMALL,
         name="gate",
-    )(mix, product, long_part, halo, rows)
+    )(mix, direct, long_part)
 
 
 def table_kernel(
@@ -370,7 +456,7 @@
     def from_zl(value, k):
         return lax.ppermute(value, "zl", [(zl, (zl - k) % SIDE) for zl in range(SIDE)])
 
-    product, gate_mix, head, halo, rows, params = mix_streams(
+    product, head, halo, rows, params = mix_streams(
         projected, short_taps, skip_gain, residue, decay_rate, mp_index
     )
     halo = lax.ppermute(halo, ("y", "zl", "x"), [(i, i + 1) for i in range(count - 1)])
@@ -378,6 +464,8 @@
     product = finish_product(product, head, halo, rows)
     product, *pieces = lax.optimization_barrier((product, *pieces))
     blocks = lax.all_to_all(product, ("y", "x"), split_axis=0, concat_axis=0, tiled=True)
+    gate_mix, direct = prepare_gate(projected, product, halo, rows)
+    blocks, gate_mix, direct = lax.optimization_barrier((blocks, gate_mix, direct))
     forward, backward = transform_tables()
     spec, step, tail, start, decay = make_tables(pieces, forward, zl_index)
     states, run = block_states(blocks, step, tail, decay)
@@ -385,7 +473,7 @@
     inner = convolve_blocks(blocks, spec, forward, backward)
     result = add_states(inner, states, runs, step, start, decay, zl_index)
     long_part = lax.all_to_all(result, ("y", "x"), split_axis=0, concat_axis=0, tiled=True)
-    return apply_gate(gate_mix, product, long_part, halo, rows)
+    return apply_gate(gate_mix, direct, long_part)
 
 
 def solution(mesh):

time: 63.3 us -> 58 us (0.916)
  local copies, waits for them, and re-layouts: 2.16 us -> 0.01 us
  waiting for transfers between devices: 13.8 us -> 11.7 us
  Pallas kernels: 14.4 us -> 13.5 us
    all_to_all x1, waiting for transfers between devices: 8.19 us -> 5.37 us  [body(): lax.all_to_all(product, ('y', 'x'), split_axis=0, concat_axis=0, tiled=True)]
    unnamed x10 -> x4, local copies, waits for them, and re-layouts: 2.16 us -> 0.01 us
    pallas_call x3 -> x4, Pallas kernels: 9.27 us -> 8.35 us  [the longest x1 3.95 us: mix_streams(): pl.pallas_call(mix_kernel, in_specs=[pl.BlockSpec(memory_space=pltpu.SMEM...]
    ppermute x6, waiting for transfers between devices: 5.57 us -> 6.3 us  [from_zl(): lax.ppermute(value, 'zl', [(zl, (zl - k) % SIDE) for zl in range(SIDE)])]
  transfers between devices with their start and end apart: 8 -> 8, of which waited for: 5 -> 6; matrix products, arithmetic and copies ran while one was open for 0% -> 0% of each run, Pallas kernels for 6% -> 10%
where the time goes in v3:
time: 58 us; the launch traced here: 57.7 us
  starting transfers between devices  19.3 us (33%)
  Pallas kernels  13.5 us (23%)
  blocking collectives  13.1 us (23%)
  waiting for transfers between devices  11.7 us (20%)
    all_to_all x1, blocking collectives, body(): lax.all_to_all(result, ('y', 'x'), split_axis=0, concat_axis=0, tiled=True)  13.1 us
    ppermute x6, starting transfers between devices, from_zl(): lax.ppermute(value, 'zl', [(zl, (zl - k) % SIDE) for zl in range(SIDE)])  8.6 us
    all_to_all x1, starting transfers between devices, body(): lax.all_to_all(product, ('y', 'x'), split_axis=0, concat_axis=0, tiled=True)  7.18 us
    ppermute x6, waiting for transfers between devices, from_zl(): lax.ppermute(value, 'zl', [(zl, (zl - k) % SIDE) for zl in range(SIDE)])  6.3 us
    all_to_all x1, waiting for transfers between devices, body(): lax.all_to_all(product, ('y', 'x'), split_axis=0, concat_axis=0, tiled=True)  5.37 us
    pallas_call x1, Pallas kernels, mix_streams(): pl.pallas_call(mix_kernel, in_specs=[pl.BlockSpec(memory_space=pltpu.SMEM...  3.95 us
    ppermute x1, starting transfers between devices, body(): lax.ppermute(halo, ('y', 'zl', 'x'), [(i, i + 1) for i in range(count - 1)])  3.53 us
    pallas_call x1, Pallas kernels, prepare_gate(): pl.pallas_call(prepare_kernel, grid=(4,), in_specs=[pl.BlockSpec((1, 512,...  2.8 us
  transfers between devices with their start and end apart: 8, of which 6 were waited for; matrix products, arithmetic and copies ran while one was open for 0% of the time, Pallas kernels for 10%

profile of v3, /device:TPU:2, one launch (start us, length us, event | category | flops | bytes accessed | tf_op | source)
XLA Modules:
  0.0 57.7 jit_solution(16046094800970602130)
XLA Ops:
  0.0 3.9 %mix.1 = (bf16[16,128,128]{2,1,0:T(8,128)(2,1)}, f32[2,16,16,128]{3,2,1,0:T(8,128)S(1)}, f32[16,8,128]{2,1,0:T(8,128)S(1)}, f32[16,16,128]{2,1,0:T(8,128)S(1)}, f32[32,128]{1,0:T(8,128)S(1)}) custom-call(s32[1]{0:T(128)} %bitcast.mp_ref, bf16[3,2048,128]{2,1,0:T(8,128)(2,1)} %q_ref.1, f32[3,3,8192]{2,1,0:T(4,128)} %taps_hbm.1, f32[1,8192]{1,0:T(1,128)} %bitcast.5, ...), custom_call_target="tpu_custom_call" | custom-call | tf_op jit(solution)/shard_map/mix/pallas_call | solution.py:164
  4.0 0.0 copy-start
  4.0 3.5 %collective-permute-start = (f32[16,8,128]{2,1,0:T(8,128)S(1)}, f32[16,8,128]{2,1,0:T(8,128)S(1)}, u32[]{:S(2)}, u32[]{:S(2)}) collective-permute-start(f32[16,8,128]{2,1,0:T(8,128)S(1)} %get-tuple-element.29), channel_id=1, source_target_pairs={{0,4},{4,8},{8,12},{12,16},{16,20},{20,24},{24,28},{28,32},{32,36}... | collective-permute-start | bytes 196616 | tf_op jit(solution)/shard_map/ppermute | solution.py:462
  7.5 4.7 %collective-permute-start.1 = (f32[32,128]{1,0:T(8,128)S(1)}, f32[32,128]{1,0:T(8,128)S(1)}, u32[]{:S(2)}, u32[]{:S(2)}) collective-permute-start(f32[32,128]{1,0:T(8,128)S(1)} %get-tuple-element.38.p0_ref), channel_id=1, source_target_pairs={{0,48},{16,0},{32,16},{48,32},{1,49},{17,1},{33,17},{49,33},{2,50}... | collective-permute-start | bytes 49160 | tf_op jit(solution)/shard_map/ppermute | solution.py:457
  12.2 0.0 collective-permute-start.2
  12.2 0.7 %collective-permute-start.3 = (f32[32,128]{1,0:T(8,128)S(1)}, f32[32,128]{1,0:T(8,128)S(1)}, u32[]{:S(2)}, u32[]{:S(2)}) collective-permute-start(f32[32,128]{1,0:T(8,128)S(1)} %get-tuple-element.38.p0_ref), channel_id=1, source_target_pairs={{0,16},{16,32},{32,48},{48,0},{1,17},{17,33},{33,49},{49,1},{2,18}... | collective-permute-start | bytes 49160 | tf_op jit(solution)/shard_map/ppermute | solution.py:457
  12.9 0.0 collective-permute-done.halo_ref
  12.9 0.7 %head.1.product_ref = bf16[16,128,128]{2,1,0:T(8,128)(2,1)} custom-call(bf16[16,128,128]{2,1,0:T(8,128)(2,1)} %get-tuple-element.27.product_ref, f32[2,16,16,128]{3,2,1,0:T(8,128)S(1)} %get-tuple-element.28.head_ref, f32[16,8,128]{2,1,0:T(8,128)S(1)} %collective-permute-done.halo_ref, ...), custom_call_target="tpu_custom_call", output_to_operand_aliasing={{}: (0, {})} | custom-call | tf_op jit(solution)/shard_map/head/pallas_call | solution.py:214
  13.6 0.1 collective-permute-done.1.p1_ref
  13.7 3.2 %collective-permute-done.2.p2_ref = f32[32,128]{1,0:T(8,128)S(1)} collective-permute-done((f32[32,128]{1,0:T(8,128)S(1)}, f32[32,128]{1,0:T(8,128)S(1)}, u32[]{:S(2)}, u32[]{:S(2)}) %collective-permute-start.2) | collective-permute-done | bytes 16416 | tf_op jit(solution)/shard_map/ppermute | solution.py:457
  16.8 0.9 %collective-permute-done.3.p3_ref = f32[32,128]{1,0:T(8,128)S(1)} collective-permute-done((f32[32,128]{1,0:T(8,128)S(1)}, f32[32,128]{1,0:T(8,128)S(1)}, u32[]{:S(2)}, u32[]{:S(2)}) %collective-permute-start.3) | collective-permute-done | bytes 16416 | tf_op jit(solution)/shard_map/ppermute | solution.py:457
  17.8 7.2 %all-to-all-start = ((bf16[16,128,128]{2,1,0:T(8,128)(2,1)}), bf16[16,128,128]{2,1,0:T(8,128)(2,1)S(1)}, u32[]{:S(2)}, u32[]{:S(2)}) async-start(bf16[16,128,128]{2,1,0:T(8,128)(2,1)} %head.1.product_ref), calls=%async_computation | async-start | bytes 1048576 | tf_op jit(solution)/shard_map/all_to_all | solution.py:466
  24.9 0.0 copy-done
  24.9 0.0 copy-start.1
  25.0 0.5 tables.1
  25.5 2.8 %prepare.1 = (f32[16,128,128]{2,1,0:T(8,128)S(1)}, f32[16,128,128]{2,1,0:T(8,128)S(1)}) custom-call(bf16[3,2048,128]{2,1,0:T(8,128)(2,1)} %q_ref.1, bf16[16,128,128]{2,1,0:T(8,128)(2,1)} %head.1.product_ref, f32[16,8,128]{2,1,0:T(8,128)S(1)} %collective-permute-done.halo_ref, f32[16,16,128]{2,1,0:T(8,128)S(1)} %get-tuple-element.30.rows_ref), custom_call_target="tpu_custom_call" | custom-call | tf_op jit(solution)/shard_map/prepare/pallas_call | solution.py:241
  28.3 5.4 %all-to-all-done.x_ref = bf16[16,128,128]{2,1,0:T(8,128)(2,1)S(1)} async-done(((bf16[16,128,128]{2,1,0:T(8,128)(2,1)}), bf16[16,128,128]{2,1,0:T(8,128)(2,1)S(1)}, u32[]{:S(2)}, u32[]{:S(2)}) %all-to-all-start) | async-done | bytes 524320 | tf_op jit(solution)/shard_map/all_to_all | solution.py:466
  33.7 1.5 %states.1 = (f32[16,16,128]{2,1,0:T(8,128)S(1)}, f32[4,16,128]{2,1,0:T(8,128)S(1)}) custom-call(bf16[16,128,128]{2,1,0:T(8,128)(2,1)S(1)} %all-to-all-done.x_ref, f32[16,8,128]{2,1,0:T(8,128)S(1)} %get-tuple-element.43.step_ref, f32[16,8,128]{2,1,0:T(8,128)S(1)} %get-tuple-element.44.tail_ref, f32[16,128]{1,0:T(8,128)S(1)} %get-tuple-element.45.decay_ref), custom_call_target="tpu_custom_call" | custom-call | tf_op jit(solution)/shard_map/states/pallas_call | solution.py:356
  35.1 0.7 %collective-permute-start.4 = (f32[4,16,128]{2,1,0:T(8,128)S(1)}, f32[4,16,128]{2,1,0:T(8,128)S(1)}, u32[]{:S(2)}, u32[]{:S(2)}) collective-permute-start(f32[4,16,128]{2,1,0:T(8,128)S(1)} %get-tuple-element.47.r0_ref), channel_id=1, source_target_pairs={{0,48},{16,0},{32,16},{48,32},{1,49},{17,1},{33,17},{49,33},{2,50}... | collective-permute-start | bytes 98312 | tf_op jit(solution)/shard_map/ppermute | solution.py:457
  35.9 0.6 %collective-permute-start.5 = (f32[4,16,128]{2,1,0:T(8,128)S(1)}, f32[4,16,128]{2,1,0:T(8,128)S(1)}, u32[]{:S(2)}, u32[]{:S(2)}) collective-permute-start(f32[4,16,128]{2,1,0:T(8,128)S(1)} %get-tuple-element.47.r0_ref), channel_id=1, source_target_pairs={{0,32},{16,48},{32,0},{48,16},{1,33},{17,49},{33,1},{49,17},{2,34}... | collective-permute-start | bytes 98312 | tf_op jit(solution)/shard_map/ppermute | solution.py:457
  36.4 1.9 %collective-permute-start.6 = (f32[4,16,128]{2,1,0:T(8,128)S(1)}, f32[4,16,128]{2,1,0:T(8,128)S(1)}, u32[]{:S(2)}, u32[]{:S(2)}) collective-permute-start(f32[4,16,128]{2,1,0:T(8,128)S(1)} %get-tuple-element.47.r0_ref), channel_id=1, source_target_pairs={{0,16},{16,32},{32,48},{48,0},{1,17},{17,33},{33,49},{49,1},{2,18}... | collective-permute-start | bytes 98312 | tf_op jit(solution)/shard_map/ppermute | solution.py:457
  38.4 0.0 copy-done.1
  38.4 1.6 %conv.1.inner_ref = f32[16,128,128]{2,1,0:T(8,128)S(1)} custom-call(bf16[16,128,128]{2,1,0:T(8,128)(2,1)S(1)} %all-to-all-done.x_ref, f32[256,256]{1,0:T(8,128)S(1)} %get-tuple-element.42.spec_ref, bf16[256,256]{1,0:T(8,128)(2,1)S(1)} %copy-done, bf16[256,256]{1,0:T(8,128)(2,1)S(1)} %copy-done.1), custom_call_target="tpu_custom_call" | custom-call | tf_op jit(solution)/shard_map/conv/pallas_call | solution.py:382
  40.0 0.0 collective-permute-done.4.r1_ref
  40.0 0.6 %collective-permute-done.5.r2_ref = f32[4,16,128]{2,1,0:T(8,128)S(1)} collective-permute-done((f32[4,16,128]{2,1,0:T(8,128)S(1)}, f32[4,16,128]{2,1,0:T(8,128)S(1)}, u32[]{:S(2)}, u32[]{:S(2)}) %collective-permute-start.5) | collective-permute-done | bytes 32800 | tf_op jit(solution)/shard_map/ppermute | solution.py:457
  40.7 1.5 %collective-permute-done.6.r3_ref = f32[4,16,128]{2,1,0:T(8,128)S(1)} collective-permute-done((f32[4,16,128]{2,1,0:T(8,128)S(1)}, f32[4,16,128]{2,1,0:T(8,128)S(1)}, u32[]{:S(2)}, u32[]{:S(2)}) %collective-permute-start.6) | collective-permute-done | bytes 32800 | tf_op jit(solution)/shard_map/ppermute | solution.py:457
  42.2 1.5 %readout.1 = bf16[16,128,128]{2,1,0:T(8,128)(2,1)S(1)} custom-call(s32[1]{0:T(128)} %bitcast.4.zl_ref, f32[16,128,128]{2,1,0:T(8,128)S(1)} %conv.1.inner_ref, f32[16,16,128]{2,1,0:T(8,128)S(1)} %get-tuple-element.46.state_ref, f32[4,16,128]{2,1,0:T(8,128)S(1)} %get-tuple-element.47.r0_ref, f32[4,16,128]{2,1,0:T(8,128)S(1)} %collective-permute-done.4.r1_ref, ...), custom_call_target="tpu_custom_call" | custom-call | tf_op jit(solution)/shard_map/readout/pallas_call | solution.py:430
  43.7 13.1 %all_to_all.10.long_ref = bf16[16,128,128]{2,1,0:T(8,128)(2,1)S(1)} all-to-all(bf16[16,128,128]{2,1,0:T(8,128)(2,1)S(1)} %readout.1), channel_id=1, replica_groups=mesh['y'=4,'zl'=4,'x'=4,'mp'=4] {'y','x'}, dimensions={0} | all-to-all | bytes 1048576 | tf_op jit(solution)/shard_map/all_to_all | solution.py:475
  56.8 0.9 %gate.1 = bf16[2048,128]{1,0:T(8,128)(2,1)} custom-call(f32[16,128,128]{2,1,0:T(8,128)S(1)} %get-tuple-element.35.mix_ref, f32[16,128,128]{2,1,0:T(8,128)S(1)} %get-tuple-element.36.direct_ref, bf16[16,128,128]{2,1,0:T(8,128)(2,1)S(1)} %all_to_all.10.long_ref), custom_call_target="tpu_custom_call" | custom-call | tf_op jit(solution)/shard_map/gate/pallas_call | solution.py:273
Async XLA Ops:
  4.0 21.0 %copy-start = (bf16[256,256]{1,0:T(8,128)(2,1)S(1)}, bf16[256,256]{1,0:T(8,128)(2,1)}, u32[]{:S(2)}) copy-start(bf16[256,256]{1,0:T(8,128)(2,1)} %constant.12.clone.forward_ref) | copy-start | bytes 393220
  4.0 8.9 %collective-permute-start = (f32[16,8,128]{2,1,0:T(8,128)S(1)}, f32[16,8,128]{2,1,0:T(8,128)S(1)}, u32[]{:S(2)}, u32[]{:S(2)}) collective-permute-start(f32[16,8,128]{2,1,0:T(8,128)S(1)} %get-tuple-element.29), channel_id=1, source_target_pairs={{0,4},{4,8},{8,12},{12,16},{16,20},{20,24},{24,28},{28,32},{32,36}... | collective-permute-start | bytes 196616 | tf_op jit(solution)/shard_map/ppermute | solution.py:462
  7.5 6.1 %collective-permute-start.1 = (f32[32,128]{1,0:T(8,128)S(1)}, f32[32,128]{1,0:T(8,128)S(1)}, u32[]{:S(2)}, u32[]{:S(2)}) collective-permute-start(f32[32,128]{1,0:T(8,128)S(1)} %get-tuple-element.38.p0_ref), channel_id=1, source_target_pairs={{0,48},{16,0},{32,16},{48,32},{1,49},{17,1},{33,17},{49,33},{2,50}... | collective-permute-start | bytes 49160 | tf_op jit(solution)/shard_map/ppermute | solution.py:457
  12.2 4.6 %collective-permute-start.2 = (f32[32,128]{1,0:T(8,128)S(1)}, f32[32,128]{1,0:T(8,128)S(1)}, u32[]{:S(2)}, u32[]{:S(2)}) collective-permute-start(f32[32,128]{1,0:T(8,128)S(1)} %get-tuple-element.38.p0_ref), channel_id=1, source_target_pairs={{0,32},{16,48},{32,0},{48,16},{1,33},{17,49},{33,1},{49,17},{2,34}... | collective-permute-start | bytes 49160 | tf_op jit(solution)/shard_map/ppermute | solution.py:457
  12.2 5.5 %collective-permute-start.3 = (f32[32,128]{1,0:T(8,128)S(1)}, f32[32,128]{1,0:T(8,128)S(1)}, u32[]{:S(2)}, u32[]{:S(2)}) collective-permute-start(f32[32,128]{1,0:T(8,128)S(1)} %get-tuple-element.38.p0_ref), channel_id=1, source_target_pairs={{0,16},{16,32},{32,48},{48,0},{1,17},{17,33},{33,49},{49,1},{2,18}... | collective-permute-start | bytes 49160 | tf_op jit(solution)/shard_map/ppermute | solution.py:457
  17.8 15.9 %all-to-all-start = ((bf16[16,128,128]{2,1,0:T(8,128)(2,1)}), bf16[16,128,128]{2,1,0:T(8,128)(2,1)S(1)}, u32[]{:S(2)}, u32[]{:S(2)}) async-start(bf16[16,128,128]{2,1,0:T(8,128)(2,1)} %head.1.product_ref), calls=%async_computation | async-start | bytes 1048576 | tf_op jit(solution)/shard_map/all_to_all | solution.py:466
  24.9 13.4 %copy-start.1 = (bf16[256,256]{1,0:T(8,128)(2,1)S(1)}, bf16[256,256]{1,0:T(8,128)(2,1)}, u32[]{:S(2)}) copy-start(bf16[256,256]{1,0:T(8,128)(2,1)} %constant.13.clone.backward_ref) | copy-start | bytes 393220
  35.1 4.9 %collective-permute-start.4 = (f32[4,16,128]{2,1,0:T(8,128)S(1)}, f32[4,16,128]{2,1,0:T(8,128)S(1)}, u32[]{:S(2)}, u32[]{:S(2)}) collective-permute-start(f32[4,16,128]{2,1,0:T(8,128)S(1)} %get-tuple-element.47.r0_ref), channel_id=1, source_target_pairs={{0,48},{16,0},{32,16},{48,32},{1,49},{17,1},{33,17},{49,33},{2,50}... | collective-permute-start | bytes 98312 | tf_op jit(solution)/shard_map/ppermute | solution.py:457
  35.9 4.8 %collective-permute-start.5 = (f32[4,16,128]{2,1,0:T(8,128)S(1)}, f32[4,16,128]{2,1,0:T(8,128)S(1)}, u32[]{:S(2)}, u32[]{:S(2)}) collective-permute-start(f32[4,16,128]{2,1,0:T(8,128)S(1)} %get-tuple-element.47.r0_ref), channel_id=1, source_target_pairs={{0,32},{16,48},{32,0},{48,16},{1,33},{17,49},{33,1},{49,17},{2,34}... | collective-permute-start | bytes 98312 | tf_op jit(solution)/shard_map/ppermute | solution.py:457
  36.4 5.7 %collective-permute-start.6 = (f32[4,16,128]{2,1,0:T(8,128)S(1)}, f32[4,16,128]{2,1,0:T(8,128)S(1)}, u32[]{:S(2)}, u32[]{:S(2)}) collective-permute-start(f32[4,16,128]{2,1,0:T(8,128)S(1)} %get-tuple-element.47.r0_ref), channel_id=1, source_target_pairs={{0,16},{16,32},{32,48},{48,0},{1,17},{17,33},{33,49},{49,1},{2,18}... | collective-permute-start | bytes 98312 | tf_op jit(solution)/shard_map/ppermute | solution.py:457

commit v4 on v3

--- a/solution.py
+++ b/solution.py
@@ -34,12 +34,6 @@
     return jnp.asarray(forward), jnp.asarray(backward)
 
 
-def shift_table():
-    row = lax.broadcasted_iota(jnp.int32, (BLOCK, BLOCK), 0)
-    column = lax.broadcasted_iota(jnp.int32, (BLOCK, BLOCK), 1)
-    return jnp.concatenate([(row - lag == column).astype(bf16) for lag in range(3)], axis=0)
-
-
 def mm(left, right):
     return lax.dot_general(left, right, (((1,), (0,)), ((), ())), preferred_element_type=f32)
 
@@ -54,17 +48,27 @@
     return pl.BlockSpec(shape, lambda *_: (0,) * len(shape))
 
 
-def short_mix(moved, rows, stream):
+def later(value, steps):
+    moved = pltpu.roll(value, steps, 0)
+    row = lax.broadcasted_iota(jnp.int32, (8, BLOCK), 0)
+    return jnp.concatenate([jnp.where(row < steps, 0.0, moved[:8]), moved[8:]], axis=0)
+
+
+def short_mix(block, rows, stream):
     return (
-        rows[stream : stream + 1] * moved[:BLOCK]
-        + rows[3 + stream : 4 + stream] * moved[BLOCK : 2 * BLOCK]
-        + rows[6 + stream : 7 + stream] * moved[2 * BLOCK :]
+        rows[stream : stream + 1] * block
+        + rows[3 + stream : 4 + stream] * later(block, 1)
+        + rows[6 + stream : 7 + stream] * later(block, 2)
     )
 
 
 def owner_rows(g):
     first = 512 * (g // SIDE) + 32 * (g % SIDE)
     return [slice(first + 128 * zl, first + 128 * zl + 32) for zl in range(SIDE)]
+
+
+def owner_tile(x_ref, stream, g):
+    return jnp.concatenate([x_ref[stream, span, :] for span in owner_rows(g)], axis=0)
 
 
 def mix_kernel(
@@ -102,11 +106,10 @@
         )
         for y in range(SIDE)
     ]
-    for copy in small[:2] + large[0] + large[1] + large[2] + large[3] + small[2:]:
+    inner = [large[y][stream] for y in range(SIDE) for stream in (1, 2)]
+    outer = [large[y][0] for y in range(SIDE)]
+    for copy in small[:2] + inner + outer + small[2:]:
         copy.start()
-    shifts = shift_table()
-    last = lax.broadcasted_iota(jnp.int32, (16, BLOCK), 0) + (BLOCK - 2)
-    last = (last == lax.broadcasted_iota(jnp.int32, (16, BLOCK), 1)).astype(bf16)
     lane = lax.broadcasted_iota(jnp.int32, (16, BLOCK), 1) // 32
     small[0].wait()
     small[1].wait()
@@ -116,31 +119,34 @@
             + [skip_ref[:, 512 * y : 512 * y + 512], jnp.zeros((6, 4 * BLOCK), f32)],
             axis=0,
         )
-        for copy in large[y]:
-            copy.wait()
         for x in range(SIDE):
-            g = SIDE * y + x
             rows = jnp.zeros((16, BLOCK), f32)
             for zl in range(SIDE):
                 piece = table[:, zl * BLOCK : (zl + 1) * BLOCK]
                 if zl != x:
                     piece = pltpu.roll(piece, (32 * (zl - x)) % BLOCK, 1)
                 rows = jnp.where(lane == zl, piece, rows)
-            rows_ref[g] = rows
-            tiles = [
-                jnp.concatenate([x_ref[stream, span, :] for span in owner_rows(g)], axis=0)
-                for stream in range(3)
-            ]
-            halo_ref[g, 0:2, :] = mm_nt(last, tiles[0])[0:2]
+            rows_ref[SIDE * y + x] = rows
+    for y in range(SIDE):
+        large[y][1].wait()
+        large[y][2].wait()
+        for g in range(SIDE * y, SIDE * y + SIDE):
+            rows = rows_ref[g]
             mixes = []
             for stream in (1, 2):
-                moved = mm_nt(shifts, tiles[stream])
-                halo_ref[g, 2 * stream : 2 * stream + 2, :] = moved[BLOCK - 2 : BLOCK]
-                mixes.append(short_mix(moved, rows, stream))
+                block = owner_tile(x_ref, stream, g).T.astype(f32)
+                halo_ref[g, 2 * stream : 2 * stream + 2, :] = block[BLOCK - 2 :]
+                mixes.append(short_mix(block, rows, stream))
                 head_ref[stream - 1, g] = mixes[-1][:16]
-            halo_ref[g, 6:8, :] = jnp.zeros((2, BLOCK), f32)
             product_ref[g] = (mixes[0] * mixes[1]).astype(bf16)
         out[y].start()
+    last = lax.broadcasted_iota(jnp.int32, (16, BLOCK), 0) + (BLOCK - 2)
+    last = (last == lax.broadcasted_iota(jnp.int32, (16, BLOCK), 1)).astype(bf16)
+    for y in range(SIDE):
+        large[y][0].wait()
+        for g in range(SIDE * y, SIDE * y + SIDE):
+            halo_ref[g, 0:2, :] = mm_nt(last, owner_tile(x_ref, 0, g))[0:2]
+            halo_ref[g, 6:8, :] = jnp.zeros((2, BLOCK), f32)
     small[2].wait()
     small[3].wait()
     rate = rate_ref[...]
@@ -226,11 +232,9 @@
 
 
 def prepare_kernel(q_ref, product_ref, halo_ref, rows_ref, mix_ref, direct_ref):
-    shifts = shift_table()
     for x in range(SIDE):
         rows = rows_ref[x]
-        tile = jnp.concatenate([q_ref[0, span, :] for span in owner_rows(x)], axis=0)
-        mix = short_mix(mm_nt(shifts, tile), rows, 0)
+        mix = short_mix(owner_tile(q_ref, 0, x).T.astype(f32), rows, 0)
         mix_ref[x, :16, :] = mix[:16] + halo_term(halo_ref[x], rows, 0)
         mix_ref[x, 16:, :] = mix[16:]
         direct_ref[x] = rows[9:10] * product_ref[x].astype(f32)

time: 58 us -> 57.5 us (level)
  Pallas kernels: 13.5 us -> 12.6 us
  transfers between devices with their start and end apart: 8 -> 8, of which waited for: 6 -> 6; matrix products, arithmetic and copies ran while one was open for 0% -> 0% of each run, Pallas kernels for 10% -> 9%
where the time goes in v4:
time: 57.5 us; the launch traced here: 57.2 us
  starting transfers between devices  19.3 us (34%)
  blocking collectives  13.1 us (23%)
  Pallas kernels  12.6 us (22%)
  waiting for transfers between devices  12 us (21%)
    all_to_all x1, blocking collectives, body(): lax.all_to_all(result, ('y', 'x'), split_axis=0, concat_axis=0, tiled=True)  13.1 us
    ppermute x6, starting transfers between devices, from_zl(): lax.ppermute(value, 'zl', [(zl, (zl - k) % SIDE) for zl in range(SIDE)])  8.6 us
    all_to_all x1, starting transfers between devices, body(): lax.all_to_all(product, ('y', 'x'), split_axis=0, concat_axis=0, tiled=True)  7.18 us
    ppermute x6, waiting for transfers between devices, from_zl(): lax.ppermute(value, 'zl', [(zl, (zl - k) % SIDE) for zl in range(SIDE)])  6.3 us
    all_to_all x1, waiting for transfers between devices, body(): lax.all_to_all(product, ('y', 'x'), split_axis=0, concat_axis=0, tiled=True)  5.71 us
    ppermute x1, starting transfers between devices, body(): lax.ppermute(halo, ('y', 'zl', 'x'), [(i, i + 1) for i in range(count - 1)])  3.53 us
    pallas_call x1, Pallas kernels, mix_streams(): pl.pallas_call(mix_kernel, in_specs=[pl.BlockSpec(memory_space=pltpu.SMEM...  3.39 us
    pallas_call x1, Pallas kernels, prepare_gate(): pl.pallas_call(prepare_kernel, grid=(4,), in_specs=[pl.BlockSpec((1, 512,...  2.45 us
  transfers between devices with their start and end apart: 8, of which 6 were waited for; matrix products, arithmetic and copies ran while one was open for 0% of the time, Pallas kernels for 9%

profile of v4, /device:TPU:2, one launch (start us, length us, event | category | flops | bytes accessed | tf_op | source)
XLA Modules:
  0.0 57.2 jit_solution(7461533348720666221)
XLA Ops:
  0.0 3.4 %mix.1 = (bf16[16,128,128]{2,1,0:T(8,128)(2,1)}, f32[2,16,16,128]{3,2,1,0:T(8,128)S(1)}, f32[16,8,128]{2,1,0:T(8,128)S(1)}, f32[16,16,128]{2,1,0:T(8,128)S(1)}, f32[32,128]{1,0:T(8,128)S(1)}) custom-call(s32[1]{0:T(128)} %bitcast.mp_ref, bf16[3,2048,128]{2,1,0:T(8,128)(2,1)} %q_ref.1, f32[3,3,8192]{2,1,0:T(4,128)} %taps_hbm.1, f32[1,8192]{1,0:T(1,128)} %bitcast.5, ...), custom_call_target="tpu_custom_call" | custom-call | tf_op jit(solution)/shard_map/mix/pallas_call | solution.py:170
  3.4 0.0 copy-start
  3.4 3.5 %collective-permute-start = (f32[16,8,128]{2,1,0:T(8,128)S(1)}, f32[16,8,128]{2,1,0:T(8,128)S(1)}, u32[]{:S(2)}, u32[]{:S(2)}) collective-permute-start(f32[16,8,128]{2,1,0:T(8,128)S(1)} %get-tuple-element.29), channel_id=1, source_target_pairs={{0,4},{4,8},{8,12},{12,16},{16,20},{20,24},{24,28},{28,32},{32,36}... | collective-permute-start | bytes 196616 | tf_op jit(solution)/shard_map/ppermute | solution.py:466
  7.0 4.7 %collective-permute-start.1 = (f32[32,128]{1,0:T(8,128)S(1)}, f32[32,128]{1,0:T(8,128)S(1)}, u32[]{:S(2)}, u32[]{:S(2)}) collective-permute-start(f32[32,128]{1,0:T(8,128)S(1)} %get-tuple-element.38.p0_ref), channel_id=1, source_target_pairs={{0,48},{16,0},{32,16},{48,32},{1,49},{17,1},{33,17},{49,33},{2,50}... | collective-permute-start | bytes 49160 | tf_op jit(solution)/shard_map/ppermute | solution.py:461
  11.7 0.0 collective-permute-start.2
  11.7 0.7 %collective-permute-start.3 = (f32[32,128]{1,0:T(8,128)S(1)}, f32[32,128]{1,0:T(8,128)S(1)}, u32[]{:S(2)}, u32[]{:S(2)}) collective-permute-start(f32[32,128]{1,0:T(8,128)S(1)} %get-tuple-element.38.p0_ref), channel_id=1, source_target_pairs={{0,16},{16,32},{32,48},{48,0},{1,17},{17,33},{33,49},{49,1},{2,18}... | collective-permute-start | bytes 49160 | tf_op jit(solution)/shard_map/ppermute | solution.py:461
  12.3 0.0 collective-permute-done.halo_ref
  12.3 0.7 %head.1.product_ref = bf16[16,128,128]{2,1,0:T(8,128)(2,1)} custom-call(bf16[16,128,128]{2,1,0:T(8,128)(2,1)} %get-tuple-element.27.product_ref, f32[2,16,16,128]{3,2,1,0:T(8,128)S(1)} %get-tuple-element.28.head_ref, f32[16,8,128]{2,1,0:T(8,128)S(1)} %collective-permute-done.halo_ref, ...), custom_call_target="tpu_custom_call", output_to_operand_aliasing={{}: (0, {})} | custom-call | tf_op jit(solution)/shard_map/head/pallas_call | solution.py:220
  13.0 0.1 collective-permute-done.1.p1_ref
  13.1 3.2 %collective-permute-done.2.p2_ref = f32[32,128]{1,0:T(8,128)S(1)} collective-permute-done((f32[32,128]{1,0:T(8,128)S(1)}, f32[32,128]{1,0:T(8,128)S(1)}, u32[]{:S(2)}, u32[]{:S(2)}) %collective-permute-start.2) | collective-permute-done | bytes 16416 | tf_op jit(solution)/shard_map/ppermute | solution.py:461
  16.3 0.9 %collective-permute-done.3.p3_ref = f32[32,128]{1,0:T(8,128)S(1)} collective-permute-done((f32[32,128]{1,0:T(8,128)S(1)}, f32[32,128]{1,0:T(8,128)S(1)}, u32[]{:S(2)}, u32[]{:S(2)}) %collective-permute-start.3) | collective-permute-done | bytes 16416 | tf_op jit(solution)/shard_map/ppermute | solution.py:461
  17.2 7.2 %all-to-all-start = ((bf16[16,128,128]{2,1,0:T(8,128)(2,1)}), bf16[16,128,128]{2,1,0:T(8,128)(2,1)S(1)}, u32[]{:S(2)}, u32[]{:S(2)}) async-start(bf16[16,128,128]{2,1,0:T(8,128)(2,1)} %head.1.product_ref), calls=%async_computation | async-start | bytes 1048576 | tf_op jit(solution)/shard_map/all_to_all | solution.py:470
  24.4 0.0 copy-done
  24.4 0.0 copy-start.1
  24.4 0.5 tables.1
  24.9 2.5 %prepare.1 = (f32[16,128,128]{2,1,0:T(8,128)S(1)}, f32[16,128,128]{2,1,0:T(8,128)S(1)}) custom-call(bf16[3,2048,128]{2,1,0:T(8,128)(2,1)} %q_ref.1, bf16[16,128,128]{2,1,0:T(8,128)(2,1)} %head.1.product_ref, f32[16,8,128]{2,1,0:T(8,128)S(1)} %collective-permute-done.halo_ref, f32[16,16,128]{2,1,0:T(8,128)S(1)} %get-tuple-element.30.rows_ref), custom_call_target="tpu_custom_call" | custom-call | tf_op jit(solution)/shard_map/prepare/pallas_call | solution.py:245
  27.4 5.7 %all-to-all-done.x_ref = bf16[16,128,128]{2,1,0:T(8,128)(2,1)S(1)} async-done(((bf16[16,128,128]{2,1,0:T(8,128)(2,1)}), bf16[16,128,128]{2,1,0:T(8,128)(2,1)S(1)}, u32[]{:S(2)}, u32[]{:S(2)}) %all-to-all-start) | async-done | bytes 524320 | tf_op jit(solution)/shard_map/all_to_all | solution.py:470
  33.1 1.5 %states.1 = (f32[16,16,128]{2,1,0:T(8,128)S(1)}, f32[4,16,128]{2,1,0:T(8,128)S(1)}) custom-call(bf16[16,128,128]{2,1,0:T(8,128)(2,1)S(1)} %all-to-all-done.x_ref, f32[16,8,128]{2,1,0:T(8,128)S(1)} %get-tuple-element.43.step_ref, f32[16,8,128]{2,1,0:T(8,128)S(1)} %get-tuple-element.44.tail_ref, f32[16,128]{1,0:T(8,128)S(1)} %get-tuple-element.45.decay_ref), custom_call_target="tpu_custom_call" | custom-call | tf_op jit(solution)/shard_map/states/pallas_call | solution.py:360
  34.6 0.7 %collective-permute-start.4 = (f32[4,16,128]{2,1,0:T(8,128)S(1)}, f32[4,16,128]{2,1,0:T(8,128)S(1)}, u32[]{:S(2)}, u32[]{:S(2)}) collective-permute-start(f32[4,16,128]{2,1,0:T(8,128)S(1)} %get-tuple-element.47.r0_ref), channel_id=1, source_target_pairs={{0,48},{16,0},{32,16},{48,32},{1,49},{17,1},{33,17},{49,33},{2,50}... | collective-permute-start | bytes 98312 | tf_op jit(solution)/shard_map/ppermute | solution.py:461
  35.3 0.6 %collective-permute-start.5 = (f32[4,16,128]{2,1,0:T(8,128)S(1)}, f32[4,16,128]{2,1,0:T(8,128)S(1)}, u32[]{:S(2)}, u32[]{:S(2)}) collective-permute-start(f32[4,16,128]{2,1,0:T(8,128)S(1)} %get-tuple-element.47.r0_ref), channel_id=1, source_target_pairs={{0,32},{16,48},{32,0},{48,16},{1,33},{17,49},{33,1},{49,17},{2,34}... | collective-permute-start | bytes 98312 | tf_op jit(solution)/shard_map/ppermute | solution.py:461
  35.9 1.9 %collective-permute-start.6 = (f32[4,16,128]{2,1,0:T(8,128)S(1)}, f32[4,16,128]{2,1,0:T(8,128)S(1)}, u32[]{:S(2)}, u32[]{:S(2)}) collective-permute-start(f32[4,16,128]{2,1,0:T(8,128)S(1)} %get-tuple-element.47.r0_ref), channel_id=1, source_target_pairs={{0,16},{16,32},{32,48},{48,0},{1,17},{17,33},{33,49},{49,1},{2,18}... | collective-permute-start | bytes 98312 | tf_op jit(solution)/shard_map/ppermute | solution.py:461
  37.8 0.0 copy-done.1
  37.8 1.6 %conv.1.inner_ref = f32[16,128,128]{2,1,0:T(8,128)S(1)} custom-call(bf16[16,128,128]{2,1,0:T(8,128)(2,1)S(1)} %all-to-all-done.x_ref, f32[256,256]{1,0:T(8,128)S(1)} %get-tuple-element.42.spec_ref, bf16[256,256]{1,0:T(8,128)(2,1)S(1)} %copy-done, bf16[256,256]{1,0:T(8,128)(2,1)S(1)} %copy-done.1), custom_call_target="tpu_custom_call" | custom-call | tf_op jit(solution)/shard_map/conv/pallas_call | solution.py:386
  39.5 0.0 collective-permute-done.4.r1_ref
  39.5 0.6 %collective-permute-done.5.r2_ref = f32[4,16,128]{2,1,0:T(8,128)S(1)} collective-permute-done((f32[4,16,128]{2,1,0:T(8,128)S(1)}, f32[4,16,128]{2,1,0:T(8,128)S(1)}, u32[]{:S(2)}, u32[]{:S(2)}) %collective-permute-start.5) | collective-permute-done | bytes 32800 | tf_op jit(solution)/shard_map/ppermute | solution.py:461
  40.1 1.5 %collective-permute-done.6.r3_ref = f32[4,16,128]{2,1,0:T(8,128)S(1)} collective-permute-done((f32[4,16,128]{2,1,0:T(8,128)S(1)}, f32[4,16,128]{2,1,0:T(8,128)S(1)}, u32[]{:S(2)}, u32[]{:S(2)}) %collective-permute-start.6) | collective-permute-done | bytes 32800 | tf_op jit(solution)/shard_map/ppermute | solution.py:461
  41.6 1.5 %readout.1 = bf16[16,128,128]{2,1,0:T(8,128)(2,1)S(1)} custom-call(s32[1]{0:T(128)} %bitcast.4.zl_ref, f32[16,128,128]{2,1,0:T(8,128)S(1)} %conv.1.inner_ref, f32[16,16,128]{2,1,0:T(8,128)S(1)} %get-tuple-element.46.state_ref, f32[4,16,128]{2,1,0:T(8,128)S(1)} %get-tuple-element.47.r0_ref, f32[4,16,128]{2,1,0:T(8,128)S(1)} %collective-permute-done.4.r1_ref, ...), custom_call_target="tpu_custom_call" | custom-call | tf_op jit(solution)/shard_map/readout/pallas_call | solution.py:434
  43.1 13.1 %all_to_all.10.long_ref = bf16[16,128,128]{2,1,0:T(8,128)(2,1)S(1)} all-to-all(bf16[16,128,128]{2,1,0:T(8,128)(2,1)S(1)} %readout.1), channel_id=1, replica_groups=mesh['y'=4,'zl'=4,'x'=4,'mp'=4] {'y','x'}, dimensions={0} | all-to-all | bytes 1048576 | tf_op jit(solution)/shard_map/all_to_all | solution.py:479
  56.2 0.9 %gate.1 = bf16[2048,128]{1,0:T(8,128)(2,1)} custom-call(f32[16,128,128]{2,1,0:T(8,128)S(1)} %get-tuple-element.35.mix_ref, f32[16,128,128]{2,1,0:T(8,128)S(1)} %get-tuple-element.36.direct_ref, bf16[16,128,128]{2,1,0:T(8,128)(2,1)S(1)} %all_to_all.10.long_ref), custom_call_target="tpu_custom_call" | custom-call | tf_op jit(solution)/shard_map/gate/pallas_call | solution.py:277
Async XLA Ops:
  3.4 21.0 %copy-start = (bf16[256,256]{1,0:T(8,128)(2,1)S(1)}, bf16[256,256]{1,0:T(8,128)(2,1)}, u32[]{:S(2)}) copy-start(bf16[256,256]{1,0:T(8,128)(2,1)} %constant.12.clone.forward_ref) | copy-start | bytes 393220
  3.4 8.9 %collective-permute-start = (f32[16,8,128]{2,1,0:T(8,128)S(1)}, f32[16,8,128]{2,1,0:T(8,128)S(1)}, u32[]{:S(2)}, u32[]{:S(2)}) collective-permute-start(f32[16,8,128]{2,1,0:T(8,128)S(1)} %get-tuple-element.29), channel_id=1, source_target_pairs={{0,4},{4,8},{8,12},{12,16},{16,20},{20,24},{24,28},{28,32},{32,36}... | collective-permute-start | bytes 196616 | tf_op jit(solution)/shard_map/ppermute | solution.py:466
  7.0 6.1 %collective-permute-start.1 = (f32[32,128]{1,0:T(8,128)S(1)}, f32[32,128]{1,0:T(8,128)S(1)}, u32[]{:S(2)}, u32[]{:S(2)}) collective-permute-start(f32[32,128]{1,0:T(8,128)S(1)} %get-tuple-element.38.p0_ref), channel_id=1, source_target_pairs={{0,48},{16,0},{32,16},{48,32},{1,49},{17,1},{33,17},{49,33},{2,50}... | collective-permute-start | bytes 49160 | tf_op jit(solution)/shard_map/ppermute | solution.py:461
  11.7 4.6 %collective-permute-start.2 = (f32[32,128]{1,0:T(8,128)S(1)}, f32[32,128]{1,0:T(8,128)S(1)}, u32[]{:S(2)}, u32[]{:S(2)}) collective-permute-start(f32[32,128]{1,0:T(8,128)S(1)} %get-tuple-element.38.p0_ref), channel_id=1, source_target_pairs={{0,32},{16,48},{32,0},{48,16},{1,33},{17,49},{33,1},{49,17},{2,34}... | collective-permute-start | bytes 49160 | tf_op jit(solution)/shard_map/ppermute | solution.py:461
  11.7 5.5 %collective-permute-start.3 = (f32[32,128]{1,0:T(8,128)S(1)}, f32[32,128]{1,0:T(8,128)S(1)}, u32[]{:S(2)}, u32[]{:S(2)}) collective-permute-start(f32[32,128]{1,0:T(8,128)S(1)} %get-tuple-element.38.p0_ref), channel_id=1, source_target_pairs={{0,16},{16,32},{32,48},{48,0},{1,17},{17,33},{33,49},{49,1},{2,18}... | collective-permute-start | bytes 49160 | tf_op jit(solution)/shard_map/ppermute | solution.py:461
  17.2 15.9 %all-to-all-start = ((bf16[16,128,128]{2,1,0:T(8,128)(2,1)}), bf16[16,128,128]{2,1,0:T(8,128)(2,1)S(1)}, u32[]{:S(2)}, u32[]{:S(2)}) async-start(bf16[16,128,128]{2,1,0:T(8,128)(2,1)} %head.1.product_ref), calls=%async_computation | async-start | bytes 1048576 | tf_op jit(solution)/shard_map/all_to_all | solution.py:470
  24.4 13.4 %copy-start.1 = (bf16[256,256]{1,0:T(8,128)(2,1)S(1)}, bf16[256,256]{1,0:T(8,128)(2,1)}, u32[]{:S(2)}) copy-start(bf16[256,256]{1,0:T(8,128)(2,1)} %constant.13.clone.backward_ref) | copy-start | bytes 393220
  34.6 4.9 %collective-permute-start.4 = (f32[4,16,128]{2,1,0:T(8,128)S(1)}, f32[4,16,128]{2,1,0:T(8,128)S(1)}, u32[]{:S(2)}, u32[]{:S(2)}) collective-permute-start(f32[4,16,128]{2,1,0:T(8,128)S(1)} %get-tuple-element.47.r0_ref), channel_id=1, source_target_pairs={{0,48},{16,0},{32,16},{48,32},{1,49},{17,1},{33,17},{49,33},{2,50}... | collective-permute-start | bytes 98312 | tf_op jit(solution)/shard_map/ppermute | solution.py:461
  35.3 4.8 %collective-permute-start.5 = (f32[4,16,128]{2,1,0:T(8,128)S(1)}, f32[4,16,128]{2,1,0:T(8,128)S(1)}, u32[]{:S(2)}, u32[]{:S(2)}) collective-permute-start(f32[4,16,128]{2,1,0:T(8,128)S(1)} %get-tuple-element.47.r0_ref), channel_id=1, source_target_pairs={{0,32},{16,48},{32,0},{48,16},{1,33},{17,49},{33,1},{49,17},{2,34}... | collective-permute-start | bytes 98312 | tf_op jit(solution)/shard_map/ppermute | solution.py:461
  35.9 5.7 %collective-permute-start.6 = (f32[4,16,128]{2,1,0:T(8,128)S(1)}, f32[4,16,128]{2,1,0:T(8,128)S(1)}, u32[]{:S(2)}, u32[]{:S(2)}) collective-permute-start(f32[4,16,128]{2,1,0:T(8,128)S(1)} %get-tuple-element.47.r0_ref), channel_id=1, source_target_pairs={{0,16},{16,32},{32,48},{48,0},{1,17},{17,33},{33,49},{49,1},{2,18}... | collective-permute-start | bytes 98312 | tf_op jit(solution)/shard_map/ppermute | solution.py:461

commit v5 on v4

--- a/solution.py
+++ b/solution.py
@@ -466,7 +466,7 @@
     halo = lax.ppermute(halo, ("y", "zl", "x"), [(i, i + 1) for i in range(count - 1)])
     pieces = [params] + [from_zl(params, k) for k in range(1, SIDE)]
     product = finish_product(product, head, halo, rows)
-    product, *pieces = lax.optimization_barrier((product, *pieces))
+    product, pieces[1] = lax.optimization_barrier((product, pieces[1]))
     blocks = lax.all_to_all(product, ("y", "x"), split_axis=0, concat_axis=0, tiled=True)
     gate_mix, direct = prepare_gate(projected, product, halo, rows)
     blocks, gate_mix, direct = lax.optimization_barrier((blocks, gate_mix, direct))

time: 57.5 us -> 56.3 us (0.979)
  waiting for transfers between devices: 12 us -> 5.91 us
  starting transfers between devices: 19.3 us -> 24.1 us
    ppermute x6, starting transfers between devices: 8.6 us -> 13.2 us  [from_zl(): lax.ppermute(value, 'zl', [(zl, (zl - k) % SIDE) for zl in range(SIDE)])]
    all_to_all x1, waiting for transfers between devices: 5.71 us -> 1.76 us  [body(): lax.all_to_all(product, ('y', 'x'), split_axis=0, concat_axis=0, tiled=True)]
    ppermute x6, waiting for transfers between devices: 6.3 us -> 4.15 us  [from_zl(): lax.ppermute(value, 'zl', [(zl, (zl - k) % SIDE) for zl in range(SIDE)])]
  transfers between devices with their start and end apart: 8 -> 8, of which waited for: 6 -> 4; matrix products, arithmetic and copies ran while one was open for 0% -> 0% of each run, Pallas kernels for 9% -> 10%
where the time goes in v5:
time: 56.3 us; the launch traced here: 56 us
  starting transfers between devices  24.1 us (43%)
  blocking collectives  13.3 us (24%)
  Pallas kernels  12.6 us (22%)
  waiting for transfers between devices  5.91 us (10%)
    all_to_all x1, blocking collectives, body(): lax.all_to_all(result, ('y', 'x'), split_axis=0, concat_axis=0, tiled=True)  13.3 us
    ppermute x6, starting transfers between devices, from_zl(): lax.ppermute(value, 'zl', [(zl, (zl - k) % SIDE) for zl in range(SIDE)])  13.2 us
    all_to_all x1, starting transfers between devices, body(): lax.all_to_all(product, ('y', 'x'), split_axis=0, concat_axis=0, tiled=True)  7.45 us
    ppermute x6, waiting for transfers between devices, from_zl(): lax.ppermute(value, 'zl', [(zl, (zl - k) % SIDE) for zl in range(SIDE)])  4.15 us
    ppermute x1, starting transfers between devices, body(): lax.ppermute(halo, ('y', 'zl', 'x'), [(i, i + 1) for i in range(count - 1)])  3.4 us
    pallas_call x1, Pallas kernels, mix_streams(): pl.pallas_call(mix_kernel, in_specs=[pl.BlockSpec(memory_space=pltpu.SMEM...  3.39 us
    pallas_call x1, Pallas kernels, prepare_gate(): pl.pallas_call(prepare_kernel, grid=(4,), in_specs=[pl.BlockSpec((1, 512,...  2.48 us
    all_to_all x1, waiting for transfers between devices, body(): lax.all_to_all(product, ('y', 'x'), split_axis=0, concat_axis=0, tiled=True)  1.76 us
  transfers between devices with their start and end apart: 8, of which 4 were waited for; matrix products, arithmetic and copies ran while one was open for 0% of the time, Pallas kernels for 10%

profile of v5, /device:TPU:2, one launch (start us, length us, event | category | flops | bytes accessed | tf_op | source)
XLA Modules:
  0.0 56.0 jit_solution(16659838953545795734)
XLA Ops:
  0.0 3.4 %mix.1 = (bf16[16,128,128]{2,1,0:T(8,128)(2,1)}, f32[2,16,16,128]{3,2,1,0:T(8,128)S(1)}, f32[16,8,128]{2,1,0:T(8,128)S(1)}, f32[16,16,128]{2,1,0:T(8,128)S(1)}, f32[32,128]{1,0:T(8,128)S(1)}) custom-call(s32[1]{0:T(128)} %bitcast.mp_ref, bf16[3,2048,128]{2,1,0:T(8,128)(2,1)} %q_ref.1, f32[3,3,8192]{2,1,0:T(4,128)} %taps_hbm.1, f32[1,8192]{1,0:T(1,128)} %bitcast.5, ...), custom_call_target="tpu_custom_call" | custom-call | tf_op jit(solution)/shard_map/mix/pallas_call | solution.py:170
  3.4 3.4 %collective-permute-start = (f32[16,8,128]{2,1,0:T(8,128)S(1)}, f32[16,8,128]{2,1,0:T(8,128)S(1)}, u32[]{:S(2)}, u32[]{:S(2)}) collective-permute-start(f32[16,8,128]{2,1,0:T(8,128)S(1)} %get-tuple-element.26), channel_id=1, source_target_pairs={{0,4},{4,8},{8,12},{12,16},{16,20},{20,24},{24,28},{28,32},{32,36}... | collective-permute-start | bytes 196616 | tf_op jit(solution)/shard_map/ppermute | solution.py:466
  6.8 4.7 %collective-permute-start.1 = (f32[32,128]{1,0:T(8,128)S(1)}, f32[32,128]{1,0:T(8,128)S(1)}, u32[]{:S(2)}, u32[]{:S(2)}) collective-permute-start(f32[32,128]{1,0:T(8,128)S(1)} %get-tuple-element.28.p0_ref), channel_id=1, source_target_pairs={{0,48},{16,0},{32,16},{48,32},{1,49},{17,1},{33,17},{49,33},{2,50}... | collective-permute-start | bytes 49160 | tf_op jit(solution)/shard_map/ppermute | solution.py:461
  11.5 0.0 collective-permute-done.halo_ref
  11.5 0.7 %head.1.product_ref = bf16[16,128,128]{2,1,0:T(8,128)(2,1)} custom-call(bf16[16,128,128]{2,1,0:T(8,128)(2,1)} %get-tuple-element.24.product_ref, f32[2,16,16,128]{3,2,1,0:T(8,128)S(1)} %get-tuple-element.25.head_ref, f32[16,8,128]{2,1,0:T(8,128)S(1)} %collective-permute-done.halo_ref, ...), custom_call_target="tpu_custom_call", output_to_operand_aliasing={{}: (0, {})} | custom-call | tf_op jit(solution)/shard_map/head/pallas_call | solution.py:220
  12.2 0.0 copy-start
  12.2 0.7 %collective-permute-done.1.p1_ref = f32[32,128]{1,0:T(8,128)S(1)} collective-permute-done((f32[32,128]{1,0:T(8,128)S(1)}, f32[32,128]{1,0:T(8,128)S(1)}, u32[]{:S(2)}, u32[]{:S(2)}) %collective-permute-start.1) | collective-permute-done | bytes 16416 | tf_op jit(solution)/shard_map/ppermute | solution.py:461
  13.0 7.5 %all-to-all-start = ((bf16[16,128,128]{2,1,0:T(8,128)(2,1)}), bf16[16,128,128]{2,1,0:T(8,128)(2,1)S(1)}, u32[]{:S(2)}, u32[]{:S(2)}) async-start(bf16[16,128,128]{2,1,0:T(8,128)(2,1)} %head.1.product_ref), calls=%async_computation | async-start | bytes 1048576 | tf_op jit(solution)/shard_map/all_to_all | solution.py:470
  20.4 1.0 %collective-permute-start.2 = (f32[32,128]{1,0:T(8,128)S(1)}, f32[32,128]{1,0:T(8,128)S(1)}, u32[]{:S(2)}, u32[]{:S(2)}) collective-permute-start(f32[32,128]{1,0:T(8,128)S(1)} %get-tuple-element.28.p0_ref), channel_id=1, source_target_pairs={{0,32},{16,48},{32,0},{48,16},{1,33},{17,49},{33,1},{49,17},{2,34}... | collective-permute-start | bytes 49160 | tf_op jit(solution)/shard_map/ppermute | solution.py:461
  21.4 3.3 %collective-permute-start.3 = (f32[32,128]{1,0:T(8,128)S(1)}, f32[32,128]{1,0:T(8,128)S(1)}, u32[]{:S(2)}, u32[]{:S(2)}) collective-permute-start(f32[32,128]{1,0:T(8,128)S(1)} %get-tuple-element.28.p0_ref), channel_id=1, source_target_pairs={{0,16},{16,32},{32,48},{48,0},{1,17},{17,33},{33,49},{49,1},{2,18}... | collective-permute-start | bytes 49160 | tf_op jit(solution)/shard_map/ppermute | solution.py:461
  24.8 0.0 copy-start.1
  24.8 2.5 %prepare.1 = (f32[16,128,128]{2,1,0:T(8,128)S(1)}, f32[16,128,128]{2,1,0:T(8,128)S(1)}) custom-call(bf16[3,2048,128]{2,1,0:T(8,128)(2,1)} %q_ref.1, bf16[16,128,128]{2,1,0:T(8,128)(2,1)} %head.1.product_ref, f32[16,8,128]{2,1,0:T(8,128)S(1)} %collective-permute-done.halo_ref, f32[16,16,128]{2,1,0:T(8,128)S(1)} %get-tuple-element.27.rows_ref), custom_call_target="tpu_custom_call" | custom-call | tf_op jit(solution)/shard_map/prepare/pallas_call | solution.py:245
  27.3 0.0 collective-permute-done.2.p2_ref
  27.3 0.0 collective-permute-done.3.p3_ref
  27.3 0.0 copy-done
  27.3 0.5 tables.1
  27.9 1.8 %all-to-all-done.x_ref = bf16[16,128,128]{2,1,0:T(8,128)(2,1)S(1)} async-done(((bf16[16,128,128]{2,1,0:T(8,128)(2,1)}), bf16[16,128,128]{2,1,0:T(8,128)(2,1)S(1)}, u32[]{:S(2)}, u32[]{:S(2)}) %all-to-all-start) | async-done | bytes 524320 | tf_op jit(solution)/shard_map/all_to_all | solution.py:470
  29.6 1.5 %states.1 = (f32[16,16,128]{2,1,0:T(8,128)S(1)}, f32[4,16,128]{2,1,0:T(8,128)S(1)}) custom-call(bf16[16,128,128]{2,1,0:T(8,128)(2,1)S(1)} %all-to-all-done.x_ref, f32[16,8,128]{2,1,0:T(8,128)S(1)} %get-tuple-element.37.step_ref, f32[16,8,128]{2,1,0:T(8,128)S(1)} %get-tuple-element.38.tail_ref, f32[16,128]{1,0:T(8,128)S(1)} %get-tuple-element.39.decay_ref), custom_call_target="tpu_custom_call" | custom-call | tf_op jit(solution)/shard_map/states/pallas_call | solution.py:360
  31.1 3.5 %collective-permute-start.4 = (f32[4,16,128]{2,1,0:T(8,128)S(1)}, f32[4,16,128]{2,1,0:T(8,128)S(1)}, u32[]{:S(2)}, u32[]{:S(2)}) collective-permute-start(f32[4,16,128]{2,1,0:T(8,128)S(1)} %get-tuple-element.41.r0_ref), channel_id=1, source_target_pairs={{0,48},{16,0},{32,16},{48,32},{1,49},{17,1},{33,17},{49,33},{2,50}... | collective-permute-start | bytes 98312 | tf_op jit(solution)/shard_map/ppermute | solution.py:461
  34.6 0.0 collective-permute-start.5
  34.6 0.7 %collective-permute-start.6 = (f32[4,16,128]{2,1,0:T(8,128)S(1)}, f32[4,16,128]{2,1,0:T(8,128)S(1)}, u32[]{:S(2)}, u32[]{:S(2)}) collective-permute-start(f32[4,16,128]{2,1,0:T(8,128)S(1)} %get-tuple-element.41.r0_ref), channel_id=1, source_target_pairs={{0,16},{16,32},{32,48},{48,0},{1,17},{17,33},{33,49},{49,1},{2,18}... | collective-permute-start | bytes 98312 | tf_op jit(solution)/shard_map/ppermute | solution.py:461
  35.2 0.0 copy-done.1
  35.2 1.6 %conv.1.inner_ref = f32[16,128,128]{2,1,0:T(8,128)S(1)} custom-call(bf16[16,128,128]{2,1,0:T(8,128)(2,1)S(1)} %all-to-all-done.x_ref, f32[256,256]{1,0:T(8,128)S(1)} %get-tuple-element.36.spec_ref, bf16[256,256]{1,0:T(8,128)(2,1)S(1)} %copy-done, bf16[256,256]{1,0:T(8,128)(2,1)S(1)} %copy-done.1), custom_call_target="tpu_custom_call" | custom-call | tf_op jit(solution)/shard_map/conv/pallas_call | solution.py:386
  36.9 0.0 collective-permute-done.4.r1_ref
  36.9 2.5 %collective-permute-done.5.r2_ref = f32[4,16,128]{2,1,0:T(8,128)S(1)} collective-permute-done((f32[4,16,128]{2,1,0:T(8,128)S(1)}, f32[4,16,128]{2,1,0:T(8,128)S(1)}, u32[]{:S(2)}, u32[]{:S(2)}) %collective-permute-start.5) | collective-permute-done | bytes 32800 | tf_op jit(solution)/shard_map/ppermute | solution.py:461
  39.4 0.9 %collective-permute-done.6.r3_ref = f32[4,16,128]{2,1,0:T(8,128)S(1)} collective-permute-done((f32[4,16,128]{2,1,0:T(8,128)S(1)}, f32[4,16,128]{2,1,0:T(8,128)S(1)}, u32[]{:S(2)}, u32[]{:S(2)}) %collective-permute-start.6) | collective-permute-done | bytes 32800 | tf_op jit(solution)/shard_map/ppermute | solution.py:461
  40.3 1.5 %readout.1 = bf16[16,128,128]{2,1,0:T(8,128)(2,1)S(1)} custom-call(s32[1]{0:T(128)} %bitcast.4.zl_ref, f32[16,128,128]{2,1,0:T(8,128)S(1)} %conv.1.inner_ref, f32[16,16,128]{2,1,0:T(8,128)S(1)} %get-tuple-element.40.state_ref, f32[4,16,128]{2,1,0:T(8,128)S(1)} %get-tuple-element.41.r0_ref, f32[4,16,128]{2,1,0:T(8,128)S(1)} %collective-permute-done.4.r1_ref, ...), custom_call_target="tpu_custom_call" | custom-call | tf_op jit(solution)/shard_map/readout/pallas_call | solution.py:434
  41.8 13.3 %all_to_all.10.long_ref = bf16[16,128,128]{2,1,0:T(8,128)(2,1)S(1)} all-to-all(bf16[16,128,128]{2,1,0:T(8,128)(2,1)S(1)} %readout.1), channel_id=1, replica_groups=mesh['y'=4,'zl'=4,'x'=4,'mp'=4] {'y','x'}, dimensions={0} | all-to-all | bytes 1048576 | tf_op jit(solution)/shard_map/all_to_all | solution.py:479
  55.1 0.9 %gate.1 = bf16[2048,128]{1,0:T(8,128)(2,1)} custom-call(f32[16,128,128]{2,1,0:T(8,128)S(1)} %get-tuple-element.32.mix_ref, f32[16,128,128]{2,1,0:T(8,128)S(1)} %get-tuple-element.33.direct_ref, bf16[16,128,128]{2,1,0:T(8,128)(2,1)S(1)} %all_to_all.10.long_ref), custom_call_target="tpu_custom_call" | custom-call | tf_op jit(solution)/shard_map/gate/pallas_call | solution.py:277
Async XLA Ops:
  3.4 8.1 %collective-permute-start = (f32[16,8,128]{2,1,0:T(8,128)S(1)}, f32[16,8,128]{2,1,0:T(8,128)S(1)}, u32[]{:S(2)}, u32[]{:S(2)}) collective-permute-start(f32[16,8,128]{2,1,0:T(8,128)S(1)} %get-tuple-element.26), channel_id=1, source_target_pairs={{0,4},{4,8},{8,12},{12,16},{16,20},{20,24},{24,28},{28,32},{32,36}... | collective-permute-start | bytes 196616 | tf_op jit(solution)/shard_map/ppermute | solution.py:466
  6.8 6.1 %collective-permute-start.1 = (f32[32,128]{1,0:T(8,128)S(1)}, f32[32,128]{1,0:T(8,128)S(1)}, u32[]{:S(2)}, u32[]{:S(2)}) collective-permute-start(f32[32,128]{1,0:T(8,128)S(1)} %get-tuple-element.28.p0_ref), channel_id=1, source_target_pairs={{0,48},{16,0},{32,16},{48,32},{1,49},{17,1},{33,17},{49,33},{2,50}... | collective-permute-start | bytes 49160 | tf_op jit(solution)/shard_map/ppermute | solution.py:461
  12.2 15.1 %copy-start = (bf16[256,256]{1,0:T(8,128)(2,1)S(1)}, bf16[256,256]{1,0:T(8,128)(2,1)}, u32[]{:S(2)}) copy-start(bf16[256,256]{1,0:T(8,128)(2,1)} %constant.12.clone.forward_ref) | copy-start | bytes 393220
  13.0 16.7 %all-to-all-start = ((bf16[16,128,128]{2,1,0:T(8,128)(2,1)}), bf16[16,128,128]{2,1,0:T(8,128)(2,1)S(1)}, u32[]{:S(2)}, u32[]{:S(2)}) async-start(bf16[16,128,128]{2,1,0:T(8,128)(2,1)} %head.1.product_ref), calls=%async_computation | async-start | bytes 1048576 | tf_op jit(solution)/shard_map/all_to_all | solution.py:470
  20.4 6.9 %collective-permute-start.2 = (f32[32,128]{1,0:T(8,128)S(1)}, f32[32,128]{1,0:T(8,128)S(1)}, u32[]{:S(2)}, u32[]{:S(2)}) collective-permute-start(f32[32,128]{1,0:T(8,128)S(1)} %get-tuple-element.28.p0_ref), channel_id=1, source_target_pairs={{0,32},{16,48},{32,0},{48,16},{1,33},{17,49},{33,1},{49,17},{2,34}... | collective-permute-start | bytes 49160 | tf_op jit(solution)/shard_map/ppermute | solution.py:461
  21.4 5.8 %collective-permute-start.3 = (f32[32,128]{1,0:T(8,128)S(1)}, f32[32,128]{1,0:T(8,128)S(1)}, u32[]{:S(2)}, u32[]{:S(2)}) collective-permute-start(f32[32,128]{1,0:T(8,128)S(1)} %get-tuple-element.28.p0_ref), channel_id=1, source_target_pairs={{0,16},{16,32},{32,48},{48,0},{1,17},{17,33},{33,49},{49,1},{2,18}... | collective-permute-start | bytes 49160 | tf_op jit(solution)/shard_map/ppermute | solution.py:461
  24.8 10.4 %copy-start.1 = (bf16[256,256]{1,0:T(8,128)(2,1)S(1)}, bf16[256,256]{1,0:T(8,128)(2,1)}, u32[]{:S(2)}) copy-start(bf16[256,256]{1,0:T(8,128)(2,1)} %constant.13.clone.backward_ref) | copy-start | bytes 393220
  31.1 5.8 %collective-permute-start.4 = (f32[4,16,128]{2,1,0:T(8,128)S(1)}, f32[4,16,128]{2,1,0:T(8,128)S(1)}, u32[]{:S(2)}, u32[]{:S(2)}) collective-permute-start(f32[4,16,128]{2,1,0:T(8,128)S(1)} %get-tuple-element.41.r0_ref), channel_id=1, source_target_pairs={{0,48},{16,0},{32,16},{48,32},{1,49},{17,1},{33,17},{49,33},{2,50}... | collective-permute-start | bytes 98312 | tf_op jit(solution)/shard_map/ppermute | solution.py:461
  34.6 4.8 %collective-permute-start.5 = (f32[4,16,128]{2,1,0:T(8,128)S(1)}, f32[4,16,128]{2,1,0:T(8,128)S(1)}, u32[]{:S(2)}, u32[]{:S(2)}) collective-permute-start(f32[4,16,128]{2,1,0:T(8,128)S(1)} %get-tuple-element.41.r0_ref), channel_id=1, source_target_pairs={{0,32},{16,48},{32,0},{48,16},{1,33},{17,49},{33,1},{49,17},{2,34}... | collective-permute-start | bytes 98312 | tf_op jit(solution)/shard_map/ppermute | solution.py:461
  34.6 5.7 %collective-permute-start.6 = (f32[4,16,128]{2,1,0:T(8,128)S(1)}, f32[4,16,128]{2,1,0:T(8,128)S(1)}, u32[]{:S(2)}, u32[]{:S(2)}) collective-permute-start(f32[4,16,128]{2,1,0:T(8,128)S(1)} %get-tuple-element.41.r0_ref), channel_id=1, source_target_pairs={{0,16},{16,32},{32,48},{48,0},{1,17},{17,33},{33,49},{49,1},{2,18}... | collective-permute-start | bytes 98312 | tf_op jit(solution)/shard_map/ppermute | solution.py:461

commit v6 on v5

--- a/solution.py
+++ b/solution.py
@@ -466,7 +466,7 @@
     halo = lax.ppermute(halo, ("y", "zl", "x"), [(i, i + 1) for i in range(count - 1)])
     pieces = [params] + [from_zl(params, k) for k in range(1, SIDE)]
     product = finish_product(product, head, halo, rows)
-    product, pieces[1] = lax.optimization_barrier((product, pieces[1]))
+    product, pieces[3] = lax.optimization_barrier((product, pieces[3]))
     blocks = lax.all_to_all(product, ("y", "x"), split_axis=0, concat_axis=0, tiled=True)
     gate_mix, direct = prepare_gate(projected, product, halo, rows)
     blocks, gate_mix, direct = lax.optimization_barrier((blocks, gate_mix, direct))

time: 56.3 us -> 55.6 us (0.988); the launches traced: 56 us -> 54.6 us
  starting transfers between devices: 24.1 us -> 17.7 us
  waiting for transfers between devices: 5.91 us -> 10.8 us
    ppermute x6, starting transfers between devices: 13.2 us -> 7.1 us  [from_zl(): lax.ppermute(value, 'zl', [(zl, (zl - k) % SIDE) for zl in range(SIDE)])]
    ppermute x6, waiting for transfers between devices: 4.15 us -> 8.12 us  [from_zl(): lax.ppermute(value, 'zl', [(zl, (zl - k) % SIDE) for zl in range(SIDE)])]
    ppermute x1, waiting for transfers between devices: 0.01 us -> 0.76 us  [body(): lax.ppermute(halo, ('y', 'zl', 'x'), [(i, i + 1) for i in range(count - 1)])]
  transfers between devices with their start and end apart: 8 -> 8, of which waited for: 4 -> 6; matrix products, arithmetic and copies ran while one was open for 0% -> 0% of each run, Pallas kernels for 10% -> 10%
where the time goes in v6:
time: 55.6 us; the launch traced here: 54.6 us
  starting transfers between devices  17.7 us (32%)
  blocking collectives  13.4 us (24%)
  Pallas kernels  12.6 us (23%)
  waiting for transfers between devices  10.8 us (19%)
    all_to_all x1, blocking collectives, body(): lax.all_to_all(result, ('y', 'x'), split_axis=0, concat_axis=0, tiled=True)  13.4 us
    ppermute x6, waiting for transfers between devices, from_zl(): lax.ppermute(value, 'zl', [(zl, (zl - k) % SIDE) for zl in range(SIDE)])  8.12 us
    all_to_all x1, starting transfers between devices, body(): lax.all_to_all(product, ('y', 'x'), split_axis=0, concat_axis=0, tiled=True)  7.18 us
    ppermute x6, starting transfers between devices, from_zl(): lax.ppermute(value, 'zl', [(zl, (zl - k) % SIDE) for zl in range(SIDE)])  7.1 us
    ppermute x1, starting transfers between devices, body(): lax.ppermute(halo, ('y', 'zl', 'x'), [(i, i + 1) for i in range(count - 1)])  3.4 us
    pallas_call x1, Pallas kernels, mix_streams(): pl.pallas_call(mix_kernel, in_specs=[pl.BlockSpec(memory_space=pltpu.SMEM...  3.39 us
    pallas_call x1, Pallas kernels, prepare_gate(): pl.pallas_call(prepare_kernel, grid=(4,), in_specs=[pl.BlockSpec((1, 512,...  2.48 us
    all_to_all x1, waiting for transfers between devices, body(): lax.all_to_all(product, ('y', 'x'), split_axis=0, concat_axis=0, tiled=True)  1.95 us
  transfers between devices with their start and end apart: 8, of which 6 were waited for; matrix products, arithmetic and copies ran while one was open for 0% of the time, Pallas kernels for 10%

profile of v6, /device:TPU:2, one launch (start us, length us, event | category | flops | bytes accessed | tf_op | source)
XLA Modules:
  0.0 54.6 jit_solution(4044327198803435546)
XLA Ops:
  0.0 3.4 %mix.1 = (bf16[16,128,128]{2,1,0:T(8,128)(2,1)}, f32[2,16,16,128]{3,2,1,0:T(8,128)S(1)}, f32[16,8,128]{2,1,0:T(8,128)S(1)}, f32[16,16,128]{2,1,0:T(8,128)S(1)}, f32[32,128]{1,0:T(8,128)S(1)}) custom-call(s32[1]{0:T(128)} %bitcast.mp_ref, bf16[3,2048,128]{2,1,0:T(8,128)(2,1)} %q_ref.1, f32[3,3,8192]{2,1,0:T(4,128)} %taps_hbm.1, f32[1,8192]{1,0:T(1,128)} %bitcast.5, ...), custom_call_target="tpu_custom_call" | custom-call | tf_op jit(solution)/shard_map/mix/pallas_call | solution.py:170
  3.4 3.4 %collective-permute-start = (f32[16,8,128]{2,1,0:T(8,128)S(1)}, f32[16,8,128]{2,1,0:T(8,128)S(1)}, u32[]{:S(2)}, u32[]{:S(2)}) collective-permute-start(f32[16,8,128]{2,1,0:T(8,128)S(1)} %get-tuple-element.26), channel_id=1, source_target_pairs={{0,4},{4,8},{8,12},{12,16},{16,20},{20,24},{24,28},{28,32},{32,36}... | collective-permute-start | bytes 196616 | tf_op jit(solution)/shard_map/ppermute | solution.py:466
  6.8 2.0 %collective-permute-start.1 = (f32[32,128]{1,0:T(8,128)S(1)}, f32[32,128]{1,0:T(8,128)S(1)}, u32[]{:S(2)}, u32[]{:S(2)}) collective-permute-start(f32[32,128]{1,0:T(8,128)S(1)} %get-tuple-element.28.p0_ref), channel_id=1, source_target_pairs={{0,16},{16,32},{32,48},{48,0},{1,17},{17,33},{33,49},{49,1},{2,18}... | collective-permute-start | bytes 49160 | tf_op jit(solution)/shard_map/ppermute | solution.py:461
  8.8 0.8 %collective-permute-done.halo_ref = f32[16,8,128]{2,1,0:T(8,128)S(1)} collective-permute-done((f32[16,8,128]{2,1,0:T(8,128)S(1)}, f32[16,8,128]{2,1,0:T(8,128)S(1)}, u32[]{:S(2)}, u32[]{:S(2)}) %collective-permute-start) | collective-permute-done | bytes 65568 | tf_op jit(solution)/shard_map/ppermute | solution.py:466
  9.6 0.7 %head.1.product_ref = bf16[16,128,128]{2,1,0:T(8,128)(2,1)} custom-call(bf16[16,128,128]{2,1,0:T(8,128)(2,1)} %get-tuple-element.24.product_ref, f32[2,16,16,128]{3,2,1,0:T(8,128)S(1)} %get-tuple-element.25.head_ref, f32[16,8,128]{2,1,0:T(8,128)S(1)} %collective-permute-done.halo_ref, ...), custom_call_target="tpu_custom_call", output_to_operand_aliasing={{}: (0, {})} | custom-call | tf_op jit(solution)/shard_map/head/pallas_call | solution.py:220
  10.3 0.0 copy-start
  10.3 3.0 %collective-permute-done.1.p3_ref = f32[32,128]{1,0:T(8,128)S(1)} collective-permute-done((f32[32,128]{1,0:T(8,128)S(1)}, f32[32,128]{1,0:T(8,128)S(1)}, u32[]{:S(2)}, u32[]{:S(2)}) %collective-permute-start.1) | collective-permute-done | bytes 16416 | tf_op jit(solution)/shard_map/ppermute | solution.py:461
  13.2 7.2 %all-to-all-start = ((bf16[16,128,128]{2,1,0:T(8,128)(2,1)}), bf16[16,128,128]{2,1,0:T(8,128)(2,1)S(1)}, u32[]{:S(2)}, u32[]{:S(2)}) async-start(bf16[16,128,128]{2,1,0:T(8,128)(2,1)} %head.1.product_ref), calls=%async_computation | async-start | bytes 1048576 | tf_op jit(solution)/shard_map/all_to_all | solution.py:470
  20.4 2.0 %collective-permute-start.2 = (f32[32,128]{1,0:T(8,128)S(1)}, f32[32,128]{1,0:T(8,128)S(1)}, u32[]{:S(2)}, u32[]{:S(2)}) collective-permute-start(f32[32,128]{1,0:T(8,128)S(1)} %get-tuple-element.28.p0_ref), channel_id=1, source_target_pairs={{0,48},{16,0},{32,16},{48,32},{1,49},{17,1},{33,17},{49,33},{2,50}... | collective-permute-start | bytes 49160 | tf_op jit(solution)/shard_map/ppermute | solution.py:461
  22.4 0.0 collective-permute-start.3
  22.4 0.0 copy-start.1
  22.4 2.5 %prepare.1 = (f32[16,128,128]{2,1,0:T(8,128)S(1)}, f32[16,128,128]{2,1,0:T(8,128)S(1)}) custom-call(bf16[3,2048,128]{2,1,0:T(8,128)(2,1)} %q_ref.1, bf16[16,128,128]{2,1,0:T(8,128)(2,1)} %head.1.product_ref, f32[16,8,128]{2,1,0:T(8,128)S(1)} %collective-permute-done.halo_ref, f32[16,16,128]{2,1,0:T(8,128)S(1)} %get-tuple-element.27.rows_ref), custom_call_target="tpu_custom_call" | custom-call | tf_op jit(solution)/shard_map/prepare/pallas_call | solution.py:245
  24.9 0.0 collective-permute-done.2.p1_ref
  24.9 2.1 %collective-permute-done.3.p2_ref = f32[32,128]{1,0:T(8,128)S(1)} collective-permute-done((f32[32,128]{1,0:T(8,128)S(1)}, f32[32,128]{1,0:T(8,128)S(1)}, u32[]{:S(2)}, u32[]{:S(2)}) %collective-permute-start.3) | collective-permute-done | bytes 16416 | tf_op jit(solution)/shard_map/ppermute | solution.py:461
  27.1 0.0 copy-done
  27.1 0.5 tables.1
  27.6 2.0 %all-to-all-done.x_ref = bf16[16,128,128]{2,1,0:T(8,128)(2,1)S(1)} async-done(((bf16[16,128,128]{2,1,0:T(8,128)(2,1)}), bf16[16,128,128]{2,1,0:T(8,128)(2,1)S(1)}, u32[]{:S(2)}, u32[]{:S(2)}) %all-to-all-start) | async-done | bytes 524320 | tf_op jit(solution)/shard_map/all_to_all | solution.py:470
  29.6 1.5 %states.1 = (f32[16,16,128]{2,1,0:T(8,128)S(1)}, f32[4,16,128]{2,1,0:T(8,128)S(1)}) custom-call(bf16[16,128,128]{2,1,0:T(8,128)(2,1)S(1)} %all-to-all-done.x_ref, f32[16,8,128]{2,1,0:T(8,128)S(1)} %get-tuple-element.37.step_ref, f32[16,8,128]{2,1,0:T(8,128)S(1)} %get-tuple-element.38.tail_ref, f32[16,128]{1,0:T(8,128)S(1)} %get-tuple-element.39.decay_ref), custom_call_target="tpu_custom_call" | custom-call | tf_op jit(solution)/shard_map/states/pallas_call | solution.py:360
  31.0 2.0 %collective-permute-start.4 = (f32[4,16,128]{2,1,0:T(8,128)S(1)}, f32[4,16,128]{2,1,0:T(8,128)S(1)}, u32[]{:S(2)}, u32[]{:S(2)}) collective-permute-start(f32[4,16,128]{2,1,0:T(8,128)S(1)} %get-tuple-element.41.r0_ref), channel_id=1, source_target_pairs={{0,48},{16,0},{32,16},{48,32},{1,49},{17,1},{33,17},{49,33},{2,50}... | collective-permute-start | bytes 98312 | tf_op jit(solution)/shard_map/ppermute | solution.py:461
  33.1 0.0 collective-permute-start.5
  33.1 1.0 %collective-permute-start.6 = (f32[4,16,128]{2,1,0:T(8,128)S(1)}, f32[4,16,128]{2,1,0:T(8,128)S(1)}, u32[]{:S(2)}, u32[]{:S(2)}) collective-permute-start(f32[4,16,128]{2,1,0:T(8,128)S(1)} %get-tuple-element.41.r0_ref), channel_id=1, source_target_pairs={{0,16},{16,32},{32,48},{48,0},{1,17},{17,33},{33,49},{49,1},{2,18}... | collective-permute-start | bytes 98312 | tf_op jit(solution)/shard_map/ppermute | solution.py:461
  34.1 0.0 copy-done.1
  34.1 1.6 %conv.1.inner_ref = f32[16,128,128]{2,1,0:T(8,128)S(1)} custom-call(bf16[16,128,128]{2,1,0:T(8,128)(2,1)S(1)} %all-to-all-done.x_ref, f32[256,256]{1,0:T(8,128)S(1)} %get-tuple-element.36.spec_ref, bf16[256,256]{1,0:T(8,128)(2,1)S(1)} %copy-done, bf16[256,256]{1,0:T(8,128)(2,1)S(1)} %copy-done.1), custom_call_target="tpu_custom_call" | custom-call | tf_op jit(solution)/shard_map/conv/pallas_call | solution.py:386
  35.8 0.0 collective-permute-done.4.r1_ref
  35.8 2.1 %collective-permute-done.5.r2_ref = f32[4,16,128]{2,1,0:T(8,128)S(1)} collective-permute-done((f32[4,16,128]{2,1,0:T(8,128)S(1)}, f32[4,16,128]{2,1,0:T(8,128)S(1)}, u32[]{:S(2)}, u32[]{:S(2)}) %collective-permute-start.5) | collective-permute-done | bytes 32800 | tf_op jit(solution)/shard_map/ppermute | solution.py:461
  37.9 0.9 %collective-permute-done.6.r3_ref = f32[4,16,128]{2,1,0:T(8,128)S(1)} collective-permute-done((f32[4,16,128]{2,1,0:T(8,128)S(1)}, f32[4,16,128]{2,1,0:T(8,128)S(1)}, u32[]{:S(2)}, u32[]{:S(2)}) %collective-permute-start.6) | collective-permute-done | bytes 32800 | tf_op jit(solution)/shard_map/ppermute | solution.py:461
  38.8 1.5 %readout.1 = bf16[16,128,128]{2,1,0:T(8,128)(2,1)S(1)} custom-call(s32[1]{0:T(128)} %bitcast.4.zl_ref, f32[16,128,128]{2,1,0:T(8,128)S(1)} %conv.1.inner_ref, f32[16,16,128]{2,1,0:T(8,128)S(1)} %get-tuple-element.40.state_ref, f32[4,16,128]{2,1,0:T(8,128)S(1)} %get-tuple-element.41.r0_ref, f32[4,16,128]{2,1,0:T(8,128)S(1)} %collective-permute-done.4.r1_ref, ...), custom_call_target="tpu_custom_call" | custom-call | tf_op jit(solution)/shard_map/readout/pallas_call | solution.py:434
  40.3 13.4 %all_to_all.10.long_ref = bf16[16,128,128]{2,1,0:T(8,128)(2,1)S(1)} all-to-all(bf16[16,128,128]{2,1,0:T(8,128)(2,1)S(1)} %readout.1), channel_id=1, replica_groups=mesh['y'=4,'zl'=4,'x'=4,'mp'=4] {'y','x'}, dimensions={0} | all-to-all | bytes 1048576 | tf_op jit(solution)/shard_map/all_to_all | solution.py:479
  53.7 0.9 %gate.1 = bf16[2048,128]{1,0:T(8,128)(2,1)} custom-call(f32[16,128,128]{2,1,0:T(8,128)S(1)} %get-tuple-element.32.mix_ref, f32[16,128,128]{2,1,0:T(8,128)S(1)} %get-tuple-element.33.direct_ref, bf16[16,128,128]{2,1,0:T(8,128)(2,1)S(1)} %all_to_all.10.long_ref), custom_call_target="tpu_custom_call" | custom-call | tf_op jit(solution)/shard_map/gate/pallas_call | solution.py:277
Async XLA Ops:
  3.4 6.2 %collective-permute-start = (f32[16,8,128]{2,1,0:T(8,128)S(1)}, f32[16,8,128]{2,1,0:T(8,128)S(1)}, u32[]{:S(2)}, u32[]{:S(2)}) collective-permute-start(f32[16,8,128]{2,1,0:T(8,128)S(1)} %get-tuple-element.26), channel_id=1, source_target_pairs={{0,4},{4,8},{8,12},{12,16},{16,20},{20,24},{24,28},{28,32},{32,36}... | collective-permute-start | bytes 196616 | tf_op jit(solution)/shard_map/ppermute | solution.py:466
  6.8 6.4 %collective-permute-start.1 = (f32[32,128]{1,0:T(8,128)S(1)}, f32[32,128]{1,0:T(8,128)S(1)}, u32[]{:S(2)}, u32[]{:S(2)}) collective-permute-start(f32[32,128]{1,0:T(8,128)S(1)} %get-tuple-element.28.p0_ref), channel_id=1, source_target_pairs={{0,16},{16,32},{32,48},{48,0},{1,17},{17,33},{33,49},{49,1},{2,18}... | collective-permute-start | bytes 49160 | tf_op jit(solution)/shard_map/ppermute | solution.py:461
  10.3 16.8 %copy-start = (bf16[256,256]{1,0:T(8,128)(2,1)S(1)}, bf16[256,256]{1,0:T(8,128)(2,1)}, u32[]{:S(2)}) copy-start(bf16[256,256]{1,0:T(8,128)(2,1)} %constant.12.clone.forward_ref) | copy-start | bytes 393220
  13.2 16.3 %all-to-all-start = ((bf16[16,128,128]{2,1,0:T(8,128)(2,1)}), bf16[16,128,128]{2,1,0:T(8,128)(2,1)S(1)}, u32[]{:S(2)}, u32[]{:S(2)}) async-start(bf16[16,128,128]{2,1,0:T(8,128)(2,1)} %head.1.product_ref), calls=%async_computation | async-start | bytes 1048576 | tf_op jit(solution)/shard_map/all_to_all | solution.py:470
  20.4 4.5 %collective-permute-start.2 = (f32[32,128]{1,0:T(8,128)S(1)}, f32[32,128]{1,0:T(8,128)S(1)}, u32[]{:S(2)}, u32[]{:S(2)}) collective-permute-start(f32[32,128]{1,0:T(8,128)S(1)} %get-tuple-element.28.p0_ref), channel_id=1, source_target_pairs={{0,48},{16,0},{32,16},{48,32},{1,49},{17,1},{33,17},{49,33},{2,50}... | collective-permute-start | bytes 49160 | tf_op jit(solution)/shard_map/ppermute | solution.py:461
  22.4 4.6 %collective-permute-start.3 = (f32[32,128]{1,0:T(8,128)S(1)}, f32[32,128]{1,0:T(8,128)S(1)}, u32[]{:S(2)}, u32[]{:S(2)}) collective-permute-start(f32[32,128]{1,0:T(8,128)S(1)} %get-tuple-element.28.p0_ref), channel_id=1, source_target_pairs={{0,32},{16,48},{32,0},{48,16},{1,33},{17,49},{33,1},{49,17},{2,34}... | collective-permute-start | bytes 49160 | tf_op jit(solution)/shard_map/ppermute | solution.py:461
  22.4 11.7 %copy-start.1 = (bf16[256,256]{1,0:T(8,128)(2,1)S(1)}, bf16[256,256]{1,0:T(8,128)(2,1)}, u32[]{:S(2)}) copy-start(bf16[256,256]{1,0:T(8,128)(2,1)} %constant.13.clone.backward_ref) | copy-start | bytes 393220
  31.0 4.7 %collective-permute-start.4 = (f32[4,16,128]{2,1,0:T(8,128)S(1)}, f32[4,16,128]{2,1,0:T(8,128)S(1)}, u32[]{:S(2)}, u32[]{:S(2)}) collective-permute-start(f32[4,16,128]{2,1,0:T(8,128)S(1)} %get-tuple-element.41.r0_ref), channel_id=1, source_target_pairs={{0,48},{16,0},{32,16},{48,32},{1,49},{17,1},{33,17},{49,33},{2,50}... | collective-permute-start | bytes 98312 | tf_op jit(solution)/shard_map/ppermute | solution.py:461
  33.1 4.8 %collective-permute-start.5 = (f32[4,16,128]{2,1,0:T(8,128)S(1)}, f32[4,16,128]{2,1,0:T(8,128)S(1)}, u32[]{:S(2)}, u32[]{:S(2)}) collective-permute-start(f32[4,16,128]{2,1,0:T(8,128)S(1)} %get-tuple-element.41.r0_ref), channel_id=1, source_target_pairs={{0,32},{16,48},{32,0},{48,16},{1,33},{17,49},{33,1},{49,17},{2,34}... | collective-permute-start | bytes 98312 | tf_op jit(solution)/shard_map/ppermute | solution.py:461
  33.1 5.7 %collective-permute-start.6 = (f32[4,16,128]{2,1,0:T(8,128)S(1)}, f32[4,16,128]{2,1,0:T(8,128)S(1)}, u32[]{:S(2)}, u32[]{:S(2)}) collective-permute-start(f32[4,16,128]{2,1,0:T(8,128)S(1)} %get-tuple-element.41.r0_ref), channel_id=1, source_target_pairs={{0,16},{16,32},{32,48},{48,0},{1,17},{17,33},{33,49},{49,1},{2,18}... | collective-permute-start | bytes 98312 | tf_op jit(solution)/shard_map/ppermute | solution.py:461

commit v7 on v6

--- a/solution.py
+++ b/solution.py
@@ -135,7 +135,7 @@
             mixes = []
             for stream in (1, 2):
                 block = owner_tile(x_ref, stream, g).T.astype(f32)
-                halo_ref[g, 2 * stream : 2 * stream + 2, :] = block[BLOCK - 2 :]
+                halo_ref[g, 2 * stream : 2 * stream + 2, :] = block[BLOCK - 2 :].astype(bf16)
                 mixes.append(short_mix(block, rows, stream))
                 head_ref[stream - 1, g] = mixes[-1][:16]
             product_ref[g] = (mixes[0] * mixes[1]).astype(bf16)
@@ -145,8 +145,8 @@
     for y in range(SIDE):
         large[y][0].wait()
         for g in range(SIDE * y, SIDE * y + SIDE):
-            halo_ref[g, 0:2, :] = mm_nt(last, owner_tile(x_ref, 0, g))[0:2]
-            halo_ref[g, 6:8, :] = jnp.zeros((2, BLOCK), f32)
+            halo_ref[g, 0:2, :] = mm_nt(last, owner_tile(x_ref, 0, g))[0:2].astype(bf16)
+            halo_ref[g, 6:8, :] = jnp.zeros((2, BLOCK), bf16)
     small[2].wait()
     small[3].wait()
     rate = rate_ref[...]
@@ -174,7 +174,7 @@
         out_shape=[
             jax.ShapeDtypeStruct((OWNERS, BLOCK, BLOCK), bf16),
             jax.ShapeDtypeStruct((2, OWNERS, 16, BLOCK), f32),
-            jax.ShapeDtypeStruct((OWNERS, 8, BLOCK), f32),
+            jax.ShapeDtypeStruct((OWNERS, 8, BLOCK), bf16),
             jax.ShapeDtypeStruct((OWNERS, 16, BLOCK), f32),
             jax.ShapeDtypeStruct((2 * MODES, BLOCK), f32),
         ],
@@ -209,7 +209,7 @@
 def head_kernel(product_ref, head_ref, halo_ref, rows_ref, out_ref):
     del product_ref
     for g in range(OWNERS):
-        halo = halo_ref[g]
+        halo = halo_ref[g].astype(f32)
         rows = rows_ref[g]
         k_mix = head_ref[0, g] + halo_term(halo, rows, 1)
         v_mix = head_ref[1, g] + halo_term(halo, rows, 2)
@@ -235,7 +235,7 @@
     for x in range(SIDE):
         rows = rows_ref[x]
         mix = short_mix(owner_tile(q_ref, 0, x).T.astype(f32), rows, 0)
-        mix_ref[x, :16, :] = mix[:16] + halo_term(halo_ref[x], rows, 0)
+        mix_ref[x, :16, :] = mix[:16] + halo_term(halo_ref[x].astype(f32), rows, 0)
         mix_ref[x, 16:, :] = mix[16:]
         direct_ref[x] = rows[9:10] * product_ref[x].astype(f32)
 
@@ -473,7 +473,8 @@
     forward, backward = transform_tables()
     spec, step, tail, start, decay = make_tables(pieces, forward, zl_index)
     states, run = block_states(blocks, step, tail, decay)
-    runs = [run] + [from_zl(run, k) for k in range(1, SIDE)]
+    arriving = {k: from_zl(run, k) for k in range(SIDE - 1, 0, -1)}
+    runs = [run] + [arriving[k] for k in range(1, SIDE)]
     inner = convolve_blocks(blocks, spec, forward, backward)
     result = add_states(inner, states, runs, step, start, decay, zl_index)
     long_part = lax.all_to_all(result, ("y", "x"), split_axis=0, concat_axis=0, tiled=True)

time: 55.6 us -> 55.4 us (level)
    ppermute x6, waiting for transfers between devices: 8.12 us -> 8.81 us  [from_zl(): lax.ppermute(value, 'zl', [(zl, (zl - k) % SIDE) for zl in range(SIDE)])]
where the time goes in v7:
time: 55.4 us; the launch traced here: 54.7 us
  starting transfers between devices  17.5 us (32%)
  blocking collectives  13.5 us (24%)
  Pallas kernels  12.6 us (23%)
  waiting for transfers between devices  11 us (20%)
    all_to_all x1, blocking collectives, body(): lax.all_to_all(result, ('y', 'x'), split_axis=0, concat_axis=0, tiled=True)  13.5 us
    ppermute x6, waiting for transfers between devices, from_zl(): lax.ppermute(value, 'zl', [(zl, (zl - k) % SIDE) for zl in range(SIDE)])  8.81 us
    all_to_all x1, starting transfers between devices, body(): lax.all_to_all(product, ('y', 'x'), split_axis=0, concat_axis=0, tiled=True)  7.18 us
    ppermute x6, starting transfers between devices, from_zl(): lax.ppermute(value, 'zl', [(zl, (zl - k) % SIDE) for zl in range(SIDE)])  6.95 us
    pallas_call x1, Pallas kernels, mix_streams(): pl.pallas_call(mix_kernel, in_specs=[pl.BlockSpec(memory_space=pltpu.SMEM...  3.4 us
    ppermute x1, starting transfers between devices, body(): lax.ppermute(halo, ('y', 'zl', 'x'), [(i, i + 1) for i in range(count - 1)])  3.4 us
    pallas_call x1, Pallas kernels, prepare_gate(): pl.pallas_call(prepare_kernel, grid=(4,), in_specs=[pl.BlockSpec((1, 512,...  2.44 us
    all_to_all x1, waiting for transfers between devices, body(): lax.all_to_all(product, ('y', 'x'), split_axis=0, concat_axis=0, tiled=True)  1.78 us
  transfers between devices with their start and end apart: 8, of which 6 were waited for; matrix products, arithmetic and copies ran while one was open for 0% of the time, Pallas kernels for 10%

profile of v7, /device:TPU:2, one launch (start us, length us, event | category | flops | bytes accessed | tf_op | source)
XLA Modules:
  0.0 54.7 jit_solution(2861014593077462986)
XLA Ops:
  0.0 3.4 %mix.1 = (bf16[16,128,128]{2,1,0:T(8,128)(2,1)}, f32[2,16,16,128]{3,2,1,0:T(8,128)S(1)}, bf16[16,8,128]{2,1,0:T(8,128)(2,1)S(1)}, f32[16,16,128]{2,1,0:T(8,128)S(1)}, f32[32,128]{1,0:T(8,128)S(1)}) custom-call(s32[1]{0:T(128)} %bitcast.mp_ref, bf16[3,2048,128]{2,1,0:T(8,128)(2,1)} %q_ref.1, f32[3,3,8192]{2,1,0:T(4,128)} %taps_hbm.1, f32[1,8192]{1,0:T(1,128)} %bitcast.5, ...), custom_call_target="tpu_custom_call" | custom-call | tf_op jit(solution)/shard_map/mix/pallas_call | solution.py:170
  3.4 3.4 %collective-permute-start = (bf16[16,8,128]{2,1,0:T(8,128)(2,1)S(1)}, bf16[16,8,128]{2,1,0:T(8,128)(2,1)S(1)}, u32[]{:S(2)}, u32[]{:S(2)}) collective-permute-start(bf16[16,8,128]{2,1,0:T(8,128)(2,1)S(1)} %get-tuple-element.26), channel_id=1, source_target_pairs={{0,4},{4,8},{8,12},{12,16},{16,20},{20,24},{24,28},{28,32},{32,36}... | collective-permute-start | bytes 98312 | tf_op jit(solution)/shard_map/ppermute | solution.py:466
  6.8 2.0 %collective-permute-start.1 = (f32[32,128]{1,0:T(8,128)S(1)}, f32[32,128]{1,0:T(8,128)S(1)}, u32[]{:S(2)}, u32[]{:S(2)}) collective-permute-start(f32[32,128]{1,0:T(8,128)S(1)} %get-tuple-element.28.p0_ref), channel_id=1, source_target_pairs={{0,16},{16,32},{32,48},{48,0},{1,17},{17,33},{33,49},{49,1},{2,18}... | collective-permute-start | bytes 49160 | tf_op jit(solution)/shard_map/ppermute | solution.py:461
  8.8 0.4 collective-permute-done.halo_ref
  9.2 0.7 %head.1.product_ref = bf16[16,128,128]{2,1,0:T(8,128)(2,1)} custom-call(bf16[16,128,128]{2,1,0:T(8,128)(2,1)} %get-tuple-element.24.product_ref, f32[2,16,16,128]{3,2,1,0:T(8,128)S(1)} %get-tuple-element.25.head_ref, bf16[16,8,128]{2,1,0:T(8,128)(2,1)S(1)} %collective-permute-done.halo_ref, ...), custom_call_target="tpu_custom_call", output_to_operand_aliasing={{}: (0, {})} | custom-call | tf_op jit(solution)/shard_map/head/pallas_call | solution.py:220
  9.9 0.0 copy-start
  9.9 3.3 %collective-permute-done.1.p3_ref = f32[32,128]{1,0:T(8,128)S(1)} collective-permute-done((f32[32,128]{1,0:T(8,128)S(1)}, f32[32,128]{1,0:T(8,128)S(1)}, u32[]{:S(2)}, u32[]{:S(2)}) %collective-permute-start.1) | collective-permute-done | bytes 16416 | tf_op jit(solution)/shard_map/ppermute | solution.py:461
  13.2 7.2 %all-to-all-start = ((bf16[16,128,128]{2,1,0:T(8,128)(2,1)}), bf16[16,128,128]{2,1,0:T(8,128)(2,1)S(1)}, u32[]{:S(2)}, u32[]{:S(2)}) async-start(bf16[16,128,128]{2,1,0:T(8,128)(2,1)} %head.1.product_ref), calls=%async_computation | async-start | bytes 1048576 | tf_op jit(solution)/shard_map/all_to_all | solution.py:470
  20.4 0.0 copy-start.1
  20.4 2.1 %collective-permute-start.2 = (f32[32,128]{1,0:T(8,128)S(1)}, f32[32,128]{1,0:T(8,128)S(1)}, u32[]{:S(2)}, u32[]{:S(2)}) collective-permute-start(f32[32,128]{1,0:T(8,128)S(1)} %get-tuple-element.28.p0_ref), channel_id=1, source_target_pairs={{0,48},{16,0},{32,16},{48,32},{1,49},{17,1},{33,17},{49,33},{2,50}... | collective-permute-start | bytes 49160 | tf_op jit(solution)/shard_map/ppermute | solution.py:461
  22.5 0.0 collective-permute-start.3
  22.5 2.4 %prepare.1 = (f32[16,128,128]{2,1,0:T(8,128)S(1)}, f32[16,128,128]{2,1,0:T(8,128)S(1)}) custom-call(bf16[3,2048,128]{2,1,0:T(8,128)(2,1)} %q_ref.1, bf16[16,128,128]{2,1,0:T(8,128)(2,1)} %head.1.product_ref, bf16[16,8,128]{2,1,0:T(8,128)(2,1)S(1)} %collective-permute-done.halo_ref, f32[16,16,128]{2,1,0:T(8,128)S(1)} %get-tuple-element.27.rows_ref), custom_call_target="tpu_custom_call" | custom-call | tf_op jit(solution)/shard_map/prepare/pallas_call | solution.py:245
  25.0 0.0 collective-permute-done.2.p1_ref
  25.0 2.2 %collective-permute-done.3.p2_ref = f32[32,128]{1,0:T(8,128)S(1)} collective-permute-done((f32[32,128]{1,0:T(8,128)S(1)}, f32[32,128]{1,0:T(8,128)S(1)}, u32[]{:S(2)}, u32[]{:S(2)}) %collective-permute-start.3) | collective-permute-done | bytes 16416 | tf_op jit(solution)/shard_map/ppermute | solution.py:461
  27.2 0.0 copy-done
  27.2 0.5 tables.1
  27.7 1.8 %all-to-all-done.x_ref = bf16[16,128,128]{2,1,0:T(8,128)(2,1)S(1)} async-done(((bf16[16,128,128]{2,1,0:T(8,128)(2,1)}), bf16[16,128,128]{2,1,0:T(8,128)(2,1)S(1)}, u32[]{:S(2)}, u32[]{:S(2)}) %all-to-all-start) | async-done | bytes 524320 | tf_op jit(solution)/shard_map/all_to_all | solution.py:470
  29.5 1.5 %states.1 = (f32[16,16,128]{2,1,0:T(8,128)S(1)}, f32[4,16,128]{2,1,0:T(8,128)S(1)}) custom-call(bf16[16,128,128]{2,1,0:T(8,128)(2,1)S(1)} %all-to-all-done.x_ref, f32[16,8,128]{2,1,0:T(8,128)S(1)} %get-tuple-element.37.step_ref, f32[16,8,128]{2,1,0:T(8,128)S(1)} %get-tuple-element.38.tail_ref, f32[16,128]{1,0:T(8,128)S(1)} %get-tuple-element.39.decay_ref), custom_call_target="tpu_custom_call" | custom-call | tf_op jit(solution)/shard_map/states/pallas_call | solution.py:360
  31.0 2.1 %collective-permute-start.4 = (f32[4,16,128]{2,1,0:T(8,128)S(1)}, f32[4,16,128]{2,1,0:T(8,128)S(1)}, u32[]{:S(2)}, u32[]{:S(2)}) collective-permute-start(f32[4,16,128]{2,1,0:T(8,128)S(1)} %get-tuple-element.41.r0_ref), channel_id=1, source_target_pairs={{0,48},{16,0},{32,16},{48,32},{1,49},{17,1},{33,17},{49,33},{2,50}... | collective-permute-start | bytes 98312 | tf_op jit(solution)/shard_map/ppermute | solution.py:461
  33.1 0.0 collective-permute-start.5
  33.1 0.7 %collective-permute-start.6 = (f32[4,16,128]{2,1,0:T(8,128)S(1)}, f32[4,16,128]{2,1,0:T(8,128)S(1)}, u32[]{:S(2)}, u32[]{:S(2)}) collective-permute-start(f32[4,16,128]{2,1,0:T(8,128)S(1)} %get-tuple-element.41.r0_ref), channel_id=1, source_target_pairs={{0,16},{16,32},{32,48},{48,0},{1,17},{17,33},{33,49},{49,1},{2,18}... | collective-permute-start | bytes 98312 | tf_op jit(solution)/shard_map/ppermute | solution.py:461
  33.8 0.0 copy-done.1
  33.8 1.6 %conv.1.inner_ref = f32[16,128,128]{2,1,0:T(8,128)S(1)} custom-call(bf16[16,128,128]{2,1,0:T(8,128)(2,1)S(1)} %all-to-all-done.x_ref, f32[256,256]{1,0:T(8,128)S(1)} %get-tuple-element.36.spec_ref, bf16[256,256]{1,0:T(8,128)(2,1)S(1)} %copy-done, bf16[256,256]{1,0:T(8,128)(2,1)S(1)} %copy-done.1), custom_call_target="tpu_custom_call" | custom-call | tf_op jit(solution)/shard_map/conv/pallas_call | solution.py:386
  35.5 0.0 collective-permute-done.4.r1_ref
  35.5 2.4 %collective-permute-done.5.r2_ref = f32[4,16,128]{2,1,0:T(8,128)S(1)} collective-permute-done((f32[4,16,128]{2,1,0:T(8,128)S(1)}, f32[4,16,128]{2,1,0:T(8,128)S(1)}, u32[]{:S(2)}, u32[]{:S(2)}) %collective-permute-start.5) | collective-permute-done | bytes 32800 | tf_op jit(solution)/shard_map/ppermute | solution.py:461
  37.9 0.9 %collective-permute-done.6.r3_ref = f32[4,16,128]{2,1,0:T(8,128)S(1)} collective-permute-done((f32[4,16,128]{2,1,0:T(8,128)S(1)}, f32[4,16,128]{2,1,0:T(8,128)S(1)}, u32[]{:S(2)}, u32[]{:S(2)}) %collective-permute-start.6) | collective-permute-done | bytes 32800 | tf_op jit(solution)/shard_map/ppermute | solution.py:461
  38.8 1.5 %readout.1 = bf16[16,128,128]{2,1,0:T(8,128)(2,1)S(1)} custom-call(s32[1]{0:T(128)} %bitcast.4.zl_ref, f32[16,128,128]{2,1,0:T(8,128)S(1)} %conv.1.inner_ref, f32[16,16,128]{2,1,0:T(8,128)S(1)} %get-tuple-element.40.state_ref, f32[4,16,128]{2,1,0:T(8,128)S(1)} %get-tuple-element.41.r0_ref, f32[4,16,128]{2,1,0:T(8,128)S(1)} %collective-permute-done.4.r1_ref, ...), custom_call_target="tpu_custom_call" | custom-call | tf_op jit(solution)/shard_map/readout/pallas_call | solution.py:434
  40.3 13.5 %all_to_all.10.long_ref = bf16[16,128,128]{2,1,0:T(8,128)(2,1)S(1)} all-to-all(bf16[16,128,128]{2,1,0:T(8,128)(2,1)S(1)} %readout.1), channel_id=1, replica_groups=mesh['y'=4,'zl'=4,'x'=4,'mp'=4] {'y','x'}, dimensions={0} | all-to-all | bytes 1048576 | tf_op jit(solution)/shard_map/all_to_all | solution.py:480
  53.8 0.9 %gate.1 = bf16[2048,128]{1,0:T(8,128)(2,1)} custom-call(f32[16,128,128]{2,1,0:T(8,128)S(1)} %get-tuple-element.32.mix_ref, f32[16,128,128]{2,1,0:T(8,128)S(1)} %get-tuple-element.33.direct_ref, bf16[16,128,128]{2,1,0:T(8,128)(2,1)S(1)} %all_to_all.10.long_ref), custom_call_target="tpu_custom_call" | custom-call | tf_op jit(solution)/shard_map/gate/pallas_call | solution.py:277
Async XLA Ops:
  3.4 5.8 %collective-permute-start = (bf16[16,8,128]{2,1,0:T(8,128)(2,1)S(1)}, bf16[16,8,128]{2,1,0:T(8,128)(2,1)S(1)}, u32[]{:S(2)}, u32[]{:S(2)}) collective-permute-start(bf16[16,8,128]{2,1,0:T(8,128)(2,1)S(1)} %get-tuple-element.26), channel_id=1, source_target_pairs={{0,4},{4,8},{8,12},{12,16},{16,20},{20,24},{24,28},{28,32},{32,36}... | collective-permute-start | bytes 98312 | tf_op jit(solution)/shard_map/ppermute | solution.py:466
  6.8 6.4 %collective-permute-start.1 = (f32[32,128]{1,0:T(8,128)S(1)}, f32[32,128]{1,0:T(8,128)S(1)}, u32[]{:S(2)}, u32[]{:S(2)}) collective-permute-start(f32[32,128]{1,0:T(8,128)S(1)} %get-tuple-element.28.p0_ref), channel_id=1, source_target_pairs={{0,16},{16,32},{32,48},{48,0},{1,17},{17,33},{33,49},{49,1},{2,18}... | collective-permute-start | bytes 49160 | tf_op jit(solution)/shard_map/ppermute | solution.py:461
  9.9 17.3 %copy-start = (bf16[256,256]{1,0:T(8,128)(2,1)S(1)}, bf16[256,256]{1,0:T(8,128)(2,1)}, u32[]{:S(2)}) copy-start(bf16[256,256]{1,0:T(8,128)(2,1)} %constant.12.clone.forward_ref) | copy-start | bytes 393220
  13.2 16.3 %all-to-all-start = ((bf16[16,128,128]{2,1,0:T(8,128)(2,1)}), bf16[16,128,128]{2,1,0:T(8,128)(2,1)S(1)}, u32[]{:S(2)}, u32[]{:S(2)}) async-start(bf16[16,128,128]{2,1,0:T(8,128)(2,1)} %head.1.product_ref), calls=%async_computation | async-start | bytes 1048576 | tf_op jit(solution)/shard_map/all_to_all | solution.py:470
  20.4 13.4 %copy-start.1 = (bf16[256,256]{1,0:T(8,128)(2,1)S(1)}, bf16[256,256]{1,0:T(8,128)(2,1)}, u32[]{:S(2)}) copy-start(bf16[256,256]{1,0:T(8,128)(2,1)} %constant.13.clone.backward_ref) | copy-start | bytes 393220
  20.4 4.6 %collective-permute-start.2 = (f32[32,128]{1,0:T(8,128)S(1)}, f32[32,128]{1,0:T(8,128)S(1)}, u32[]{:S(2)}, u32[]{:S(2)}) collective-permute-start(f32[32,128]{1,0:T(8,128)S(1)} %get-tuple-element.28.p0_ref), channel_id=1, source_target_pairs={{0,48},{16,0},{32,16},{48,32},{1,49},{17,1},{33,17},{49,33},{2,50}... | collective-permute-start | bytes 49160 | tf_op jit(solution)/shard_map/ppermute | solution.py:461
  22.5 4.6 %collective-permute-start.3 = (f32[32,128]{1,0:T(8,128)S(1)}, f32[32,128]{1,0:T(8,128)S(1)}, u32[]{:S(2)}, u32[]{:S(2)}) collective-permute-start(f32[32,128]{1,0:T(8,128)S(1)} %get-tuple-element.28.p0_ref), channel_id=1, source_target_pairs={{0,32},{16,48},{32,0},{48,16},{1,33},{17,49},{33,1},{49,17},{2,34}... | collective-permute-start | bytes 49160 | tf_op jit(solution)/shard_map/ppermute | solution.py:461
  31.0 4.5 %collective-permute-start.4 = (f32[4,16,128]{2,1,0:T(8,128)S(1)}, f32[4,16,128]{2,1,0:T(8,128)S(1)}, u32[]{:S(2)}, u32[]{:S(2)}) collective-permute-start(f32[4,16,128]{2,1,0:T(8,128)S(1)} %get-tuple-element.41.r0_ref), channel_id=1, source_target_pairs={{0,48},{16,0},{32,16},{48,32},{1,49},{17,1},{33,17},{49,33},{2,50}... | collective-permute-start | bytes 98312 | tf_op jit(solution)/shard_map/ppermute | solution.py:461
  33.1 4.8 %collective-permute-start.5 = (f32[4,16,128]{2,1,0:T(8,128)S(1)}, f32[4,16,128]{2,1,0:T(8,128)S(1)}, u32[]{:S(2)}, u32[]{:S(2)}) collective-permute-start(f32[4,16,128]{2,1,0:T(8,128)S(1)} %get-tuple-element.41.r0_ref), channel_id=1, source_target_pairs={{0,32},{16,48},{32,0},{48,16},{1,33},{17,49},{33,1},{49,17},{2,34}... | collective-permute-start | bytes 98312 | tf_op jit(solution)/shard_map/ppermute | solution.py:461
  33.1 5.7 %collective-permute-start.6 = (f32[4,16,128]{2,1,0:T(8,128)S(1)}, f32[4,16,128]{2,1,0:T(8,128)S(1)}, u32[]{:S(2)}, u32[]{:S(2)}) collective-permute-start(f32[4,16,128]{2,1,0:T(8,128)S(1)} %get-tuple-element.41.r0_ref), channel_id=1, source_target_pairs={{0,16},{16,32},{32,48},{48,0},{1,17},{17,33},{33,49},{49,1},{2,18}... | collective-permute-start | bytes 98312 | tf_op jit(solution)/shard_map/ppermute | solution.py:461
